TPU v7x, 32 devices: a whole 2x2x4 slice. The times are simulated.
32 devices in a mesh: dom: 4 (over y, x), tp: 8 (over z, core).
Axes of the slice: x: 2, y: 2, z: 4, core: 2. Of those that a mesh axis runs over, the one named last changes fastest.
Arguments:
- latent: bfloat16 [1024, 16384], P('tp', 'dom'), may hold values from -6 to 6
- w_first: bfloat16 [1024, 1024], P(None, 'tp'), may hold values from -0.1875 to 0.1875
- w_second: bfloat16 [1024, 1024], P('tp'), may hold values from -0.1875 to 0.1875
- w_env: bfloat16 [1024, 256], P('tp'), may hold values from -0.1875 to 0.1875
- edge_vec: float32 [3, 16384], P(None, 'dom'), may hold values from -3 to 3, as said below
- centers: int32 [16384], P('dom'), may hold values from 0 to 127
- block_dest: int32 [128, 1], P('dom'), may hold values from 0 to 3; in each aligned block of 32 rows (0 to 31, 32 to 63, ...) at most 16 rows name the same one
- block_fill: int32 [128], P('dom'), may hold values from 64 to 128
- species: int32 [512], P('dom'), may hold values from 0 to 3
- species_gain: float32 [4, 256], P(None, 'tp'), may hold values from 0.1 to 1.9
Outputs:
- latent_new: bfloat16 [1024, 16384], P('tp', 'dom')
- env_out: float32 [9, 256, 512], P(None, 'tp', 'dom')
- invariants: float32 [3, 256, 16384], P(None, 'tp', 'dom')
Inputs may be any that keep to these rules, and one draw needn't show every extreme that they name: `block_dest`: in the 32 blocks of one domain no destination domain is named more than 16 times, a bound that some block reaches. `edge_vec`: every component has magnitude 0.5 to 3.
All inputs are finite; a program needn't handle non-finite values.
Results may differ from a plain program's by a relative error of at most 0.0077.
Values may be sent and summed in bfloat16 or wider, within the bound.
No kernel may reach another device: no remote copies, remote signals or barrier semaphores. Data moves between devices by JAX's collectives and lax.ppermute only.
A program may use at most 128 MiB of HBM per device.

v0:
```python
import functools
import math

import jax
import jax.numpy as jnp
from jax import lax
from jax.experimental import pallas as pl
from jax.experimental.pallas import tpu as pltpu
from jax.sharding import PartitionSpec as P


root_three = math.sqrt(3.0)
root_five = math.sqrt(5.0)
root_fifteen = math.sqrt(15.0)
cutoff_radius = 6.0
parts = 9
env_factor = 0.25
lanes = 128
cores = 2
bf16 = jnp.bfloat16
f32 = jnp.float32


mib = 1024 * 1024
in_vmem = pl.BlockSpec(memory_space=pltpu.VMEM)
in_smem = pl.BlockSpec(memory_space=pltpu.SMEM)
in_hbm = pl.BlockSpec(memory_space=pltpu.HBM)
anywhere = pl.BlockSpec(memory_space=pl.ANY)


def harmonics(vectors):
    along_x = vectors[0]
    along_y = vectors[1]
    along_z = vectors[2]
    radius = jnp.sqrt(along_x * along_x + along_y * along_y + along_z * along_z)
    unit_x = along_x / radius
    unit_y = along_y / radius
    unit_z = along_z / radius
    ratio = radius / cutoff_radius
    envelope = (1.0 - ratio * ratio) ** 2
    factors = [
        jnp.ones_like(unit_x),
        root_three * unit_x,
        root_three * unit_y,
        root_three * unit_z,
        root_fifteen * unit_x * unit_y,
        root_fifteen * unit_y * unit_z,
        root_five / 2.0 * (3.0 * unit_z * unit_z - 1.0),
        root_fifteen * unit_x * unit_z,
        root_fifteen / 2.0 * (unit_x * unit_x - unit_y * unit_y),
    ]
    return [factor * envelope for factor in factors]


def contract_rows(left, right):
    return lax.dot_general(
        left, right, (((0,), (0,)), ((), ())), preferred_element_type=f32
    )


def swap_blocks(array, axis):
    return lax.all_to_all(array, axis, split_axis=0, concat_axis=0, tiled=True)


def flip_dom(array, mask):
    count = lax.axis_size("dom")
    return lax.ppermute(array, "dom", [(i, i ^ mask) for i in range(count)])


def hop_order(chips):
    return sorted(range(1, chips), key=lambda k: (k.bit_length(), -k))


def flip_tp(array, mask):
    count = lax.axis_size("tp")
    return lax.ppermute(array, "tp", [(t, t ^ mask) for t in range(count)])


def other_core(array):
    return flip_tp(array, 1)


def stay(array):
    return pltpu.with_memory_space_constraint(array, pltpu.HBM)


def grant(size):
    return pltpu.CompilerParams(vmem_limit_bytes=size * mib)


def prepare_kernel(*refs):
    sources, (full_ref, own_ref), held, sems = refs[:3], refs[3:5], refs[5:8], refs[8]
    copies = [
        pltpu.make_async_copy(source, place, sems.at[i])
        for i, (source, place) in enumerate(zip(sources, held))
    ]
    for copy in copies:
        copy.start()
    first_ref, second_ref, env_ref = held
    quarters = full_ref.shape[0]
    width = first_ref.shape[0] // quarters
    chan = env_ref.shape[1] // quarters
    copies[0].wait()
    for q in range(quarters):
        for i in range(width // lanes):
            start = q * width + i * lanes
            full_ref[q, i * lanes : (i + 1) * lanes, :] = first_ref[start : start + lanes, :].T
    copies[1].wait()
    for q in range(quarters):
        full_ref[q, width : 2 * width, :] = second_ref[:, q * width : (q + 1) * width].T
    copies[2].wait()
    for q in range(quarters):
        full_ref[q, 2 * width :, :] = env_ref[:, q * chan : (q + 1) * chan].T
    own_ref[...] = full_ref[lax.axis_index("dom")]


def mlp_kernel(x_ref, *refs, quarters, chips, chan, order):
    per_group = 1 + len(order) * quarters
    sources = [refs[g * per_group : (g + 1) * per_group] for g in range(cores)]
    shards, depth, _ = x_ref.shape
    outs = refs[cores * per_group :]
    new_refs, outs = outs[:shards], outs[shards:]
    out_ref, first, second, env, moved, hidden, fresh, rows_out, sems = outs
    total = shards * depth
    width = total // quarters
    per_quarter = shards // quarters
    dom, place = lax.axis_index("dom"), lax.axis_index("tp")
    chip, core = place // cores, lax.rem(place, cores)
    for j in range(quarters):
        for i in range(per_quarter):
            start = j * width + i * depth
            moved[start : start + depth, :] = x_ref[(dom ^ j) * per_quarter + i]
    for k in range(chips):
        for g in range(cores):
            at = (k * cores + g) * depth
            for j in range(quarters):
                if k == 0:
                    block = sources[g][0].at[dom ^ j]
                else:
                    block = sources[g][1 + order.index(k) * quarters + j]
                for i in range(width // lanes):
                    column = j * width + i * lanes
                    first[at : at + depth, column : column + lanes] = block[
                        i * depth : (i + 1) * depth, :
                    ]
                row = width // lanes * depth
                start = pl.multiple_of((dom ^ j) * width, lanes)
                second[pl.ds(start, width), at : at + depth] = block[row : row + width, :]
                row += width
                start = pl.multiple_of((dom ^ j) * chan, chan)
                env[pl.ds(start, chan), at : at + depth] = block[row : row + chan, :]
    value = jnp.dot(first[...], moved[...], preferred_element_type=f32)
    hidden[...] = (value / (1.0 + jnp.exp(-value))).astype(bf16)
    update = jnp.dot(second[...], hidden[...], preferred_element_type=f32)
    for s in range(shards):
        rows = slice(s * depth, (s + 1) * depth)
        fresh[s] = (x_ref[s].astype(f32) + update[rows, :]).astype(bf16)
    copies = [
        pltpu.make_async_copy(fresh.at[place ^ s], out, sems.at[s])
        for s, out in enumerate(new_refs)
    ]
    for copy in copies:
        copy.start()
    for k in range(chips):
        for g in range(cores):
            at = (k * cores + g) * depth
            source = (chip ^ k) * cores + (core if g == 0 else 1 - core)
            moved[at : at + depth, :] = fresh[source]
    rows = jnp.dot(env[...], moved[...], preferred_element_type=f32).astype(bf16)
    per = rows.shape[0] // shards
    for s in range(shards):
        rows_out[s] = rows[s * per : (s + 1) * per, :]
    copies.append(pltpu.make_async_copy(rows_out, out_ref, sems.at[shards]))
    copies[-1].start()
    for copy in copies:
        copy.wait()


def split_kernel(x_ref, tie_ref, out_ref, held, sems_in, sems_out):
    shards, _, edges = held.shape
    arriving = [
        pltpu.make_async_copy(x_ref.at[:, pl.ds(s * edges, edges)], held.at[s], sems_in.at[s])
        for s in range(shards)
    ]
    leaving = [
        pltpu.make_async_copy(held.at[s], out_ref.at[s], sems_out.at[s]) for s in range(shards)
    ]
    for copy in arriving:
        copy.start()
    for before, after in zip(arriving, leaving):
        before.wait()
        after.start()
    for copy in leaving:
        copy.wait()


def join_kernel(tie_ref, *refs):
    pieces, out_ref = refs[:-1], refs[-1]
    edges = pieces[0].shape[1]
    for s, piece in enumerate(pieces):
        at = pl.multiple_of((lax.axis_index("tp") ^ s) * edges, lanes)
        out_ref[:, pl.ds(at, edges)] = piece[...]


def join_pieces(back, tie):
    depth, edges = back[0].shape
    return pl.pallas_call(
        join_kernel,
        out_shape=jax.ShapeDtypeStruct((depth, edges * len(back)), bf16),
        in_specs=[anywhere] + [in_vmem] * len(back),
        out_specs=in_vmem,
        compiler_params=grant(8),
        name="join",
    )(tie, *back)


def spread_mlp(latent, w_first, w_second, w_env, ties):
    domains = lax.axis_size("dom")
    shards = lax.axis_size("tp")
    chips = shards // cores
    total = w_first.shape[0]
    depth = w_first.shape[1]
    channels = w_env.shape[1]
    width = total // domains
    chan = channels // domains
    rows = 2 * width + chan
    edges = latent.shape[1] // shards
    full, own = pl.pallas_call(
        prepare_kernel,
        out_shape=(
            jax.ShapeDtypeStruct((domains, rows, depth), bf16),
            jax.ShapeDtypeStruct((rows, depth), bf16),
        ),
        in_specs=[in_hbm] * 3,
        out_specs=(in_vmem, in_vmem),
        scratch_shapes=[pltpu.VMEM(w.shape, bf16) for w in (w_first, w_second, w_env)]
        + [pltpu.SemaphoreType.DMA((3,))],
        compiler_params=grant(8),
        name="prepare",
    )(stay(w_first), stay(w_second), stay(w_env))
    pieces = pl.pallas_call(
        split_kernel,
        out_shape=pltpu.HBM((shards, depth, edges), bf16),
        in_specs=[in_hbm, anywhere],
        out_specs=in_hbm,
        scratch_shapes=[pltpu.VMEM((shards, depth, edges), bf16)]
        + [pltpu.SemaphoreType.DMA((shards,))] * 2,
        compiler_params=grant(8),
        name="split",
    )(stay(latent), own)
    order = hop_order(chips)
    shifted = {}
    for k in order:
        shifted[k] = flip_tp(own, k * cores)
    edge_rows = swap_blocks(pieces, "tp")
    edge_rows, *ties = lax.optimization_barrier((edge_rows, *ties))
    mine = [full]
    for k in order:
        mine += [shifted[k]] + [flip_dom(shifted[k], j) for j in range(1, domains)]
    others = [other_core(array) for array in mine]
    *new_rows, weight_rows = pl.pallas_call(
        functools.partial(mlp_kernel, quarters=domains, chips=chips, chan=chan, order=order),
        out_shape=[pltpu.HBM((depth, edges), bf16)] * shards
        + [pltpu.HBM((shards, channels // shards, edges), bf16)],
        in_specs=[in_vmem] * (1 + 2 * len(mine)),
        out_specs=[in_hbm] * (shards + 1),
        scratch_shapes=[
            pltpu.VMEM((total, total), bf16),
            pltpu.VMEM((total, total), bf16),
            pltpu.VMEM((channels, total), bf16),
            pltpu.VMEM((total, edges), bf16),
            pltpu.VMEM((total, edges), bf16),
            pltpu.VMEM((shards, depth, edges), bf16),
            pltpu.VMEM((shards, channels // shards, edges), bf16),
            pltpu.SemaphoreType.DMA((shards + 1,)),
        ],
        compiler_params=grant(28),
        name="mlp",
    )(edge_rows, *mine, *others)
    weights = swap_blocks(weight_rows, "tp")
    back = {0: new_rows[0]}
    for s in range(1, shards):
        back[s] = flip_tp(new_rows[s], s)
    back = [back[s] for s in range(shards)]
    return (lambda tie: join_pieces(back, tie)), weights, ties


def gathered_mlp(latent, w_first, w_second, w_env, ties):
    edge_rows = lax.all_to_all(latent, "tp", split_axis=1, concat_axis=0, tiled=True)
    full_first = lax.all_gather(w_first, "tp", axis=1, tiled=True)
    full_second = lax.all_gather(w_second, "tp", axis=0, tiled=True)
    full_env = lax.all_gather(w_env, "tp", axis=0, tiled=True)
    hidden = jax.nn.silu(contract_rows(full_first, edge_rows)).astype(bf16)
    update = contract_rows(full_second, hidden)
    new_rows = (edge_rows.astype(f32) + update).astype(bf16)
    weight_rows = contract_rows(full_env, new_rows).astype(bf16)
    shards = lax.axis_size("tp")
    weights = swap_blocks(weight_rows.reshape(shards, -1, weight_rows.shape[1]), "tp")
    new_rows, weights = lax.optimization_barrier((new_rows, weights))
    latent_new = lax.all_to_all(new_rows, "tp", split_axis=0, concat_axis=1, tiled=True)
    return (lambda tie: latent_new), weights, ties


def geometry_kernel(vec_ref, fill_ref, centers_ref, out_ref):
    vectors = [vec_ref[i] for i in range(3)]
    ids = lax.broadcasted_iota(jnp.int32, vectors[0].shape, 1)
    alive = (ids < fill_ref[...]).astype(f32)
    for m, part in enumerate(harmonics(vectors)):
        out_ref[m] = part * alive
    out_ref[parts] = centers_ref[...].astype(f32)


def select_atoms(h_ref, block, atoms):
    ids = lax.broadcasted_iota(jnp.int32, (atoms, lanes), 0).astype(f32)
    return (ids == h_ref[parts, pl.ds(block, 1), :]).astype(f32).astype(bf16)


def sums_kernel(dest_ref, w_ref, h_ref, *refs):
    outs, total = refs[:-1], refs[-1]
    shards, _, edges = w_ref.shape
    atoms = total.shape[2]
    per = edges // lanes
    total[...] = jnp.zeros_like(total)

    def step(s, carry):
        for i in range(per):
            block = s * per + i
            weight = w_ref[s, :, i * lanes : (i + 1) * lanes].astype(f32)
            terms = [
                (h_ref[m, pl.ds(block, 1), :] * weight).astype(bf16) for m in range(parts)
            ]
            contrib = jnp.concatenate(terms, axis=0)
            chosen = select_atoms(h_ref, block, atoms)
            slot = dest_ref[block] ^ lax.axis_index("dom")
            total[slot] += lax.dot_general(
                contrib, chosen, (((1,), (1,)), ((), ())), preferred_element_type=f32
            )
        return carry

    lax.fori_loop(0, shards, step, 0)
    for j, out in enumerate(outs):
        out[...] = total[j].astype(out.dtype)


def invariants_kernel(dest_ref, w_ref, h_ref, *refs):
    domains = len(refs) - 3
    out_ref, token_ref, env = refs[domains:]
    token_ref[...] = jnp.zeros_like(token_ref)
    shards, chan, edges = w_ref.shape
    atoms = env.shape[2]
    per = edges // lanes
    for j in range(domains):
        env[j] = refs[j][...]

    def step(s, carry):
        for i in range(per):
            block = s * per + i
            weight = w_ref[s, :, i * lanes : (i + 1) * lanes].astype(f32)
            chosen = select_atoms(h_ref, block, atoms)
            slot = dest_ref[block] ^ lax.axis_index("dom")
            found = jnp.dot(env[slot], chosen, preferred_element_type=f32)
            products = [
                found[m * chan : (m + 1) * chan, :] * h_ref[m, pl.ds(block, 1), :]
                for m in range(parts)
            ]
            at = pl.multiple_of(block * lanes, lanes)
            out_ref[0, :, pl.ds(at, lanes)] = products[0] * weight
            out_ref[1, :, pl.ds(at, lanes)] = sum(products[2:4], products[1]) * weight
            out_ref[2, :, pl.ds(at, lanes)] = sum(products[5:9], products[4]) * weight
        return carry

    lax.fori_loop(0, shards, step, 0)


def on_device(
    latent,
    w_first,
    w_second,
    w_env,
    edge_vec,
    centers,
    block_dest,
    block_fill,
    species,
    species_gain,
):
    domains = lax.axis_size("dom")
    shards = lax.axis_size("tp")
    nblocks = block_fill.shape[0]
    atoms = species.shape[0]
    chan = species_gain.shape[1]
    depth, edges = latent.shape
    spread = (
        depth == lanes
        and w_first.shape[0] % (domains * lanes) == 0
        and w_env.shape[1] % (domains * 16) == 0
        and shards % cores == 0
        and shards & (shards - 1) == 0
        and domains & (domains - 1) == 0
    )
    harmonic = pl.pallas_call(
        geometry_kernel,
        out_shape=jax.ShapeDtypeStruct((parts + 1, nblocks, lanes), f32),
        in_specs=[in_vmem] * 3,
        out_specs=in_vmem,
        compiler_params=grant(4),
        name="geometry",
    )(edge_vec.reshape(3, nblocks, lanes), block_fill[:, None], centers.reshape(nblocks, lanes))
    target = stay(block_dest[:, 0])
    species_ids = jnp.arange(species_gain.shape[0], dtype=jnp.int32)
    gain_sel = jnp.sum(
        jnp.where(
            species[None, None, :] == species_ids[:, None, None], species_gain[:, :, None], 0.0
        ),
        axis=0,
    )
    mlp = spread_mlp if spread else gathered_mlp
    finish, weights, (harmonic, gain_sel) = mlp(
        latent, w_first, w_second, w_env, (harmonic, gain_sel)
    )

    rows = parts * chan
    sums = pl.pallas_call(
        sums_kernel,
        out_shape=[jax.ShapeDtypeStruct((rows, atoms), f32)]
        + [jax.ShapeDtypeStruct((rows, atoms), bf16)] * (domains - 1),
        in_specs=[in_smem] + [in_vmem] * 2,
        out_specs=[in_vmem] * domains,
        scratch_shapes=[pltpu.VMEM((domains, rows, atoms), f32)],
        compiler_params=grant(8),
        name="sums",
    )(target, weights, harmonic)
    env_raw = sums[0]
    for j in range(1, domains):
        env_raw = env_raw + flip_dom(sums[j], j).astype(f32)
    env_out = env_raw.reshape(parts, chan, atoms) * gain_sel[None, :, :] * env_factor
    env_half = env_out.astype(bf16).reshape(rows, atoms)
    looked = [env_half] + [flip_dom(env_half, j) for j in range(1, domains)]
    invariants, token = pl.pallas_call(
        invariants_kernel,
        out_shape=(
            jax.ShapeDtypeStruct((3, chan, edges), f32),
            jax.ShapeDtypeStruct((8, lanes), f32),
        ),
        in_specs=[in_smem] + [in_vmem] * (2 + domains),
        out_specs=(in_vmem, in_vmem),
        scratch_shapes=[pltpu.VMEM((domains, rows, atoms), bf16)],
        compiler_params=grant(10),
        name="invariants",
    )(target, weights, harmonic, *looked)
    return (finish(token), env_out, invariants)


def solution(mesh):
    in_specs = (
        P("tp", "dom"),
        P(None, "tp"),
        P("tp", None),
        P("tp", None),
        P(None, "dom"),
        P("dom"),
        P("dom", None),
        P("dom"),
        P("dom"),
        P(None, "tp"),
    )
    out_specs = (P("tp", "dom"), P(None, "tp", "dom"), P(None, "tp", "dom"))

    return jax.shard_map(on_device, mesh=mesh, in_specs=in_specs, out_specs=out_specs, check_vma=False)
```

profile of v0, /device:TPU:9, one launch (start us, length us, event | category | flops | bytes accessed | tf_op | source)
XLA Modules:
  0.0 144.5 jit_solution(7787807470438233635)
XLA Ops:
  2.0 2.1 %split.1 = bf16[8,128,512]{2,1,0:T(8,128)(2,1)} custom-call(bf16[128,4096]{1,0:T(8,128)(2,1)} %x_ref.1, bf16[576,128]{1,0:T(8,128)(2,1)S(1)} %get-tuple-element.23.tie_ref), custom_call_target="tpu_custom_call" | custom-call | tf_op jit(solution)/shard_map/split/pallas_call | solution.py:241
  4.2 5.7 %all-to-all-start = ((bf16[8,128,512]{2,1,0:T(8,128)(2,1)}), bf16[8,128,512]{2,1,0:T(8,128)(2,1)S(1)}, u32[]{:S(2)}, u32[]{:S(2)}) async-start(bf16[8,128,512]{2,1,0:T(8,128)(2,1)} %split.1), calls=%async_computation | async-start | bytes 2097152 | tf_op jit(solution)/shard_map/all_to_all | solution.py:62
  9.9 2.1 %collective-permute-start.8 = (bf16[576,128]{1,0:T(8,128)(2,1)S(1)}, bf16[576,128]{1,0:T(8,128)(2,1)S(1)}, u32[]{:S(2)}, u32[]{:S(2)}) collective-permute-start(bf16[576,128]{1,0:T(8,128)(2,1)S(1)} %get-tuple-element.23.tie_ref), channel_id=1, source_target_pairs={{0,4},{1,5},{2,6},{3,7},{4,0},{5,1},{6,2},{7,3},{8,12},{9,13},{10,... | collective-permute-start | bytes 442376 | tf_op jit(solution)/shard_map/ppermute | solution.py:76
  12.0 1.5 %collective-permute-start = (bf16[576,128]{1,0:T(8,128)(2,1)S(1)}, bf16[576,128]{1,0:T(8,128)(2,1)S(1)}, u32[]{:S(2)}, u32[]{:S(2)}) collective-permute-start(bf16[576,128]{1,0:T(8,128)(2,1)S(1)} %get-tuple-element.23.tie_ref), channel_id=1, source_target_pairs={{0,2},{1,3},{2,0},{3,1},{4,6},{5,7},{6,4},{7,5},{8,10},{9,11},{10,... | collective-permute-start | bytes 442376 | tf_op jit(solution)/shard_map/ppermute | solution.py:76
  13.5 28.9 %collective-permute-done.8.refs_9_ = bf16[576,128]{1,0:T(8,128)(2,1)S(1)} collective-permute-done((bf16[576,128]{1,0:T(8,128)(2,1)S(1)}, bf16[576,128]{1,0:T(8,128)(2,1)S(1)}, u32[]{:S(2)}, u32[]{:S(2)}) %collective-permute-start.8) | collective-permute-done | bytes 147488 | tf_op jit(solution)/shard_map/ppermute | solution.py:76
  42.9 2.2 %collective-permute-start.11 = (bf16[576,128]{1,0:T(8,128)(2,1)S(1)}, bf16[576,128]{1,0:T(8,128)(2,1)S(1)}, u32[]{:S(2)}, u32[]{:S(2)}) collective-permute-start(bf16[576,128]{1,0:T(8,128)(2,1)S(1)} %collective-permute-done.8.refs_9_), channel_id=1, source_target_pairs={{0,24},{8,16},{16,8},{24,0},{1,25},{9,17},{17,9},{25,1},{2,26},{10... | collective-permute-start | bytes 442376 | tf_op jit(solution)/shard_map/ppermute | solution.py:67
  45.3 1.8 %collective-permute-done.4.refs_5_ = bf16[576,128]{1,0:T(8,128)(2,1)S(1)} collective-permute-done((bf16[576,128]{1,0:T(8,128)(2,1)S(1)}, bf16[576,128]{1,0:T(8,128)(2,1)S(1)}, u32[]{:S(2)}, u32[]{:S(2)}) %collective-permute-start.4) | collective-permute-done | bytes 147488 | tf_op jit(solution)/shard_map/ppermute | solution.py:76
  51.0 1.7 %collective-permute-done.10.refs_11_ = bf16[576,128]{1,0:T(8,128)(2,1)S(1)} collective-permute-done((bf16[576,128]{1,0:T(8,128)(2,1)S(1)}, bf16[576,128]{1,0:T(8,128)(2,1)S(1)}, u32[]{:S(2)}, u32[]{:S(2)}) %collective-permute-start.10) | collective-permute-done | bytes 147488 | tf_op jit(solution)/shard_map/ppermute | solution.py:67
  55.6 2.0 %collective-permute-start.3 = (bf16[576,128]{1,0:T(8,128)(2,1)S(1)}, bf16[576,128]{1,0:T(8,128)(2,1)}, u32[]{:S(2)}, u32[]{:S(2)}) collective-permute-start(bf16[576,128]{1,0:T(8,128)(2,1)S(1)} %collective-permute-done.refs_1_), channel_id=1, source_target_pairs={{0,24},{8,16},{16,8},{24,0},{1,25},{9,17},{17,9},{25,1},{2,26},{10... | collective-permute-start | bytes 442376 | tf_op jit(solution)/shard_map/ppermute | solution.py:67
  57.6 1.7 %collective-permute-done.6.refs_7_ = bf16[576,128]{1,0:T(8,128)(2,1)S(1)} collective-permute-done((bf16[576,128]{1,0:T(8,128)(2,1)S(1)}, bf16[576,128]{1,0:T(8,128)(2,1)S(1)}, u32[]{:S(2)}, u32[]{:S(2)}) %collective-permute-start.6) | collective-permute-done | bytes 147488 | tf_op jit(solution)/shard_map/ppermute | solution.py:67
  60.3 2.2 %collective-permute-start.24 = (bf16[576,128]{1,0:T(8,128)(2,1)S(1)}, bf16[576,128]{1,0:T(8,128)(2,1)S(1)}, u32[]{:S(2)}, u32[]{:S(2)}) collective-permute-start(bf16[576,128]{1,0:T(8,128)(2,1)S(1)} %collective-permute-done.11.refs_12_), channel_id=1, source_target_pairs={{0,1},{1,0},{2,3},{3,2},{4,5},{5,4},{6,7},{7,6},{8,9},{9,8},{10,11... | collective-permute-start | bytes 442376 | tf_op jit(solution)/shard_map/ppermute | solution.py:76
  63.2 1.5 %collective-permute-start.23 = (bf16[576,128]{1,0:T(8,128)(2,1)S(1)}, bf16[576,128]{1,0:T(8,128)(2,1)S(1)}, u32[]{:S(2)}, u32[]{:S(2)}) collective-permute-start(bf16[576,128]{1,0:T(8,128)(2,1)S(1)} %collective-permute-done.10.refs_11_), channel_id=1, source_target_pairs={{0,1},{1,0},{2,3},{3,2},{4,5},{5,4},{6,7},{7,6},{8,9},{9,8},{10,11... | collective-permute-start | bytes 442376 | tf_op jit(solution)/shard_map/ppermute | solution.py:76
  82.5 5.8 %mlp.1 = (bf16[128,512]{1,0:T(8,128)(2,1)}, bf16[128,512]{1,0:T(8,128)(2,1)}, bf16[128,512]{1,0:T(8,128)(2,1)}, bf16[128,512]{1,0:T(8,128)(2,1)}, bf16[128,512]{...) custom-call(bf16[8,128,512]{2,1,0:T(8,128)(2,1)S(1)} %all-to-all-don, ...), custom_call_target="tpu_custom_call" | custom-call | tf_op jit(solution)/shard_map/mlp/pallas_call | solution.py:261
  88.3 14.3 %all_to_all.10.w_ref = bf16[8,32,512]{2,1,0:T(8,128)(2,1)S(1)} all-to-all(bf16[8,32,512]{2,1,0:T(8,128)(2,1)} %get-tuple-element.26), channel_id=1, replica_groups=mesh['dom'=4,'tp'=8] {'tp'}, dimensions={0} | all-to-all | bytes 524288 | tf_op jit(solution)/shard_map/all_to_all | solution.py:62
  102.7 2.8 %sums.1 = (f32[288,128]{1,0:T(8,128)S(1)}, bf16[288,128]{1,0:T(8,128)(2,1)S(1)}, bf16[288,128]{1,0:T(8,128)(2,1)S(1)}, bf16[288,128]{1,0:T(8,128)(2,1)S(1)}) custom-call(s32[32]{0:T(128)} %bitcast.18, bf16[8,32,512]{2,1,0:T(8,128)(2,1)S(1)} %all_to_all.10.w_ref, f32[10,32,128]{2,1,0:T(8,128)S(1)} %geometry.1.h_ref), custom_call_target="tpu_custom_call" | custom-call | tf_op jit(solution)/shard_map/sums/pallas_call | solution.py:423
  108.2 1.9 %collective-permute-start.31 = (bf16[128,512]{1,0:T(8,128)(2,1)}, bf16[128,512]{1,0:T(8,128)(2,1)S(1)}, u32[]{:S(2)}, u32[]{:S(2)}) collective-permute-start(bf16[128,512]{1,0:T(8,128)(2,1)} %get-tuple-element.35), channel_id=1, source_target_pairs={{0,1},{1,0},{2,3},{3,2},{4,5},{5,4},{6,7},{7,6},{8,9},{9,8},{10,11... | collective-permute-start | bytes 393224 | tf_op jit(solution)/shard_map/ppermute | solution.py:76
  110.1 1.7 %collective-permute-start.32 = (bf16[128,512]{1,0:T(8,128)(2,1)}, bf16[128,512]{1,0:T(8,128)(2,1)S(1)}, u32[]{:S(2)}, u32[]{:S(2)}) collective-permute-start(bf16[128,512]{1,0:T(8,128)(2,1)} %get-tuple-element.36), channel_id=1, source_target_pairs={{0,2},{1,3},{2,0},{3,1},{4,6},{5,7},{6,4},{7,5},{8,10},{9,11},{10,... | collective-permute-start | bytes 393224 | tf_op jit(solution)/shard_map/ppermute | solution.py:76
  114.5 4.5 %collective-permute-start.33 = (bf16[128,512]{1,0:T(8,128)(2,1)S(1)}, bf16[128,512]{1,0:T(8,128)(2,1)S(1)}, u32[]{:S(2)}, u32[]{:S(2)}) collective-permute-start(bf16[128,512]{1,0:T(8,128)(2,1)S(1)} %copy-done.27), channel_id=1, source_target_pairs={{0,3},{1,2},{2,1},{3,0},{4,7},{5,6},{6,5},{7,4},{8,11},{9,10},{10,... | collective-permute-start | bytes 393224 | tf_op jit(solution)/shard_map/ppermute | solution.py:76
  119.0 1.6 %collective-permute-start.35 = (bf16[128,512]{1,0:T(8,128)(2,1)S(1)}, bf16[128,512]{1,0:T(8,128)(2,1)S(1)}, u32[]{:S(2)}, u32[]{:S(2)}) collective-permute-start(bf16[128,512]{1,0:T(8,128)(2,1)S(1)} %copy-done.25), channel_id=1, source_target_pairs={{0,5},{1,4},{2,7},{3,6},{4,1},{5,0},{6,3},{7,2},{8,13},{9,12},{10,... | collective-permute-start | bytes 393224 | tf_op jit(solution)/shard_map/ppermute | solution.py:76
  122.0 1.4 collective-permute-start.37
  124.1 3.7 %invariants.1 = (f32[3,32,4096]{2,1,0:T(8,128)}, f32[8,128]{1,0:T(8,128)S(1)}) custom-call(s32[32]{0:T(128)} %bitcast.19, bf16[8,32,512]{2,1,0:T(8,128)(2,1)S(1)} %all_to_all.10.w_ref, f32[10,32,128]{2,1,0:T(8,128)S(1)} %geometry.1.h_ref, bf16[288,128]{1,0:T(8,128)(2,1)S(1)} %get-tuple-element.43.refs_0_, ...), custom_call_target="tpu_custom_call" | custom-call | tf_op jit(solution)/shard_map/invariants/pallas_call | solution.py:439
  127.8 8.1 %collective-permute-done.35.refs_5_ = bf16[128,512]{1,0:T(8,128)(2,1)S(1)} collective-permute-done((bf16[128,512]{1,0:T(8,128)(2,1)S(1)}, bf16[128,512]{1,0:T(8,128)(2,1)S(1)}, u32[]{:S(2)}, u32[]{:S(2)}) %collective-permute-start.35) | collective-permute-done | bytes 131104 | tf_op jit(solution)/shard_map/ppermute | solution.py:76
  136.0 4.1 %collective-permute-done.36.refs_6_ = bf16[128,512]{1,0:T(8,128)(2,1)S(1)} collective-permute-done((bf16[128,512]{1,0:T(8,128)(2,1)S(1)}, bf16[128,512]{1,0:T(8,128)(2,1)S(1)}, u32[]{:S(2)}, u32[]{:S(2)}) %collective-permute-start.36) | collective-permute-done | bytes 131104 | tf_op jit(solution)/shard_map/ppermute | solution.py:76
  140.1 3.4 %collective-permute-done.37.refs_7_ = bf16[128,512]{1,0:T(8,128)(2,1)S(1)} collective-permute-done((bf16[128,512]{1,0:T(8,128)(2,1)S(1)}, bf16[128,512]{1,0:T(8,128)(2,1)S(1)}, u32[]{:S(2)}, u32[]{:S(2)}) %collective-permute-start.37) | collective-permute-done | bytes 131104 | tf_op jit(solution)/shard_map/ppermute | solution.py:76
  (126 shorter events, 36.9 us)
Async XLA Ops:
  4.2 69.1 %all-to-all-start = ((bf16[8,128,512]{2,1,0:T(8,128)(2,1)}), bf16[8,128,512]{2,1,0:T(8,128)(2,1)S(1)}, u32[]{:S(2)}, u32[]{:S(2)}) async-start(bf16[8,128,512]{2,1,0:T(8,128)(2,1)} %split.1), calls=%async_computation | async-start | bytes 2097152 | tf_op jit(solution)/shard_map/all_to_all | solution.py:62
  9.9 32.4 %collective-permute-start.8 = (bf16[576,128]{1,0:T(8,128)(2,1)S(1)}, bf16[576,128]{1,0:T(8,128)(2,1)S(1)}, u32[]{:S(2)}, u32[]{:S(2)}) collective-permute-start(bf16[576,128]{1,0:T(8,128)(2,1)S(1)} %get-tuple-element.23.tie_ref), channel_id=1, source_target_pairs={{0,4},{1,5},{2,6},{3,7},{4,0},{5,1},{6,2},{7,3},{8,12},{9,13},{10,... | collective-permute-start | bytes 442376 | tf_op jit(solution)/shard_map/ppermute | solution.py:76
  12.0 35.1 %collective-permute-start.4 = (bf16[576,128]{1,0:T(8,128)(2,1)S(1)}, bf16[576,128]{1,0:T(8,128)(2,1)S(1)}, u32[]{:S(2)}, u32[]{:S(2)}) collective-permute-start(bf16[576,128]{1,0:T(8,128)(2,1)S(1)} %get-tuple-element.23.tie_ref), channel_id=1, source_target_pairs={{0,6},{1,7},{2,4},{3,5},{4,2},{5,3},{6,0},{7,1},{8,14},{9,15},{10,... | collective-permute-start | bytes 442376 | tf_op jit(solution)/shard_map/ppermute | solution.py:76
  12.0 36.3 %collective-permute-start = (bf16[576,128]{1,0:T(8,128)(2,1)S(1)}, bf16[576,128]{1,0:T(8,128)(2,1)S(1)}, u32[]{:S(2)}, u32[]{:S(2)}) collective-permute-start(bf16[576,128]{1,0:T(8,128)(2,1)S(1)} %get-tuple-element.23.tie_ref), channel_id=1, source_target_pairs={{0,2},{1,3},{2,0},{3,1},{4,6},{5,7},{6,4},{7,5},{8,10},{9,11},{10,... | collective-permute-start | bytes 442376 | tf_op jit(solution)/shard_map/ppermute | solution.py:76
  42.4 7.2 %collective-permute-start.21 = (bf16[576,128]{1,0:T(8,128)(2,1)S(1)}, bf16[576,128]{1,0:T(8,128)(2,1)S(1)}, u32[]{:S(2)}, u32[]{:S(2)}) collective-permute-start(bf16[576,128]{1,0:T(8,128)(2,1)S(1)} %collective-permute-done.8.refs_9_), channel_id=1, source_target_pairs={{0,1},{1,0},{2,3},{3,2},{4,5},{5,4},{6,7},{7,6},{8,9},{9,8},{10,11... | collective-permute-start | bytes 442376 | tf_op jit(solution)/shard_map/ppermute | solution.py:76
  42.9 7.9 %collective-permute-start.11 = (bf16[576,128]{1,0:T(8,128)(2,1)S(1)}, bf16[576,128]{1,0:T(8,128)(2,1)S(1)}, u32[]{:S(2)}, u32[]{:S(2)}) collective-permute-start(bf16[576,128]{1,0:T(8,128)(2,1)S(1)} %collective-permute-done.8.refs_9_), channel_id=1, source_target_pairs={{0,24},{8,16},{16,8},{24,0},{1,25},{9,17},{17,9},{25,1},{2,26},{10... | collective-permute-start | bytes 442376 | tf_op jit(solution)/shard_map/ppermute | solution.py:67
  45.0 7.7 %collective-permute-start.10 = (bf16[576,128]{1,0:T(8,128)(2,1)S(1)}, bf16[576,128]{1,0:T(8,128)(2,1)S(1)}, u32[]{:S(2)}, u32[]{:S(2)}) collective-permute-start(bf16[576,128]{1,0:T(8,128)(2,1)S(1)} %collective-permute-done.8.refs_9_), channel_id=1, source_target_pairs={{0,16},{8,24},{16,0},{24,8},{1,17},{9,25},{17,1},{25,9},{2,18},{10... | collective-permute-start | bytes 442376 | tf_op jit(solution)/shard_map/ppermute | solution.py:67
  49.6 8.1 %collective-permute-start.7 = (bf16[576,128]{1,0:T(8,128)(2,1)S(1)}, bf16[576,128]{1,0:T(8,128)(2,1)S(1)}, u32[]{:S(2)}, u32[]{:S(2)}) collective-permute-start(bf16[576,128]{1,0:T(8,128)(2,1)S(1)} %collective-permute-done.4.refs_5_), channel_id=1, source_target_pairs={{0,24},{8,16},{16,8},{24,0},{1,25},{9,17},{17,9},{25,1},{2,26},{10... | collective-permute-start | bytes 442376 | tf_op jit(solution)/shard_map/ppermute | solution.py:67
  50.8 8.6 %collective-permute-start.6 = (bf16[576,128]{1,0:T(8,128)(2,1)S(1)}, bf16[576,128]{1,0:T(8,128)(2,1)S(1)}, u32[]{:S(2)}, u32[]{:S(2)}) collective-permute-start(bf16[576,128]{1,0:T(8,128)(2,1)S(1)} %collective-permute-done.4.refs_5_), channel_id=1, source_target_pairs={{0,16},{8,24},{16,0},{24,8},{1,17},{9,25},{17,1},{25,9},{2,18},{10... | collective-permute-start | bytes 442376 | tf_op jit(solution)/shard_map/ppermute | solution.py:67
  52.7 7.6 %collective-permute-start.5 = (bf16[576,128]{1,0:T(8,128)(2,1)S(1)}, bf16[576,128]{1,0:T(8,128)(2,1)}, u32[]{:S(2)}, u32[]{:S(2)}) collective-permute-start(bf16[576,128]{1,0:T(8,128)(2,1)S(1)} %collective-permute-done.4.refs_5_), channel_id=1, source_target_pairs={{0,8},{8,0},{16,24},{24,16},{1,9},{9,1},{17,25},{25,17},{2,10},{10... | collective-permute-start | bytes 442376 | tf_op jit(solution)/shard_map/ppermute | solution.py:67
  54.2 8.3 %collective-permute-start.13 = (bf16[576,128]{1,0:T(8,128)(2,1)S(1)}, bf16[576,128]{1,0:T(8,128)(2,1)S(1)}, u32[]{:S(2)}, u32[]{:S(2)}) collective-permute-start(bf16[576,128]{1,0:T(8,128)(2,1)S(1)} %collective-permute-done.refs_1_), channel_id=1, source_target_pairs={{0,1},{1,0},{2,3},{3,2},{4,5},{5,4},{6,7},{7,6},{8,9},{9,8},{10,11... | collective-permute-start | bytes 442376 | tf_op jit(solution)/shard_map/ppermute | solution.py:76
  55.6 7.5 %collective-permute-start.3 = (bf16[576,128]{1,0:T(8,128)(2,1)S(1)}, bf16[576,128]{1,0:T(8,128)(2,1)}, u32[]{:S(2)}, u32[]{:S(2)}) collective-permute-start(bf16[576,128]{1,0:T(8,128)(2,1)S(1)} %collective-permute-done.refs_1_), channel_id=1, source_target_pairs={{0,24},{8,16},{16,8},{24,0},{1,25},{9,17},{17,9},{25,1},{2,26},{10... | collective-permute-start | bytes 442376 | tf_op jit(solution)/shard_map/ppermute | solution.py:67
  57.6 8.3 %collective-permute-start.2 = (bf16[576,128]{1,0:T(8,128)(2,1)S(1)}, bf16[576,128]{1,0:T(8,128)(2,1)}, u32[]{:S(2)}, u32[]{:S(2)}) collective-permute-start(bf16[576,128]{1,0:T(8,128)(2,1)S(1)} %collective-permute-done.refs_1_), channel_id=1, source_target_pairs={{0,16},{8,24},{16,0},{24,8},{1,17},{9,25},{17,1},{25,9},{2,18},{10... | collective-permute-start | bytes 442376 | tf_op jit(solution)/shard_map/ppermute | solution.py:67
  59.3 7.4 %collective-permute-start.1 = (bf16[576,128]{1,0:T(8,128)(2,1)S(1)}, bf16[576,128]{1,0:T(8,128)(2,1)}, u32[]{:S(2)}, u32[]{:S(2)}) collective-permute-start(bf16[576,128]{1,0:T(8,128)(2,1)S(1)} %collective-permute-done.refs_1_), channel_id=1, source_target_pairs={{0,8},{8,0},{16,24},{24,16},{1,9},{9,1},{17,25},{25,17},{2,10},{10... | collective-permute-start | bytes 442376 | tf_op jit(solution)/shard_map/ppermute | solution.py:67
  63.2 11.1 %collective-permute-start.12 = (bf16[4,576,128]{2,1,0:T(8,128)(2,1)S(1)}, bf16[4,576,128]{2,1,0:T(8,128)(2,1)S(1)}, u32[]{:S(2)}, u32[]{:S(2)}) collective-permute-start(bf16[4,576,128]{2,1,0:T(8,128)(2,1)S(1)} %get-tuple-element.25.refs_0_), channel_id=1, source_target_pairs={{0,1},{1,0},{2,3},{3,2},{4,5},{5,4},{6,7},{7,6},{8,9},{9,8},{10,11... | collective-permute-start | bytes 1769480 | tf_op jit(solution)/shard_map/ppermute | solution.py:76
  110.1 9.0 %collective-permute-start.32 = (bf16[128,512]{1,0:T(8,128)(2,1)}, bf16[128,512]{1,0:T(8,128)(2,1)S(1)}, u32[]{:S(2)}, u32[]{:S(2)}) collective-permute-start(bf16[128,512]{1,0:T(8,128)(2,1)} %get-tuple-element.36), channel_id=1, source_target_pairs={{0,2},{1,3},{2,0},{3,1},{4,6},{5,7},{6,4},{7,5},{8,10},{9,11},{10,... | collective-permute-start | bytes 393224 | tf_op jit(solution)/shard_map/ppermute | solution.py:76
  111.8 7.2 %collective-permute-start.30 = (bf16[288,128]{1,0:T(8,128)(2,1)S(1)}, bf16[288,128]{1,0:T(8,128)(2,1)S(1)}, u32[]{:S(2)}, u32[]{:S(2)}) collective-permute-start(bf16[288,128]{1,0:T(8,128)(2,1)S(1)} %get-tuple-element.43.refs_0_), channel_id=1, source_target_pairs={{0,24},{8,16},{16,8},{24,0},{1,25},{9,17},{17,9},{25,1},{2,26},{10... | collective-permute-start | bytes 221192 | tf_op jit(solution)/shard_map/ppermute | solution.py:67
  113.0 7.6 %collective-permute-start.29 = (bf16[288,128]{1,0:T(8,128)(2,1)S(1)}, bf16[288,128]{1,0:T(8,128)(2,1)S(1)}, u32[]{:S(2)}, u32[]{:S(2)}) collective-permute-start(bf16[288,128]{1,0:T(8,128)(2,1)S(1)} %get-tuple-element.43.refs_0_), channel_id=1, source_target_pairs={{0,16},{8,24},{16,0},{24,8},{1,17},{9,25},{17,1},{25,9},{2,18},{10... | collective-permute-start | bytes 221192 | tf_op jit(solution)/shard_map/ppermute | solution.py:67
  113.7 8.3 %collective-permute-start.28 = (bf16[288,128]{1,0:T(8,128)(2,1)S(1)}, bf16[288,128]{1,0:T(8,128)(2,1)S(1)}, u32[]{:S(2)}, u32[]{:S(2)}) collective-permute-start(bf16[288,128]{1,0:T(8,128)(2,1)S(1)} %get-tuple-element.43.refs_0_), channel_id=1, source_target_pairs={{0,8},{8,0},{16,24},{24,16},{1,9},{9,1},{17,25},{25,17},{2,10},{10... | collective-permute-start | bytes 221192 | tf_op jit(solution)/shard_map/ppermute | solution.py:67
  114.5 13.3 %collective-permute-start.33 = (bf16[128,512]{1,0:T(8,128)(2,1)S(1)}, bf16[128,512]{1,0:T(8,128)(2,1)S(1)}, u32[]{:S(2)}, u32[]{:S(2)}) collective-permute-start(bf16[128,512]{1,0:T(8,128)(2,1)S(1)} %copy-done.27), channel_id=1, source_target_pairs={{0,3},{1,2},{2,1},{3,0},{4,7},{5,6},{6,5},{7,4},{8,11},{9,10},{10,... | collective-permute-start | bytes 393224 | tf_op jit(solution)/shard_map/ppermute | solution.py:76
  119.0 8.8 %collective-permute-start.34 = (bf16[128,512]{1,0:T(8,128)(2,1)S(1)}, bf16[128,512]{1,0:T(8,128)(2,1)S(1)}, u32[]{:S(2)}, u32[]{:S(2)}) collective-permute-start(bf16[128,512]{1,0:T(8,128)(2,1)S(1)} %copy-done.26), channel_id=1, source_target_pairs={{0,4},{1,5},{2,6},{3,7},{4,0},{5,1},{6,2},{7,3},{8,12},{9,13},{10,... | collective-permute-start | bytes 393224 | tf_op jit(solution)/shard_map/ppermute | solution.py:76
  119.0 16.9 %collective-permute-start.35 = (bf16[128,512]{1,0:T(8,128)(2,1)S(1)}, bf16[128,512]{1,0:T(8,128)(2,1)S(1)}, u32[]{:S(2)}, u32[]{:S(2)}) collective-permute-start(bf16[128,512]{1,0:T(8,128)(2,1)S(1)} %copy-done.25), channel_id=1, source_target_pairs={{0,5},{1,4},{2,7},{3,6},{4,1},{5,0},{6,3},{7,2},{8,13},{9,12},{10,... | collective-permute-start | bytes 393224 | tf_op jit(solution)/shard_map/ppermute | solution.py:76
  120.6 19.5 %collective-permute-start.36 = (bf16[128,512]{1,0:T(8,128)(2,1)S(1)}, bf16[128,512]{1,0:T(8,128)(2,1)S(1)}, u32[]{:S(2)}, u32[]{:S(2)}) collective-permute-start(bf16[128,512]{1,0:T(8,128)(2,1)S(1)} %copy-done.24), channel_id=1, source_target_pairs={{0,6},{1,7},{2,4},{3,5},{4,2},{5,3},{6,0},{7,1},{8,14},{9,15},{10,... | collective-permute-start | bytes 393224 | tf_op jit(solution)/shard_map/ppermute | solution.py:76
  122.0 21.5 %collective-permute-start.37 = (bf16[128,512]{1,0:T(8,128)(2,1)S(1)}, bf16[128,512]{1,0:T(8,128)(2,1)S(1)}, u32[]{:S(2)}, u32[]{:S(2)}) collective-permute-start(bf16[128,512]{1,0:T(8,128)(2,1)S(1)} %copy-done.23), channel_id=1, source_target_pairs={{0,7},{1,6},{2,5},{3,4},{4,3},{5,2},{6,1},{7,0},{8,15},{9,14},{10,... | collective-permute-start | bytes 393224 | tf_op jit(solution)/shard_map/ppermute | solution.py:76
  (44 other events, 638.8 us)
where the time goes:
time: 145 us
  waiting for transfers between devices  52.1 us (36%)
  starting transfers between devices  45.2 us (31%)
  Pallas kernels  16.9 us (12%)
  local copies, waits for them, and re-layouts  14.3 us (10%)
  blocking collectives  14.3 us (10%)
    ppermute x23, waiting for transfers between devices, flip_tp(): return lax.ppermute(array, 'tp', [(t, t ^ mask) for t in range(count)])  47.4 us
    ppermute x23, starting transfers between devices, flip_tp(): return lax.ppermute(array, 'tp', [(t, t ^ mask) for t in range(count)])  24.6 us
    ppermute x15, starting transfers between devices, flip_dom(): return lax.ppermute(array, 'dom', [(i, i ^ mask) for i in range(count)])  14.8 us
    all_to_all x1, blocking collectives, swap_blocks(): return lax.all_to_all(array, axis, split_axis=0, concat_axis=0, tiled=True)  14.3 us
    unnamed x59, local copies, waits for them, and re-layouts  14.2 us
    pallas_call x1, Pallas kernels, spread_mlp(): pl.pallas_call(functools.partial(mlp_kernel, quarters=domains, chips=chip...  5.8 us
    all_to_all x1, starting transfers between devices, swap_blocks(): return lax.all_to_all(array, axis, split_axis=0, concat_axis=0, tiled=True)  5.75 us
    ppermute x15, waiting for transfers between devices, flip_dom(): return lax.ppermute(array, 'dom', [(i, i ^ mask) for i in range(count)])  4.67 us
  transfers between devices with their start and end apart: 39, of which 10 were waited for; matrix products, arithmetic and copies ran while one was open for 1% of the time, Pallas kernels for 3%

commit v1 on v0

--- a/solution.py
+++ b/solution.py
@@ -114,23 +114,15 @@
     own_ref[...] = full_ref[lax.axis_index("dom")]
 
 
-def mlp_kernel(x_ref, *refs, quarters, chips, chan, order):
+def assemble_kernel(*refs, quarters, order):
     per_group = 1 + len(order) * quarters
     sources = [refs[g * per_group : (g + 1) * per_group] for g in range(cores)]
-    shards, depth, _ = x_ref.shape
-    outs = refs[cores * per_group :]
-    new_refs, outs = outs[:shards], outs[shards:]
-    out_ref, first, second, env, moved, hidden, fresh, rows_out, sems = outs
-    total = shards * depth
-    width = total // quarters
-    per_quarter = shards // quarters
-    dom, place = lax.axis_index("dom"), lax.axis_index("tp")
-    chip, core = place // cores, lax.rem(place, cores)
-    for j in range(quarters):
-        for i in range(per_quarter):
-            start = j * width + i * depth
-            moved[start : start + depth, :] = x_ref[(dom ^ j) * per_quarter + i]
-    for k in range(chips):
+    first, second, env = refs[cores * per_group :]
+    depth = lanes
+    width = first.shape[0] // quarters
+    chan = env.shape[0] // quarters
+    dom = lax.axis_index("dom")
+    for k in range(len(order) + 1):
         for g in range(cores):
             at = (k * cores + g) * depth
             for j in range(quarters):
@@ -149,8 +141,31 @@
                 row += width
                 start = pl.multiple_of((dom ^ j) * chan, chan)
                 env[pl.ds(start, chan), at : at + depth] = block[row : row + chan, :]
+
+
+def mlp_kernel(x_ref, *refs, quarters):
+    shards, depth, _ = x_ref.shape
+    stored, new_refs, out_ref = refs[:3], refs[3 : 3 + shards], refs[3 + shards]
+    *held, sems_in, moved, hidden, fresh, rows_out, sems = refs[4 + shards :]
+    first, second, env = held
+    loads = [
+        pltpu.make_async_copy(source, place, sems_in.at[i])
+        for i, (source, place) in enumerate(zip(stored, held))
+    ]
+    for load in loads:
+        load.start()
+    width = shards * depth // quarters
+    per_quarter = shards // quarters
+    dom, place = lax.axis_index("dom"), lax.axis_index("tp")
+    chip, core = place // cores, lax.rem(place, cores)
+    for j in range(quarters):
+        for i in range(per_quarter):
+            start = j * width + i * depth
+            moved[start : start + depth, :] = x_ref[(dom ^ j) * per_quarter + i]
+    loads[0].wait()
     value = jnp.dot(first[...], moved[...], preferred_element_type=f32)
     hidden[...] = (value / (1.0 + jnp.exp(-value))).astype(bf16)
+    loads[1].wait()
     update = jnp.dot(second[...], hidden[...], preferred_element_type=f32)
     for s in range(shards):
         rows = slice(s * depth, (s + 1) * depth)
@@ -161,11 +176,11 @@
     ]
     for copy in copies:
         copy.start()
-    for k in range(chips):
+    for k in range(shards // cores):
         for g in range(cores):
             at = (k * cores + g) * depth
-            source = (chip ^ k) * cores + (core if g == 0 else 1 - core)
-            moved[at : at + depth, :] = fresh[source]
+            moved[at : at + depth, :] = fresh[(chip ^ k) * cores + (core if g == 0 else 1 - core)]
+    loads[2].wait()
     rows = jnp.dot(env[...], moved[...], preferred_element_type=f32).astype(bf16)
     per = rows.shape[0] // shards
     for s in range(shards):
@@ -258,25 +273,36 @@
     for k in order:
         mine += [shifted[k]] + [flip_dom(shifted[k], j) for j in range(1, domains)]
     others = [other_core(array) for array in mine]
+    matrices = pl.pallas_call(
+        functools.partial(assemble_kernel, quarters=domains, order=order),
+        out_shape=[
+            pltpu.HBM((total, total), bf16),
+            pltpu.HBM((total, total), bf16),
+            pltpu.HBM((channels, total), bf16),
+        ],
+        in_specs=[in_vmem] * (2 * len(mine)),
+        out_specs=[in_vmem] * 3,
+        compiler_params=grant(20),
+        name="assemble",
+    )(*[array if array.ndim == 3 else stay(array) for array in mine + others])
     *new_rows, weight_rows = pl.pallas_call(
-        functools.partial(mlp_kernel, quarters=domains, chips=chips, chan=chan, order=order),
+        functools.partial(mlp_kernel, quarters=domains),
         out_shape=[pltpu.HBM((depth, edges), bf16)] * shards
         + [pltpu.HBM((shards, channels // shards, edges), bf16)],
-        in_specs=[in_vmem] * (1 + 2 * len(mine)),
+        in_specs=[in_vmem] + [in_hbm] * 3,
         out_specs=[in_hbm] * (shards + 1),
-        scratch_shapes=[
-            pltpu.VMEM((total, total), bf16),
-            pltpu.VMEM((total, total), bf16),
-            pltpu.VMEM((channels, total), bf16),
+        scratch_shapes=[pltpu.VMEM(array.shape, bf16) for array in matrices]
+        + [
+            pltpu.SemaphoreType.DMA((3,)),
             pltpu.VMEM((total, edges), bf16),
             pltpu.VMEM((total, edges), bf16),
             pltpu.VMEM((shards, depth, edges), bf16),
             pltpu.VMEM((shards, channels // shards, edges), bf16),
             pltpu.SemaphoreType.DMA((shards + 1,)),
         ],
-        compiler_params=grant(28),
+        compiler_params=grant(24),
         name="mlp",
-    )(edge_rows, *mine, *others)
+    )(edge_rows, *[stay(array) for array in matrices])
     weights = swap_blocks(weight_rows, "tp")
     back = {0: new_rows[0]}
     for s in range(1, shards):
@@ -343,8 +369,8 @@
 
 
 def invariants_kernel(dest_ref, w_ref, h_ref, *refs):
-    domains = len(refs) - 3
-    out_ref, token_ref, env = refs[domains:]
+    domains = len(refs) - 5
+    result_ref, token_ref, env, out_ref, sems = refs[domains:]
     token_ref[...] = jnp.zeros_like(token_ref)
     shards, chan, edges = w_ref.shape
     atoms = env.shape[2]
@@ -367,9 +393,16 @@
             out_ref[0, :, pl.ds(at, lanes)] = products[0] * weight
             out_ref[1, :, pl.ds(at, lanes)] = sum(products[2:4], products[1]) * weight
             out_ref[2, :, pl.ds(at, lanes)] = sum(products[5:9], products[4]) * weight
+        leave(s).start()
         return carry
 
+    def leave(s):
+        chunk = (slice(None), slice(None), pl.ds(pl.multiple_of(s * edges, lanes), edges))
+        return pltpu.make_async_copy(out_ref.at[chunk], result_ref.at[chunk], sems.at[s])
+
     lax.fori_loop(0, shards, step, 0)
+    for s in range(shards):
+        leave(s).wait()
 
 
 def on_device(
@@ -439,12 +472,16 @@
     invariants, token = pl.pallas_call(
         invariants_kernel,
         out_shape=(
-            jax.ShapeDtypeStruct((3, chan, edges), f32),
+            pltpu.HBM((3, chan, edges), f32),
             jax.ShapeDtypeStruct((8, lanes), f32),
         ),
         in_specs=[in_smem] + [in_vmem] * (2 + domains),
-        out_specs=(in_vmem, in_vmem),
-        scratch_shapes=[pltpu.VMEM((domains, rows, atoms), bf16)],
+        out_specs=(in_hbm, in_vmem),
+        scratch_shapes=[
+            pltpu.VMEM((domains, rows, atoms), bf16),
+            pltpu.VMEM((3, chan, edges), f32),
+            pltpu.SemaphoreType.DMA((shards,)),
+        ],
         compiler_params=grant(10),
         name="invariants",
     )(target, weights, harmonic, *looked)

time: 145 us -> 135 us (0.931)
  local copies, waits for them, and re-layouts: 14.3 us -> 1.23 us
  waiting for transfers between devices: 52.1 us -> 45.8 us
  Pallas kernels: 16.9 us -> 22 us
  starting transfers between devices: 45.2 us -> 49.8 us
    unnamed x59 -> x43, local copies, waits for them, and re-layouts: 14.2 us -> 1.14 us
    ppermute x23, starting transfers between devices: 24.6 us -> 29.9 us  [flip_tp(): return lax.ppermute(array, 'tp', [(t, t ^ mask) for t in range(count)])]
    pallas_call x2 -> x3, Pallas kernels: 9.53 us -> 14.6 us  [the longest x1 5.7 us: spread_mlp(): pl.pallas_call(functools.partial(mlp_kernel, quarters=domains), out_shape...]
    ppermute x15, waiting for transfers between devices: 4.67 us -> 0.49 us  [flip_dom(): return lax.ppermute(array, 'dom', [(i, i ^ mask) for i in range(count)])]
    ppermute x23, waiting for transfers between devices: 47.4 us -> 45.3 us  [flip_tp(): return lax.ppermute(array, 'tp', [(t, t ^ mask) for t in range(count)])]
  transfers between devices with their start and end apart: 39 -> 39, of which waited for: 10 -> 8; matrix products, arithmetic and copies ran while one was open for 1% -> 2% of each run, Pallas kernels for 3% -> 7%
where the time goes in v1:
time: 135 us
  starting transfers between devices  49.8 us (37%)
  waiting for transfers between devices  45.8 us (34%)
  Pallas kernels  22 us (16%)
  blocking collectives  13.2 us (10%)
  other arithmetic  2.01 us (1%)
    ppermute x23, waiting for transfers between devices, flip_tp(): return lax.ppermute(array, 'tp', [(t, t ^ mask) for t in range(count)])  45.3 us
    ppermute x23, starting transfers between devices, flip_tp(): return lax.ppermute(array, 'tp', [(t, t ^ mask) for t in range(count)])  29.9 us
    ppermute x15, starting transfers between devices, flip_dom(): return lax.ppermute(array, 'dom', [(i, i ^ mask) for i in range(count)])  14.3 us
    all_to_all x1, blocking collectives, swap_blocks(): return lax.all_to_all(array, axis, split_axis=0, concat_axis=0, tiled=True)  13.2 us
    pallas_call x1, Pallas kernels, spread_mlp(): pl.pallas_call(functools.partial(mlp_kernel, quarters=domains), out_shape...  5.7 us
    all_to_all x1, starting transfers between devices, swap_blocks(): return lax.all_to_all(array, axis, split_axis=0, concat_axis=0, tiled=True)  5.62 us
    pallas_call x1, Pallas kernels, spread_mlp(): pl.pallas_call(functools.partial(assemble_kernel, quarters=domains, order...  5.55 us
    pallas_call x1, Pallas kernels, on_device(): pl.pallas_call(invariants_kernel, out_shape=(pltpu.HBM((3, chan, edges),...  3.34 us
  transfers between devices with their start and end apart: 39, of which 8 were waited for; matrix products, arithmetic and copies ran while one was open for 2% of the time, Pallas kernels for 7%

profile of v1, /device:TPU:9, one launch (start us, length us, event | category | flops | bytes accessed | tf_op | source)
XLA Modules:
  0.0 134.9 jit_solution(13646677127330506947)
XLA Ops:
  0.6 1.4 %prepare.1 = (bf16[4,576,128]{2,1,0:T(8,128)(2,1)S(1)}, bf16[576,128]{1,0:T(8,128)(2,1)S(1)}) custom-call(bf16[1024,128]{1,0:T(8,128)(2,1)} %refs_0_.1, bf16[128,1024]{1,0:T(8,128)(2,1)} %refs_1_.1, bf16[128,256]{1,0:T(8,128)(2,1)} %refs_2_.1), custom_call_target="tpu_custom_call" | custom-call | tf_op jit(solution)/shard_map/prepare/pallas_call | solution.py:243
  2.1 2.1 %split.1 = bf16[8,128,512]{2,1,0:T(8,128)(2,1)} custom-call(bf16[128,4096]{1,0:T(8,128)(2,1)} %x_ref.1, bf16[576,128]{1,0:T(8,128)(2,1)S(1)} %get-tuple-element.26.tie_ref), custom_call_target="tpu_custom_call" | custom-call | tf_op jit(solution)/shard_map/split/pallas_call | solution.py:256
  4.2 5.6 %all-to-all-start = ((bf16[8,128,512]{2,1,0:T(8,128)(2,1)}), bf16[8,128,512]{2,1,0:T(8,128)(2,1)S(1)}, u32[]{:S(2)}, u32[]{:S(2)}) async-start(bf16[8,128,512]{2,1,0:T(8,128)(2,1)} %split.1), calls=%async_computation | async-start | bytes 2097152 | tf_op jit(solution)/shard_map/all_to_all | solution.py:62
  9.9 2.3 %collective-permute-start.4 = (bf16[576,128]{1,0:T(8,128)(2,1)S(1)}, bf16[576,128]{1,0:T(8,128)(2,1)S(1)}, u32[]{:S(2)}, u32[]{:S(2)}) collective-permute-start(bf16[576,128]{1,0:T(8,128)(2,1)S(1)} %get-tuple-element.26.tie_ref), channel_id=1, source_target_pairs={{0,6},{1,7},{2,4},{3,5},{4,2},{5,3},{6,0},{7,1},{8,14},{9,15},{10,... | collective-permute-start | bytes 442376 | tf_op jit(solution)/shard_map/ppermute | solution.py:76
  13.3 17.9 %collective-permute-done.refs_1_ = bf16[576,128]{1,0:T(8,128)(2,1)S(1)} collective-permute-done((bf16[576,128]{1,0:T(8,128)(2,1)S(1)}, bf16[576,128]{1,0:T(8,128)(2,1)S(1)}, u32[]{:S(2)}, u32[]{:S(2)}) %collective-permute-start) | collective-permute-done | bytes 147488 | tf_op jit(solution)/shard_map/ppermute | solution.py:76
  32.4 1.2 collective-permute-start.2
  33.9 9.9 %collective-permute-done.4.refs_5_ = bf16[576,128]{1,0:T(8,128)(2,1)S(1)} collective-permute-done((bf16[576,128]{1,0:T(8,128)(2,1)S(1)}, bf16[576,128]{1,0:T(8,128)(2,1)S(1)}, u32[]{:S(2)}, u32[]{:S(2)}) %collective-permute-start.4) | collective-permute-done | bytes 147488 | tf_op jit(solution)/shard_map/ppermute | solution.py:76
  50.5 5.8 %collective-permute-start.13 = (bf16[576,128]{1,0:T(8,128)(2,1)S(1)}, bf16[576,128]{1,0:T(8,128)(2,1)S(1)}, u32[]{:S(2)}, u32[]{:S(2)}) collective-permute-start(bf16[576,128]{1,0:T(8,128)(2,1)S(1)} %collective-permute-done.refs_1_), channel_id=1, source_target_pairs={{0,1},{1,0},{2,3},{3,2},{4,5},{5,4},{6,7},{7,6},{8,9},{9,8},{10,11... | collective-permute-start | bytes 442376 | tf_op jit(solution)/shard_map/ppermute | solution.py:76
  56.3 2.0 %collective-permute-start.21 = (bf16[576,128]{1,0:T(8,128)(2,1)S(1)}, bf16[576,128]{1,0:T(8,128)(2,1)S(1)}, u32[]{:S(2)}, u32[]{:S(2)}) collective-permute-start(bf16[576,128]{1,0:T(8,128)(2,1)S(1)} %collective-permute-done.8.refs_9_), channel_id=1, source_target_pairs={{0,1},{1,0},{2,3},{3,2},{4,5},{5,4},{6,7},{7,6},{8,9},{9,8},{10,11... | collective-permute-start | bytes 442376 | tf_op jit(solution)/shard_map/ppermute | solution.py:76
  58.4 3.2 %collective-permute-start.14 = (bf16[576,128]{1,0:T(8,128)(2,1)S(1)}, bf16[576,128]{1,0:T(8,128)(2,1)S(1)}, u32[]{:S(2)}, u32[]{:S(2)}) collective-permute-start(bf16[576,128]{1,0:T(8,128)(2,1)S(1)} %collective-permute-done.1.refs_2_), channel_id=1, source_target_pairs={{0,1},{1,0},{2,3},{3,2},{4,5},{5,4},{6,7},{7,6},{8,9},{9,8},{10,11... | collective-permute-start | bytes 442376 | tf_op jit(solution)/shard_map/ppermute | solution.py:76
  67.4 5.5 %assemble.1 = (bf16[1024,1024]{1,0:T(8,128)(2,1)}, bf16[1024,1024]{1,0:T(8,128)(2,1)}, bf16[256,1024]{1,0:T(8,128)(2,1)}) custom-call(bf16[4,576,128]{2,1,0:T(8,128)(2,1)S(1)} %get-tuple-element.28.refs_0_, bf16[576,128]{1,0:T(8,128)(2,1)} %copy-done.2, bf16[576,128]{1,0:T(8,128)(2,1)} %copy-done.5, bf16[576,128]{1,0:T(8,128)(2,1)} %copy-done.6, ...), custom_call_target="tpu_custom_call" | custom-call | tf_op jit(solution)/shard_map/assemble/pallas_call | solution.py:276
  73.0 5.7 %mlp.1 = (bf16[128,512]{1,0:T(8,128)(2,1)}, bf16[128,512]{1,0:T(8,128)(2,1)}, bf16[128,512]{1,0:T(8,128)(2,1)}, bf16[128,512]{1,0:T(8,128)(2,1)}, bf16[128,512]{...) custom-call(bf16[8,128,512]{2,1,0:T(8,128)(2,1)S(1)} %all-to-all-don, ...), custom_call_target="tpu_custom_call" | custom-call | tf_op jit(solution)/shard_map/mlp/pallas_call | solution.py:288
  78.7 13.2 %all_to_all.10.w_ref = bf16[8,32,512]{2,1,0:T(8,128)(2,1)S(1)} all-to-all(bf16[8,32,512]{2,1,0:T(8,128)(2,1)} %get-tuple-element.32), channel_id=1, replica_groups=mesh['dom'=4,'tp'=8] {'tp'}, dimensions={0} | all-to-all | bytes 524288 | tf_op jit(solution)/shard_map/all_to_all | solution.py:62
  91.9 2.8 %sums.1 = (f32[288,128]{1,0:T(8,128)S(1)}, bf16[288,128]{1,0:T(8,128)(2,1)S(1)}, bf16[288,128]{1,0:T(8,128)(2,1)S(1)}, bf16[288,128]{1,0:T(8,128)(2,1)S(1)}) custom-call(s32[32]{0:T(128)} %bitcast.18, bf16[8,32,512]{2,1,0:T(8,128)(2,1)S(1)} %all_to_all.10.w_ref, f32[10,32,128]{2,1,0:T(8,128)S(1)} %geometry.1.h_ref), custom_call_target="tpu_custom_call" | custom-call | tf_op jit(solution)/shard_map/sums/pallas_call | solution.py:456
  94.7 1.3 collective-permute-start.25
  96.0 1.3 collective-permute-start.26
  97.4 1.9 %collective-permute-start.31 = (bf16[128,512]{1,0:T(8,128)(2,1)}, bf16[128,512]{1,0:T(8,128)(2,1)S(1)}, u32[]{:S(2)}, u32[]{:S(2)}) collective-permute-start(bf16[128,512]{1,0:T(8,128)(2,1)} %get-tuple-element.41), channel_id=1, source_target_pairs={{0,1},{1,0},{2,3},{3,2},{4,5},{5,4},{6,7},{7,6},{8,9},{9,8},{10,11... | collective-permute-start | bytes 393224 | tf_op jit(solution)/shard_map/ppermute | solution.py:76
  99.3 1.7 %collective-permute-start.32 = (bf16[128,512]{1,0:T(8,128)(2,1)}, bf16[128,512]{1,0:T(8,128)(2,1)S(1)}, u32[]{:S(2)}, u32[]{:S(2)}) collective-permute-start(bf16[128,512]{1,0:T(8,128)(2,1)} %get-tuple-element.42), channel_id=1, source_target_pairs={{0,2},{1,3},{2,0},{3,1},{4,6},{5,7},{6,4},{7,5},{8,10},{9,11},{10,... | collective-permute-start | bytes 393224 | tf_op jit(solution)/shard_map/ppermute | solution.py:76
  104.2 5.0 %collective-permute-start.33 = (bf16[128,512]{1,0:T(8,128)(2,1)}, bf16[128,512]{1,0:T(8,128)(2,1)S(1)}, u32[]{:S(2)}, u32[]{:S(2)}) collective-permute-start(bf16[128,512]{1,0:T(8,128)(2,1)} %get-tuple-element.43), channel_id=1, source_target_pairs={{0,3},{1,2},{2,1},{3,0},{4,7},{5,6},{6,5},{7,4},{8,11},{9,10},{10,... | collective-permute-start | bytes 393224 | tf_op jit(solution)/shard_map/ppermute | solution.py:76
  111.3 2.4 %collective-permute-start.37 = (bf16[128,512]{1,0:T(8,128)(2,1)}, bf16[128,512]{1,0:T(8,128)(2,1)S(1)}, u32[]{:S(2)}, u32[]{:S(2)}) collective-permute-start(bf16[128,512]{1,0:T(8,128)(2,1)} %get-tuple-element.47), channel_id=1, source_target_pairs={{0,7},{1,6},{2,5},{3,4},{4,3},{5,2},{6,1},{7,0},{8,15},{9,14},{10,... | collective-permute-start | bytes 393224 | tf_op jit(solution)/shard_map/ppermute | solution.py:76
  114.3 3.3 %invariants.1 = (f32[3,32,4096]{2,1,0:T(8,128)}, f32[8,128]{1,0:T(8,128)S(1)}) custom-call(s32[32]{0:T(128)} %bitcast.19, bf16[8,32,512]{2,1,0:T(8,128)(2,1)S(1)} %all_to_all.10.w_ref, f32[10,32,128]{2,1,0:T(8,128)S(1)} %geometry.1.h_ref, bf16[288,128]{1,0:T(8,128)(2,1)S(1)} %get-tuple-element.49.refs_0_, ...), custom_call_target="tpu_custom_call" | custom-call | tf_op jit(solution)/shard_map/invariants/pallas_call | solution.py:472
  117.7 8.8 %collective-permute-done.35.refs_5_ = bf16[128,512]{1,0:T(8,128)(2,1)S(1)} collective-permute-done((bf16[128,512]{1,0:T(8,128)(2,1)}, bf16[128,512]{1,0:T(8,128)(2,1)S(1)}, u32[]{:S(2)}, u32[]{:S(2)}) %collective-permute-start.35) | collective-permute-done | bytes 131104 | tf_op jit(solution)/shard_map/ppermute | solution.py:76
  126.5 4.0 %collective-permute-done.36.refs_6_ = bf16[128,512]{1,0:T(8,128)(2,1)S(1)} collective-permute-done((bf16[128,512]{1,0:T(8,128)(2,1)}, bf16[128,512]{1,0:T(8,128)(2,1)S(1)}, u32[]{:S(2)}, u32[]{:S(2)}) %collective-permute-start.36) | collective-permute-done | bytes 131104 | tf_op jit(solution)/shard_map/ppermute | solution.py:76
  130.5 3.4 %collective-permute-done.37.refs_7_ = bf16[128,512]{1,0:T(8,128)(2,1)S(1)} collective-permute-done((bf16[128,512]{1,0:T(8,128)(2,1)}, bf16[128,512]{1,0:T(8,128)(2,1)S(1)}, u32[]{:S(2)}, u32[]{:S(2)}) %collective-permute-start.37) | collective-permute-done | bytes 131104 | tf_op jit(solution)/shard_map/ppermute | solution.py:76
  (111 shorter events, 22.3 us)
Async XLA Ops:
  4.2 68.8 %all-to-all-start = ((bf16[8,128,512]{2,1,0:T(8,128)(2,1)}), bf16[8,128,512]{2,1,0:T(8,128)(2,1)S(1)}, u32[]{:S(2)}, u32[]{:S(2)}) async-start(bf16[8,128,512]{2,1,0:T(8,128)(2,1)} %split.1), calls=%async_computation | async-start | bytes 2097152 | tf_op jit(solution)/shard_map/all_to_all | solution.py:62
  9.8 21.4 %collective-permute-start = (bf16[576,128]{1,0:T(8,128)(2,1)S(1)}, bf16[576,128]{1,0:T(8,128)(2,1)S(1)}, u32[]{:S(2)}, u32[]{:S(2)}) collective-permute-start(bf16[576,128]{1,0:T(8,128)(2,1)S(1)} %get-tuple-element.26.tie_ref), channel_id=1, source_target_pairs={{0,2},{1,3},{2,0},{3,1},{4,6},{5,7},{6,4},{7,5},{8,10},{9,11},{10,... | collective-permute-start | bytes 442376 | tf_op jit(solution)/shard_map/ppermute | solution.py:76
  9.9 33.9 %collective-permute-start.4 = (bf16[576,128]{1,0:T(8,128)(2,1)S(1)}, bf16[576,128]{1,0:T(8,128)(2,1)S(1)}, u32[]{:S(2)}, u32[]{:S(2)}) collective-permute-start(bf16[576,128]{1,0:T(8,128)(2,1)S(1)} %get-tuple-element.26.tie_ref), channel_id=1, source_target_pairs={{0,6},{1,7},{2,4},{3,5},{4,2},{5,3},{6,0},{7,1},{8,14},{9,15},{10,... | collective-permute-start | bytes 442376 | tf_op jit(solution)/shard_map/ppermute | solution.py:76
  12.2 33.2 %collective-permute-start.8 = (bf16[576,128]{1,0:T(8,128)(2,1)S(1)}, bf16[576,128]{1,0:T(8,128)(2,1)S(1)}, u32[]{:S(2)}, u32[]{:S(2)}) collective-permute-start(bf16[576,128]{1,0:T(8,128)(2,1)S(1)} %get-tuple-element.26.tie_ref), channel_id=1, source_target_pairs={{0,4},{1,5},{2,6},{3,7},{4,0},{5,1},{6,2},{7,3},{8,12},{9,13},{10,... | collective-permute-start | bytes 442376 | tf_op jit(solution)/shard_map/ppermute | solution.py:76
  31.2 15.4 %collective-permute-start.1 = (bf16[576,128]{1,0:T(8,128)(2,1)S(1)}, bf16[576,128]{1,0:T(8,128)(2,1)S(1)}, u32[]{:S(2)}, u32[]{:S(2)}) collective-permute-start(bf16[576,128]{1,0:T(8,128)(2,1)S(1)} %collective-permute-done.refs_1_), channel_id=1, source_target_pairs={{0,8},{8,0},{16,24},{24,16},{1,9},{9,1},{17,25},{25,17},{2,10},{10... | collective-permute-start | bytes 442376 | tf_op jit(solution)/shard_map/ppermute | solution.py:67
  32.4 15.4 %collective-permute-start.2 = (bf16[576,128]{1,0:T(8,128)(2,1)S(1)}, bf16[576,128]{1,0:T(8,128)(2,1)S(1)}, u32[]{:S(2)}, u32[]{:S(2)}) collective-permute-start(bf16[576,128]{1,0:T(8,128)(2,1)S(1)} %collective-permute-done.refs_1_), channel_id=1, source_target_pairs={{0,16},{8,24},{16,0},{24,8},{1,17},{9,25},{17,1},{25,9},{2,18},{10... | collective-permute-start | bytes 442376 | tf_op jit(solution)/shard_map/ppermute | solution.py:67
  33.7 14.4 %collective-permute-start.3 = (bf16[576,128]{1,0:T(8,128)(2,1)S(1)}, bf16[576,128]{1,0:T(8,128)(2,1)S(1)}, u32[]{:S(2)}, u32[]{:S(2)}) collective-permute-start(bf16[576,128]{1,0:T(8,128)(2,1)S(1)} %collective-permute-done.refs_1_), channel_id=1, source_target_pairs={{0,24},{8,16},{16,8},{24,0},{1,25},{9,17},{17,9},{25,1},{2,26},{10... | collective-permute-start | bytes 442376 | tf_op jit(solution)/shard_map/ppermute | solution.py:67
  46.7 9.6 %collective-permute-start.7 = (bf16[576,128]{1,0:T(8,128)(2,1)S(1)}, bf16[576,128]{1,0:T(8,128)(2,1)}, u32[]{:S(2)}, u32[]{:S(2)}) collective-permute-start(bf16[576,128]{1,0:T(8,128)(2,1)S(1)} %collective-permute-done.4.refs_5_), channel_id=1, source_target_pairs={{0,24},{8,16},{16,8},{24,0},{1,25},{9,17},{17,9},{25,1},{2,26},{10... | collective-permute-start | bytes 442376 | tf_op jit(solution)/shard_map/ppermute | solution.py:67
  47.8 8.5 %collective-permute-start.9 = (bf16[576,128]{1,0:T(8,128)(2,1)S(1)}, bf16[576,128]{1,0:T(8,128)(2,1)}, u32[]{:S(2)}, u32[]{:S(2)}) collective-permute-start(bf16[576,128]{1,0:T(8,128)(2,1)S(1)} %collective-permute-done.8.refs_9_), channel_id=1, source_target_pairs={{0,8},{8,0},{16,24},{24,16},{1,9},{9,1},{17,25},{25,17},{2,10},{10... | collective-permute-start | bytes 442376 | tf_op jit(solution)/shard_map/ppermute | solution.py:67
  48.1 10.3 %collective-permute-start.10 = (bf16[576,128]{1,0:T(8,128)(2,1)S(1)}, bf16[576,128]{1,0:T(8,128)(2,1)}, u32[]{:S(2)}, u32[]{:S(2)}) collective-permute-start(bf16[576,128]{1,0:T(8,128)(2,1)S(1)} %collective-permute-done.8.refs_9_), channel_id=1, source_target_pairs={{0,16},{8,24},{16,0},{24,8},{1,17},{9,25},{17,1},{25,9},{2,18},{10... | collective-permute-start | bytes 442376 | tf_op jit(solution)/shard_map/ppermute | solution.py:67
  49.3 12.3 %collective-permute-start.11 = (bf16[576,128]{1,0:T(8,128)(2,1)S(1)}, bf16[576,128]{1,0:T(8,128)(2,1)}, u32[]{:S(2)}, u32[]{:S(2)}) collective-permute-start(bf16[576,128]{1,0:T(8,128)(2,1)S(1)} %collective-permute-done.8.refs_9_), channel_id=1, source_target_pairs={{0,24},{8,16},{16,8},{24,0},{1,25},{9,17},{17,9},{25,1},{2,26},{10... | collective-permute-start | bytes 442376 | tf_op jit(solution)/shard_map/ppermute | solution.py:67
  50.5 11.1 %collective-permute-start.13 = (bf16[576,128]{1,0:T(8,128)(2,1)S(1)}, bf16[576,128]{1,0:T(8,128)(2,1)S(1)}, u32[]{:S(2)}, u32[]{:S(2)}) collective-permute-start(bf16[576,128]{1,0:T(8,128)(2,1)S(1)} %collective-permute-done.refs_1_), channel_id=1, source_target_pairs={{0,1},{1,0},{2,3},{3,2},{4,5},{5,4},{6,7},{7,6},{8,9},{9,8},{10,11... | collective-permute-start | bytes 442376 | tf_op jit(solution)/shard_map/ppermute | solution.py:76
  56.3 5.9 %collective-permute-start.21 = (bf16[576,128]{1,0:T(8,128)(2,1)S(1)}, bf16[576,128]{1,0:T(8,128)(2,1)S(1)}, u32[]{:S(2)}, u32[]{:S(2)}) collective-permute-start(bf16[576,128]{1,0:T(8,128)(2,1)S(1)} %collective-permute-done.8.refs_9_), channel_id=1, source_target_pairs={{0,1},{1,0},{2,3},{3,2},{4,5},{5,4},{6,7},{7,6},{8,9},{9,8},{10,11... | collective-permute-start | bytes 442376 | tf_op jit(solution)/shard_map/ppermute | solution.py:76
  94.7 6.3 %collective-permute-start.25 = (bf16[288,128]{1,0:T(8,128)(2,1)S(1)}, bf16[288,128]{1,0:T(8,128)(2,1)S(1)}, u32[]{:S(2)}, u32[]{:S(2)}) collective-permute-start(bf16[288,128]{1,0:T(8,128)(2,1)S(1)} %get-tuple-element.35), channel_id=1, source_target_pairs={{0,8},{8,0},{16,24},{24,16},{1,9},{9,1},{17,25},{25,17},{2,10},{10... | collective-permute-start | bytes 221192 | tf_op jit(solution)/shard_map/ppermute | solution.py:67
  97.4 6.8 %collective-permute-start.31 = (bf16[128,512]{1,0:T(8,128)(2,1)}, bf16[128,512]{1,0:T(8,128)(2,1)S(1)}, u32[]{:S(2)}, u32[]{:S(2)}) collective-permute-start(bf16[128,512]{1,0:T(8,128)(2,1)} %get-tuple-element.41), channel_id=1, source_target_pairs={{0,1},{1,0},{2,3},{3,2},{4,5},{5,4},{6,7},{7,6},{8,9},{9,8},{10,11... | collective-permute-start | bytes 393224 | tf_op jit(solution)/shard_map/ppermute | solution.py:76
  99.3 10.0 %collective-permute-start.32 = (bf16[128,512]{1,0:T(8,128)(2,1)}, bf16[128,512]{1,0:T(8,128)(2,1)S(1)}, u32[]{:S(2)}, u32[]{:S(2)}) collective-permute-start(bf16[128,512]{1,0:T(8,128)(2,1)} %get-tuple-element.42), channel_id=1, source_target_pairs={{0,2},{1,3},{2,0},{3,1},{4,6},{5,7},{6,4},{7,5},{8,10},{9,11},{10,... | collective-permute-start | bytes 393224 | tf_op jit(solution)/shard_map/ppermute | solution.py:76
  101.5 7.8 %collective-permute-start.28 = (bf16[288,128]{1,0:T(8,128)(2,1)S(1)}, bf16[288,128]{1,0:T(8,128)(2,1)S(1)}, u32[]{:S(2)}, u32[]{:S(2)}) collective-permute-start(bf16[288,128]{1,0:T(8,128)(2,1)S(1)} %get-tuple-element.49.refs_0_), channel_id=1, source_target_pairs={{0,8},{8,0},{16,24},{24,16},{1,9},{9,1},{17,25},{25,17},{2,10},{10... | collective-permute-start | bytes 221192 | tf_op jit(solution)/shard_map/ppermute | solution.py:67
  102.4 7.9 %collective-permute-start.29 = (bf16[288,128]{1,0:T(8,128)(2,1)S(1)}, bf16[288,128]{1,0:T(8,128)(2,1)S(1)}, u32[]{:S(2)}, u32[]{:S(2)}) collective-permute-start(bf16[288,128]{1,0:T(8,128)(2,1)S(1)} %get-tuple-element.49.refs_0_), channel_id=1, source_target_pairs={{0,16},{8,24},{16,0},{24,8},{1,17},{9,25},{17,1},{25,9},{2,18},{10... | collective-permute-start | bytes 221192 | tf_op jit(solution)/shard_map/ppermute | solution.py:67
  103.5 7.7 %collective-permute-start.30 = (bf16[288,128]{1,0:T(8,128)(2,1)S(1)}, bf16[288,128]{1,0:T(8,128)(2,1)S(1)}, u32[]{:S(2)}, u32[]{:S(2)}) collective-permute-start(bf16[288,128]{1,0:T(8,128)(2,1)S(1)} %get-tuple-element.49.refs_0_), channel_id=1, source_target_pairs={{0,24},{8,16},{16,8},{24,0},{1,25},{9,17},{17,9},{25,1},{2,26},{10... | collective-permute-start | bytes 221192 | tf_op jit(solution)/shard_map/ppermute | solution.py:67
  104.2 13.5 %collective-permute-start.33 = (bf16[128,512]{1,0:T(8,128)(2,1)}, bf16[128,512]{1,0:T(8,128)(2,1)S(1)}, u32[]{:S(2)}, u32[]{:S(2)}) collective-permute-start(bf16[128,512]{1,0:T(8,128)(2,1)} %get-tuple-element.43), channel_id=1, source_target_pairs={{0,3},{1,2},{2,1},{3,0},{4,7},{5,6},{6,5},{7,4},{8,11},{9,10},{10,... | collective-permute-start | bytes 393224 | tf_op jit(solution)/shard_map/ppermute | solution.py:76
  109.2 8.4 %collective-permute-start.34 = (bf16[128,512]{1,0:T(8,128)(2,1)}, bf16[128,512]{1,0:T(8,128)(2,1)S(1)}, u32[]{:S(2)}, u32[]{:S(2)}) collective-permute-start(bf16[128,512]{1,0:T(8,128)(2,1)} %get-tuple-element.44), channel_id=1, source_target_pairs={{0,4},{1,5},{2,6},{3,7},{4,0},{5,1},{6,2},{7,3},{8,12},{9,13},{10,... | collective-permute-start | bytes 393224 | tf_op jit(solution)/shard_map/ppermute | solution.py:76
  109.2 17.3 %collective-permute-start.35 = (bf16[128,512]{1,0:T(8,128)(2,1)}, bf16[128,512]{1,0:T(8,128)(2,1)S(1)}, u32[]{:S(2)}, u32[]{:S(2)}) collective-permute-start(bf16[128,512]{1,0:T(8,128)(2,1)} %get-tuple-element.45), channel_id=1, source_target_pairs={{0,5},{1,4},{2,7},{3,6},{4,1},{5,0},{6,3},{7,2},{8,13},{9,12},{10,... | collective-permute-start | bytes 393224 | tf_op jit(solution)/shard_map/ppermute | solution.py:76
  110.3 20.2 %collective-permute-start.36 = (bf16[128,512]{1,0:T(8,128)(2,1)}, bf16[128,512]{1,0:T(8,128)(2,1)S(1)}, u32[]{:S(2)}, u32[]{:S(2)}) collective-permute-start(bf16[128,512]{1,0:T(8,128)(2,1)} %get-tuple-element.46), channel_id=1, source_target_pairs={{0,6},{1,7},{2,4},{3,5},{4,2},{5,3},{6,0},{7,1},{8,14},{9,15},{10,... | collective-permute-start | bytes 393224 | tf_op jit(solution)/shard_map/ppermute | solution.py:76
  111.3 22.6 %collective-permute-start.37 = (bf16[128,512]{1,0:T(8,128)(2,1)}, bf16[128,512]{1,0:T(8,128)(2,1)S(1)}, u32[]{:S(2)}, u32[]{:S(2)}) collective-permute-start(bf16[128,512]{1,0:T(8,128)(2,1)} %get-tuple-element.47), channel_id=1, source_target_pairs={{0,7},{1,6},{2,5},{3,4},{4,3},{5,2},{6,1},{7,0},{8,15},{9,14},{10,... | collective-permute-start | bytes 393224 | tf_op jit(solution)/shard_map/ppermute | solution.py:76
  (36 other events, 555.4 us)

commit v2 on v0

--- a/solution.py
+++ b/solution.py
@@ -301,13 +301,22 @@
     return (lambda tie: latent_new), weights, ties
 
 
-def geometry_kernel(vec_ref, fill_ref, centers_ref, out_ref):
-    vectors = [vec_ref[i] for i in range(3)]
-    ids = lax.broadcasted_iota(jnp.int32, vectors[0].shape, 1)
-    alive = (ids < fill_ref[...]).astype(f32)
-    for m, part in enumerate(harmonics(vectors)):
+def geometry_kernel(fill_ref, table_ref, vec_ref, centers_ref, species_ref, out_ref, gain_ref, rows):
+    species_count, chan = table_ref.shape
+    for b in range(centers_ref.shape[0]):
+        rows[:, b, :] = vec_ref[:, b * lanes : (b + 1) * lanes]
+        ids = lax.broadcasted_iota(jnp.int32, (1, lanes), 1)
+        out_ref[parts, b : b + 1, :] = (ids < fill_ref[b]).astype(f32)
+    alive = out_ref[parts]
+    for m, part in enumerate(harmonics([rows[i] for i in range(3)])):
         out_ref[m] = part * alive
     out_ref[parts] = centers_ref[...].astype(f32)
+    species = species_ref[...]
+    for c in range(chan):
+        gain = jnp.zeros(species.shape, f32)
+        for kind in range(species_count):
+            gain = jnp.where(species == kind, table_ref[kind, c], gain)
+        gain_ref[c : c + 1, :] = gain
 
 
 def select_atoms(h_ref, block, atoms):
@@ -343,8 +352,8 @@
 
 
 def invariants_kernel(dest_ref, w_ref, h_ref, *refs):
-    domains = len(refs) - 3
-    out_ref, token_ref, env = refs[domains:]
+    domains = len(refs) - 5
+    result_ref, token_ref, env, out_ref, sems = refs[domains:]
     token_ref[...] = jnp.zeros_like(token_ref)
     shards, chan, edges = w_ref.shape
     atoms = env.shape[2]
@@ -367,9 +376,16 @@
             out_ref[0, :, pl.ds(at, lanes)] = products[0] * weight
             out_ref[1, :, pl.ds(at, lanes)] = sum(products[2:4], products[1]) * weight
             out_ref[2, :, pl.ds(at, lanes)] = sum(products[5:9], products[4]) * weight
+        leave(s).start()
         return carry
 
+    def leave(s):
+        chunk = (slice(None), slice(None), pl.ds(pl.multiple_of(s * edges, lanes), edges))
+        return pltpu.make_async_copy(out_ref.at[chunk], result_ref.at[chunk], sems.at[s])
+
     lax.fori_loop(0, shards, step, 0)
+    for s in range(shards):
+        leave(s).wait()
 
 
 def on_device(
@@ -398,22 +414,25 @@
         and shards & (shards - 1) == 0
         and domains & (domains - 1) == 0
     )
-    harmonic = pl.pallas_call(
+    harmonic, gain_sel = pl.pallas_call(
         geometry_kernel,
-        out_shape=jax.ShapeDtypeStruct((parts + 1, nblocks, lanes), f32),
-        in_specs=[in_vmem] * 3,
-        out_specs=in_vmem,
+        out_shape=(
+            jax.ShapeDtypeStruct((parts + 1, nblocks, lanes), f32),
+            jax.ShapeDtypeStruct((chan, atoms), f32),
+        ),
+        in_specs=[in_smem] * 2 + [in_vmem] * 3,
+        out_specs=(in_vmem, in_vmem),
+        scratch_shapes=[pltpu.VMEM((3, nblocks, lanes), f32)],
         compiler_params=grant(4),
         name="geometry",
-    )(edge_vec.reshape(3, nblocks, lanes), block_fill[:, None], centers.reshape(nblocks, lanes))
+    )(
+        stay(block_fill),
+        stay(species_gain),
+        edge_vec,
+        centers.reshape(nblocks, lanes),
+        species[None, :],
+    )
     target = stay(block_dest[:, 0])
-    species_ids = jnp.arange(species_gain.shape[0], dtype=jnp.int32)
-    gain_sel = jnp.sum(
-        jnp.where(
-            species[None, None, :] == species_ids[:, None, None], species_gain[:, :, None], 0.0
-        ),
-        axis=0,
-    )
     mlp = spread_mlp if spread else gathered_mlp
     finish, weights, (harmonic, gain_sel) = mlp(
         latent, w_first, w_second, w_env, (harmonic, gain_sel)
@@ -439,12 +458,16 @@
     invariants, token = pl.pallas_call(
         invariants_kernel,
         out_shape=(
-            jax.ShapeDtypeStruct((3, chan, edges), f32),
+            pltpu.HBM((3, chan, edges), f32),
             jax.ShapeDtypeStruct((8, lanes), f32),
         ),
         in_specs=[in_smem] + [in_vmem] * (2 + domains),
-        out_specs=(in_vmem, in_vmem),
-        scratch_shapes=[pltpu.VMEM((domains, rows, atoms), bf16)],
+        out_specs=(in_hbm, in_vmem),
+        scratch_shapes=[
+            pltpu.VMEM((domains, rows, atoms), bf16),
+            pltpu.VMEM((3, chan, edges), f32),
+            pltpu.SemaphoreType.DMA((shards,)),
+        ],
         compiler_params=grant(10),
         name="invariants",
     )(target, weights, harmonic, *looked)

time: 145 us -> 146 us (level)
    unnamed x59 -> x54, local copies, waits for them, and re-layouts: 14.2 us -> 14.2 us
where the time goes in v2:
time: 146 us; the launch traced here: 145 us
  waiting for transfers between devices  52.9 us (36%)
  starting transfers between devices  45.1 us (31%)
  Pallas kernels  17.3 us (12%)
  local copies, waits for them, and re-layouts  14.2 us (10%)
  blocking collectives  14 us (10%)
    ppermute x23, waiting for transfers between devices, flip_tp(): return lax.ppermute(array, 'tp', [(t, t ^ mask) for t in range(count)])  47.2 us
    ppermute x23, starting transfers between devices, flip_tp(): return lax.ppermute(array, 'tp', [(t, t ^ mask) for t in range(count)])  24.7 us
    ppermute x15, starting transfers between devices, flip_dom(): return lax.ppermute(array, 'dom', [(i, i ^ mask) for i in range(count)])  14.6 us
    unnamed x54, local copies, waits for them, and re-layouts  14.2 us
    all_to_all x1, blocking collectives, swap_blocks(): return lax.all_to_all(array, axis, split_axis=0, concat_axis=0, tiled=True)  14 us
    pallas_call x1, Pallas kernels, spread_mlp(): pl.pallas_call(functools.partial(mlp_kernel, quarters=domains, chips=chip...  5.82 us
    all_to_all x1, starting transfers between devices, swap_blocks(): return lax.all_to_all(array, axis, split_axis=0, concat_axis=0, tiled=True)  5.75 us
    ppermute x15, waiting for transfers between devices, flip_dom(): return lax.ppermute(array, 'dom', [(i, i ^ mask) for i in range(count)])  5.67 us
  transfers between devices with their start and end apart: 39, of which 10 were waited for; matrix products, arithmetic and copies ran while one was open for 1% of the time, Pallas kernels for 3%

profile of v2, /device:TPU:9, one launch (start us, length us, event | category | flops | bytes accessed | tf_op | source)
XLA Modules:
  0.0 145.1 jit_solution(18285587269473348246)
XLA Ops:
  2.0 2.1 %split.1 = bf16[8,128,512]{2,1,0:T(8,128)(2,1)} custom-call(bf16[128,4096]{1,0:T(8,128)(2,1)} %x_ref.1, bf16[576,128]{1,0:T(8,128)(2,1)S(1)} %get-tuple-element.25.tie_ref), custom_call_target="tpu_custom_call" | custom-call | tf_op jit(solution)/shard_map/split/pallas_call | solution.py:241
  4.2 5.7 %all-to-all-start = ((bf16[8,128,512]{2,1,0:T(8,128)(2,1)}), bf16[8,128,512]{2,1,0:T(8,128)(2,1)S(1)}, u32[]{:S(2)}, u32[]{:S(2)}) async-start(bf16[8,128,512]{2,1,0:T(8,128)(2,1)} %split.1), calls=%async_computation | async-start | bytes 2097152 | tf_op jit(solution)/shard_map/all_to_all | solution.py:62
  9.9 2.1 %collective-permute-start.8 = (bf16[576,128]{1,0:T(8,128)(2,1)S(1)}, bf16[576,128]{1,0:T(8,128)(2,1)S(1)}, u32[]{:S(2)}, u32[]{:S(2)}) collective-permute-start(bf16[576,128]{1,0:T(8,128)(2,1)S(1)} %get-tuple-element.25.tie_ref), channel_id=1, source_target_pairs={{0,4},{1,5},{2,6},{3,7},{4,0},{5,1},{6,2},{7,3},{8,12},{9,13},{10,... | collective-permute-start | bytes 442376 | tf_op jit(solution)/shard_map/ppermute | solution.py:76
  12.0 1.5 %collective-permute-start = (bf16[576,128]{1,0:T(8,128)(2,1)S(1)}, bf16[576,128]{1,0:T(8,128)(2,1)S(1)}, u32[]{:S(2)}, u32[]{:S(2)}) collective-permute-start(bf16[576,128]{1,0:T(8,128)(2,1)S(1)} %get-tuple-element.25.tie_ref), channel_id=1, source_target_pairs={{0,2},{1,3},{2,0},{3,1},{4,6},{5,7},{6,4},{7,5},{8,10},{9,11},{10,... | collective-permute-start | bytes 442376 | tf_op jit(solution)/shard_map/ppermute | solution.py:76
  13.4 28.9 %collective-permute-done.8.refs_9_ = bf16[576,128]{1,0:T(8,128)(2,1)S(1)} collective-permute-done((bf16[576,128]{1,0:T(8,128)(2,1)S(1)}, bf16[576,128]{1,0:T(8,128)(2,1)S(1)}, u32[]{:S(2)}, u32[]{:S(2)}) %collective-permute-start.8) | collective-permute-done | bytes 147488 | tf_op jit(solution)/shard_map/ppermute | solution.py:76
  42.8 2.2 %collective-permute-start.11 = (bf16[576,128]{1,0:T(8,128)(2,1)S(1)}, bf16[576,128]{1,0:T(8,128)(2,1)S(1)}, u32[]{:S(2)}, u32[]{:S(2)}) collective-permute-start(bf16[576,128]{1,0:T(8,128)(2,1)S(1)} %collective-permute-done.8.refs_9_), channel_id=1, source_target_pairs={{0,24},{8,16},{16,8},{24,0},{1,25},{9,17},{17,9},{25,1},{2,26},{10... | collective-permute-start | bytes 442376 | tf_op jit(solution)/shard_map/ppermute | solution.py:67
  45.2 1.8 %collective-permute-done.4.refs_5_ = bf16[576,128]{1,0:T(8,128)(2,1)S(1)} collective-permute-done((bf16[576,128]{1,0:T(8,128)(2,1)S(1)}, bf16[576,128]{1,0:T(8,128)(2,1)S(1)}, u32[]{:S(2)}, u32[]{:S(2)}) %collective-permute-start.4) | collective-permute-done | bytes 147488 | tf_op jit(solution)/shard_map/ppermute | solution.py:76
  51.0 1.7 %collective-permute-done.10.refs_11_ = bf16[576,128]{1,0:T(8,128)(2,1)S(1)} collective-permute-done((bf16[576,128]{1,0:T(8,128)(2,1)S(1)}, bf16[576,128]{1,0:T(8,128)(2,1)S(1)}, u32[]{:S(2)}, u32[]{:S(2)}) %collective-permute-start.10) | collective-permute-done | bytes 147488 | tf_op jit(solution)/shard_map/ppermute | solution.py:67
  52.7 1.4 collective-permute-start.5
  57.6 1.7 %collective-permute-done.6.refs_7_ = bf16[576,128]{1,0:T(8,128)(2,1)S(1)} collective-permute-done((bf16[576,128]{1,0:T(8,128)(2,1)S(1)}, bf16[576,128]{1,0:T(8,128)(2,1)S(1)}, u32[]{:S(2)}, u32[]{:S(2)}) %collective-permute-start.6) | collective-permute-done | bytes 147488 | tf_op jit(solution)/shard_map/ppermute | solution.py:67
  62.7 2.3 %collective-permute-start.23 = (bf16[576,128]{1,0:T(8,128)(2,1)S(1)}, bf16[576,128]{1,0:T(8,128)(2,1)S(1)}, u32[]{:S(2)}, u32[]{:S(2)}) collective-permute-start(bf16[576,128]{1,0:T(8,128)(2,1)S(1)} %collective-permute-done.10.refs_11_), channel_id=1, source_target_pairs={{0,1},{1,0},{2,3},{3,2},{4,5},{5,4},{6,7},{7,6},{8,9},{9,8},{10,11... | collective-permute-start | bytes 442376 | tf_op jit(solution)/shard_map/ppermute | solution.py:76
  65.0 1.5 %collective-permute-done.2.refs_3_ = bf16[576,128]{1,0:T(8,128)(2,1)} collective-permute-done((bf16[576,128]{1,0:T(8,128)(2,1)S(1)}, bf16[576,128]{1,0:T(8,128)(2,1)}, u32[]{:S(2)}, u32[]{:S(2)}) %collective-permute-start.2) | collective-permute-done | bytes 147488 | tf_op jit(solution)/shard_map/ppermute | solution.py:67
  83.0 5.8 %mlp.1 = (bf16[128,512]{1,0:T(8,128)(2,1)}, bf16[128,512]{1,0:T(8,128)(2,1)}, bf16[128,512]{1,0:T(8,128)(2,1)}, bf16[128,512]{1,0:T(8,128)(2,1)}, bf16[128,512]{...) custom-call(bf16[8,128,512]{2,1,0:T(8,128)(2,1)S(1)} %all-to-all-don, ...), custom_call_target="tpu_custom_call" | custom-call | tf_op jit(solution)/shard_map/mlp/pallas_call | solution.py:261
  88.9 14.0 %all_to_all.10.w_ref = bf16[8,32,512]{2,1,0:T(8,128)(2,1)S(1)} all-to-all(bf16[8,32,512]{2,1,0:T(8,128)(2,1)} %get-tuple-element.30), channel_id=1, replica_groups=mesh['dom'=4,'tp'=8] {'tp'}, dimensions={0} | all-to-all | bytes 524288 | tf_op jit(solution)/shard_map/all_to_all | solution.py:62
  102.9 2.8 %sums.1 = (f32[288,128]{1,0:T(8,128)S(1)}, bf16[288,128]{1,0:T(8,128)(2,1)S(1)}, bf16[288,128]{1,0:T(8,128)(2,1)S(1)}, bf16[288,128]{1,0:T(8,128)(2,1)S(1)}) custom-call(s32[32]{0:T(128)} %bitcast.13, bf16[8,32,512]{2,1,0:T(8,128)(2,1)S(1)} %all_to_all.10.w_ref, f32[10,32,128]{2,1,0:T(8,128)S(1)} %get-tuple-element.31.h_ref), custom_call_target="tpu_custom_call" | custom-call | tf_op jit(solution)/shard_map/sums/pallas_call | solution.py:442
  108.4 1.9 %collective-permute-start.31 = (bf16[128,512]{1,0:T(8,128)(2,1)}, bf16[128,512]{1,0:T(8,128)(2,1)S(1)}, u32[]{:S(2)}, u32[]{:S(2)}) collective-permute-start(bf16[128,512]{1,0:T(8,128)(2,1)} %get-tuple-element.39), channel_id=1, source_target_pairs={{0,1},{1,0},{2,3},{3,2},{4,5},{5,4},{6,7},{7,6},{8,9},{9,8},{10,11... | collective-permute-start | bytes 393224 | tf_op jit(solution)/shard_map/ppermute | solution.py:76
  110.3 1.7 %collective-permute-start.32 = (bf16[128,512]{1,0:T(8,128)(2,1)}, bf16[128,512]{1,0:T(8,128)(2,1)S(1)}, u32[]{:S(2)}, u32[]{:S(2)}) collective-permute-start(bf16[128,512]{1,0:T(8,128)(2,1)} %get-tuple-element.40), channel_id=1, source_target_pairs={{0,2},{1,3},{2,0},{3,1},{4,6},{5,7},{6,4},{7,5},{8,10},{9,11},{10,... | collective-permute-start | bytes 393224 | tf_op jit(solution)/shard_map/ppermute | solution.py:76
  112.0 1.5 %collective-permute-start.30 = (bf16[288,128]{1,0:T(8,128)(2,1)S(1)}, bf16[288,128]{1,0:T(8,128)(2,1)S(1)}, u32[]{:S(2)}, u32[]{:S(2)}) collective-permute-start(bf16[288,128]{1,0:T(8,128)(2,1)S(1)} %get-tuple-element.47.refs_0_), channel_id=1, source_target_pairs={{0,24},{8,16},{16,8},{24,0},{1,25},{9,17},{17,9},{25,1},{2,26},{10... | collective-permute-start | bytes 221192 | tf_op jit(solution)/shard_map/ppermute | solution.py:67
  114.8 4.8 %collective-permute-start.33 = (bf16[128,512]{1,0:T(8,128)(2,1)S(1)}, bf16[128,512]{1,0:T(8,128)(2,1)S(1)}, u32[]{:S(2)}, u32[]{:S(2)}) collective-permute-start(bf16[128,512]{1,0:T(8,128)(2,1)S(1)} %copy-done.26), channel_id=1, source_target_pairs={{0,3},{1,2},{2,1},{3,0},{4,7},{5,6},{6,5},{7,4},{8,11},{9,10},{10,... | collective-permute-start | bytes 393224 | tf_op jit(solution)/shard_map/ppermute | solution.py:76
  119.6 1.6 %collective-permute-start.35 = (bf16[128,512]{1,0:T(8,128)(2,1)S(1)}, bf16[128,512]{1,0:T(8,128)(2,1)S(1)}, u32[]{:S(2)}, u32[]{:S(2)}) collective-permute-start(bf16[128,512]{1,0:T(8,128)(2,1)S(1)} %copy-done.24), channel_id=1, source_target_pairs={{0,5},{1,4},{2,7},{3,6},{4,1},{5,0},{6,3},{7,2},{8,13},{9,12},{10,... | collective-permute-start | bytes 393224 | tf_op jit(solution)/shard_map/ppermute | solution.py:76
  124.7 3.3 %invariants.1 = (f32[3,32,4096]{2,1,0:T(8,128)}, f32[8,128]{1,0:T(8,128)S(1)}) custom-call(s32[32]{0:T(128)} %bitcast.14, bf16[8,32,512]{2,1,0:T(8,128)(2,1)S(1)} %all_to_all.10.w_ref, f32[10,32,128]{2,1,0:T(8,128)S(1)} %get-tuple-element.31.h_ref, bf16[288,128]{1,0:T(8,128)(2,1)S(1)} %get-tuple-element.47.refs_0_, ...), custom_call_target="tpu_custom_call" | custom-call | tf_op jit(solution)/shard_map/invariants/pallas_call | solution.py:458
  128.0 8.5 %collective-permute-done.35.refs_5_ = bf16[128,512]{1,0:T(8,128)(2,1)S(1)} collective-permute-done((bf16[128,512]{1,0:T(8,128)(2,1)S(1)}, bf16[128,512]{1,0:T(8,128)(2,1)S(1)}, u32[]{:S(2)}, u32[]{:S(2)}) %collective-permute-start.35) | collective-permute-done | bytes 131104 | tf_op jit(solution)/shard_map/ppermute | solution.py:76
  136.5 4.1 %collective-permute-done.36.refs_6_ = bf16[128,512]{1,0:T(8,128)(2,1)S(1)} collective-permute-done((bf16[128,512]{1,0:T(8,128)(2,1)S(1)}, bf16[128,512]{1,0:T(8,128)(2,1)S(1)}, u32[]{:S(2)}, u32[]{:S(2)}) %collective-permute-start.36) | collective-permute-done | bytes 131104 | tf_op jit(solution)/shard_map/ppermute | solution.py:76
  140.6 3.4 %collective-permute-done.37.refs_7_ = bf16[128,512]{1,0:T(8,128)(2,1)S(1)} collective-permute-done((bf16[128,512]{1,0:T(8,128)(2,1)S(1)}, bf16[128,512]{1,0:T(8,128)(2,1)S(1)}, u32[]{:S(2)}, u32[]{:S(2)}) %collective-permute-start.37) | collective-permute-done | bytes 131104 | tf_op jit(solution)/shard_map/ppermute | solution.py:76
  (118 shorter events, 37.8 us)
Async XLA Ops:
  4.2 70.1 %all-to-all-start = ((bf16[8,128,512]{2,1,0:T(8,128)(2,1)}), bf16[8,128,512]{2,1,0:T(8,128)(2,1)S(1)}, u32[]{:S(2)}, u32[]{:S(2)}) async-start(bf16[8,128,512]{2,1,0:T(8,128)(2,1)} %split.1), calls=%async_computation | async-start | bytes 2097152 | tf_op jit(solution)/shard_map/all_to_all | solution.py:62
  9.9 32.4 %collective-permute-start.8 = (bf16[576,128]{1,0:T(8,128)(2,1)S(1)}, bf16[576,128]{1,0:T(8,128)(2,1)S(1)}, u32[]{:S(2)}, u32[]{:S(2)}) collective-permute-start(bf16[576,128]{1,0:T(8,128)(2,1)S(1)} %get-tuple-element.25.tie_ref), channel_id=1, source_target_pairs={{0,4},{1,5},{2,6},{3,7},{4,0},{5,1},{6,2},{7,3},{8,12},{9,13},{10,... | collective-permute-start | bytes 442376 | tf_op jit(solution)/shard_map/ppermute | solution.py:76
  12.0 35.1 %collective-permute-start.4 = (bf16[576,128]{1,0:T(8,128)(2,1)S(1)}, bf16[576,128]{1,0:T(8,128)(2,1)S(1)}, u32[]{:S(2)}, u32[]{:S(2)}) collective-permute-start(bf16[576,128]{1,0:T(8,128)(2,1)S(1)} %get-tuple-element.25.tie_ref), channel_id=1, source_target_pairs={{0,6},{1,7},{2,4},{3,5},{4,2},{5,3},{6,0},{7,1},{8,14},{9,15},{10,... | collective-permute-start | bytes 442376 | tf_op jit(solution)/shard_map/ppermute | solution.py:76
  12.0 36.3 %collective-permute-start = (bf16[576,128]{1,0:T(8,128)(2,1)S(1)}, bf16[576,128]{1,0:T(8,128)(2,1)S(1)}, u32[]{:S(2)}, u32[]{:S(2)}) collective-permute-start(bf16[576,128]{1,0:T(8,128)(2,1)S(1)} %get-tuple-element.25.tie_ref), channel_id=1, source_target_pairs={{0,2},{1,3},{2,0},{3,1},{4,6},{5,7},{6,4},{7,5},{8,10},{9,11},{10,... | collective-permute-start | bytes 442376 | tf_op jit(solution)/shard_map/ppermute | solution.py:76
  42.3 7.2 %collective-permute-start.21 = (bf16[576,128]{1,0:T(8,128)(2,1)S(1)}, bf16[576,128]{1,0:T(8,128)(2,1)S(1)}, u32[]{:S(2)}, u32[]{:S(2)}) collective-permute-start(bf16[576,128]{1,0:T(8,128)(2,1)S(1)} %collective-permute-done.8.refs_9_), channel_id=1, source_target_pairs={{0,1},{1,0},{2,3},{3,2},{4,5},{5,4},{6,7},{7,6},{8,9},{9,8},{10,11... | collective-permute-start | bytes 442376 | tf_op jit(solution)/shard_map/ppermute | solution.py:76
  42.8 7.9 %collective-permute-start.11 = (bf16[576,128]{1,0:T(8,128)(2,1)S(1)}, bf16[576,128]{1,0:T(8,128)(2,1)S(1)}, u32[]{:S(2)}, u32[]{:S(2)}) collective-permute-start(bf16[576,128]{1,0:T(8,128)(2,1)S(1)} %collective-permute-done.8.refs_9_), channel_id=1, source_target_pairs={{0,24},{8,16},{16,8},{24,0},{1,25},{9,17},{17,9},{25,1},{2,26},{10... | collective-permute-start | bytes 442376 | tf_op jit(solution)/shard_map/ppermute | solution.py:67
  45.0 7.7 %collective-permute-start.10 = (bf16[576,128]{1,0:T(8,128)(2,1)S(1)}, bf16[576,128]{1,0:T(8,128)(2,1)S(1)}, u32[]{:S(2)}, u32[]{:S(2)}) collective-permute-start(bf16[576,128]{1,0:T(8,128)(2,1)S(1)} %collective-permute-done.8.refs_9_), channel_id=1, source_target_pairs={{0,16},{8,24},{16,0},{24,8},{1,17},{9,25},{17,1},{25,9},{2,18},{10... | collective-permute-start | bytes 442376 | tf_op jit(solution)/shard_map/ppermute | solution.py:67
  47.1 7.1 %collective-permute-start.9 = (bf16[576,128]{1,0:T(8,128)(2,1)S(1)}, bf16[576,128]{1,0:T(8,128)(2,1)S(1)}, u32[]{:S(2)}, u32[]{:S(2)}) collective-permute-start(bf16[576,128]{1,0:T(8,128)(2,1)S(1)} %collective-permute-done.8.refs_9_), channel_id=1, source_target_pairs={{0,8},{8,0},{16,24},{24,16},{1,9},{9,1},{17,25},{25,17},{2,10},{10... | collective-permute-start | bytes 442376 | tf_op jit(solution)/shard_map/ppermute | solution.py:67
  49.5 6.8 %collective-permute-start.7 = (bf16[576,128]{1,0:T(8,128)(2,1)S(1)}, bf16[576,128]{1,0:T(8,128)(2,1)S(1)}, u32[]{:S(2)}, u32[]{:S(2)}) collective-permute-start(bf16[576,128]{1,0:T(8,128)(2,1)S(1)} %collective-permute-done.4.refs_5_), channel_id=1, source_target_pairs={{0,24},{8,16},{16,8},{24,0},{1,25},{9,17},{17,9},{25,1},{2,26},{10... | collective-permute-start | bytes 442376 | tf_op jit(solution)/shard_map/ppermute | solution.py:67
  50.8 8.6 %collective-permute-start.6 = (bf16[576,128]{1,0:T(8,128)(2,1)S(1)}, bf16[576,128]{1,0:T(8,128)(2,1)S(1)}, u32[]{:S(2)}, u32[]{:S(2)}) collective-permute-start(bf16[576,128]{1,0:T(8,128)(2,1)S(1)} %collective-permute-done.4.refs_5_), channel_id=1, source_target_pairs={{0,16},{8,24},{16,0},{24,8},{1,17},{9,25},{17,1},{25,9},{2,18},{10... | collective-permute-start | bytes 442376 | tf_op jit(solution)/shard_map/ppermute | solution.py:67
  52.7 7.3 %collective-permute-start.5 = (bf16[576,128]{1,0:T(8,128)(2,1)S(1)}, bf16[576,128]{1,0:T(8,128)(2,1)}, u32[]{:S(2)}, u32[]{:S(2)}) collective-permute-start(bf16[576,128]{1,0:T(8,128)(2,1)S(1)} %collective-permute-done.4.refs_5_), channel_id=1, source_target_pairs={{0,8},{8,0},{16,24},{24,16},{1,9},{9,1},{17,25},{25,17},{2,10},{10... | collective-permute-start | bytes 442376 | tf_op jit(solution)/shard_map/ppermute | solution.py:67
  55.6 19.2 %collective-permute-start.12 = (bf16[4,576,128]{2,1,0:T(8,128)(2,1)S(1)}, bf16[4,576,128]{2,1,0:T(8,128)(2,1)S(1)}, u32[]{:S(2)}, u32[]{:S(2)}) collective-permute-start(bf16[4,576,128]{2,1,0:T(8,128)(2,1)S(1)} %get-tuple-element.29.refs_0_), channel_id=1, source_target_pairs={{0,1},{1,0},{2,3},{3,2},{4,5},{5,4},{6,7},{7,6},{8,9},{9,8},{10,11... | collective-permute-start | bytes 1769480 | tf_op jit(solution)/shard_map/ppermute | solution.py:76
  59.3 7.2 %collective-permute-start.2 = (bf16[576,128]{1,0:T(8,128)(2,1)S(1)}, bf16[576,128]{1,0:T(8,128)(2,1)}, u32[]{:S(2)}, u32[]{:S(2)}) collective-permute-start(bf16[576,128]{1,0:T(8,128)(2,1)S(1)} %collective-permute-done.refs_1_), channel_id=1, source_target_pairs={{0,16},{8,24},{16,0},{24,8},{1,17},{9,25},{17,1},{25,9},{2,18},{10... | collective-permute-start | bytes 442376 | tf_op jit(solution)/shard_map/ppermute | solution.py:67
  60.0 7.3 %collective-permute-start.1 = (bf16[576,128]{1,0:T(8,128)(2,1)S(1)}, bf16[576,128]{1,0:T(8,128)(2,1)}, u32[]{:S(2)}, u32[]{:S(2)}) collective-permute-start(bf16[576,128]{1,0:T(8,128)(2,1)S(1)} %collective-permute-done.refs_1_), channel_id=1, source_target_pairs={{0,8},{8,0},{16,24},{24,16},{1,9},{9,1},{17,25},{25,17},{2,10},{10... | collective-permute-start | bytes 442376 | tf_op jit(solution)/shard_map/ppermute | solution.py:67
  62.7 7.0 %collective-permute-start.23 = (bf16[576,128]{1,0:T(8,128)(2,1)S(1)}, bf16[576,128]{1,0:T(8,128)(2,1)S(1)}, u32[]{:S(2)}, u32[]{:S(2)}) collective-permute-start(bf16[576,128]{1,0:T(8,128)(2,1)S(1)} %collective-permute-done.10.refs_11_), channel_id=1, source_target_pairs={{0,1},{1,0},{2,3},{3,2},{4,5},{5,4},{6,7},{7,6},{8,9},{9,8},{10,11... | collective-permute-start | bytes 442376 | tf_op jit(solution)/shard_map/ppermute | solution.py:76
  110.3 9.3 %collective-permute-start.32 = (bf16[128,512]{1,0:T(8,128)(2,1)}, bf16[128,512]{1,0:T(8,128)(2,1)S(1)}, u32[]{:S(2)}, u32[]{:S(2)}) collective-permute-start(bf16[128,512]{1,0:T(8,128)(2,1)} %get-tuple-element.40), channel_id=1, source_target_pairs={{0,2},{1,3},{2,0},{3,1},{4,6},{5,7},{6,4},{7,5},{8,10},{9,11},{10,... | collective-permute-start | bytes 393224 | tf_op jit(solution)/shard_map/ppermute | solution.py:76
  112.0 7.5 %collective-permute-start.30 = (bf16[288,128]{1,0:T(8,128)(2,1)S(1)}, bf16[288,128]{1,0:T(8,128)(2,1)S(1)}, u32[]{:S(2)}, u32[]{:S(2)}) collective-permute-start(bf16[288,128]{1,0:T(8,128)(2,1)S(1)} %get-tuple-element.47.refs_0_), channel_id=1, source_target_pairs={{0,24},{8,16},{16,8},{24,0},{1,25},{9,17},{17,9},{25,1},{2,26},{10... | collective-permute-start | bytes 221192 | tf_op jit(solution)/shard_map/ppermute | solution.py:67
  113.6 7.6 %collective-permute-start.29 = (bf16[288,128]{1,0:T(8,128)(2,1)S(1)}, bf16[288,128]{1,0:T(8,128)(2,1)S(1)}, u32[]{:S(2)}, u32[]{:S(2)}) collective-permute-start(bf16[288,128]{1,0:T(8,128)(2,1)S(1)} %get-tuple-element.47.refs_0_), channel_id=1, source_target_pairs={{0,16},{8,24},{16,0},{24,8},{1,17},{9,25},{17,1},{25,9},{2,18},{10... | collective-permute-start | bytes 221192 | tf_op jit(solution)/shard_map/ppermute | solution.py:67
  114.0 8.6 %collective-permute-start.28 = (bf16[288,128]{1,0:T(8,128)(2,1)S(1)}, bf16[288,128]{1,0:T(8,128)(2,1)S(1)}, u32[]{:S(2)}, u32[]{:S(2)}) collective-permute-start(bf16[288,128]{1,0:T(8,128)(2,1)S(1)} %get-tuple-element.47.refs_0_), channel_id=1, source_target_pairs={{0,8},{8,0},{16,24},{24,16},{1,9},{9,1},{17,25},{25,17},{2,10},{10... | collective-permute-start | bytes 221192 | tf_op jit(solution)/shard_map/ppermute | solution.py:67
  114.8 13.2 %collective-permute-start.33 = (bf16[128,512]{1,0:T(8,128)(2,1)S(1)}, bf16[128,512]{1,0:T(8,128)(2,1)S(1)}, u32[]{:S(2)}, u32[]{:S(2)}) collective-permute-start(bf16[128,512]{1,0:T(8,128)(2,1)S(1)} %copy-done.26), channel_id=1, source_target_pairs={{0,3},{1,2},{2,1},{3,0},{4,7},{5,6},{6,5},{7,4},{8,11},{9,10},{10,... | collective-permute-start | bytes 393224 | tf_op jit(solution)/shard_map/ppermute | solution.py:76
  119.6 8.4 %collective-permute-start.34 = (bf16[128,512]{1,0:T(8,128)(2,1)S(1)}, bf16[128,512]{1,0:T(8,128)(2,1)S(1)}, u32[]{:S(2)}, u32[]{:S(2)}) collective-permute-start(bf16[128,512]{1,0:T(8,128)(2,1)S(1)} %copy-done.25), channel_id=1, source_target_pairs={{0,4},{1,5},{2,6},{3,7},{4,0},{5,1},{6,2},{7,3},{8,12},{9,13},{10,... | collective-permute-start | bytes 393224 | tf_op jit(solution)/shard_map/ppermute | solution.py:76
  119.6 16.9 %collective-permute-start.35 = (bf16[128,512]{1,0:T(8,128)(2,1)S(1)}, bf16[128,512]{1,0:T(8,128)(2,1)S(1)}, u32[]{:S(2)}, u32[]{:S(2)}) collective-permute-start(bf16[128,512]{1,0:T(8,128)(2,1)S(1)} %copy-done.24), channel_id=1, source_target_pairs={{0,5},{1,4},{2,7},{3,6},{4,1},{5,0},{6,3},{7,2},{8,13},{9,12},{10,... | collective-permute-start | bytes 393224 | tf_op jit(solution)/shard_map/ppermute | solution.py:76
  121.2 19.4 %collective-permute-start.36 = (bf16[128,512]{1,0:T(8,128)(2,1)S(1)}, bf16[128,512]{1,0:T(8,128)(2,1)S(1)}, u32[]{:S(2)}, u32[]{:S(2)}) collective-permute-start(bf16[128,512]{1,0:T(8,128)(2,1)S(1)} %copy-done.23), channel_id=1, source_target_pairs={{0,6},{1,7},{2,4},{3,5},{4,2},{5,3},{6,0},{7,1},{8,14},{9,15},{10,... | collective-permute-start | bytes 393224 | tf_op jit(solution)/shard_map/ppermute | solution.py:76
  122.6 21.4 %collective-permute-start.37 = (bf16[128,512]{1,0:T(8,128)(2,1)S(1)}, bf16[128,512]{1,0:T(8,128)(2,1)S(1)}, u32[]{:S(2)}, u32[]{:S(2)}) collective-permute-start(bf16[128,512]{1,0:T(8,128)(2,1)S(1)} %copy-done.22), channel_id=1, source_target_pairs={{0,7},{1,6},{2,5},{3,4},{4,3},{5,2},{6,1},{7,0},{8,15},{9,14},{10,... | collective-permute-start | bytes 393224 | tf_op jit(solution)/shard_map/ppermute | solution.py:76
  (42 other events, 502.4 us)

commit v3 on v2

--- a/solution.py
+++ b/solution.py
@@ -67,8 +67,9 @@
     return lax.ppermute(array, "dom", [(i, i ^ mask) for i in range(count)])
 
 
-def hop_order(chips):
-    return sorted(range(1, chips), key=lambda k: (k.bit_length(), -k))
+def send_chips(array, moves):
+    pairs = [(a * cores + c, b * cores + c) for a, b in moves for c in range(cores)]
+    return lax.ppermute(array, "tp", pairs)
 
 
 def flip_tp(array, mask):
@@ -114,8 +115,8 @@
     own_ref[...] = full_ref[lax.axis_index("dom")]
 
 
-def mlp_kernel(x_ref, *refs, quarters, chips, chan, order):
-    per_group = 1 + len(order) * quarters
+def mlp_kernel(x_ref, *refs, quarters, chips, chan):
+    per_group = 1 + (chips - 1) * quarters
     sources = [refs[g * per_group : (g + 1) * per_group] for g in range(cores)]
     shards, depth, _ = x_ref.shape
     outs = refs[cores * per_group :]
@@ -137,7 +138,7 @@
                 if k == 0:
                     block = sources[g][0].at[dom ^ j]
                 else:
-                    block = sources[g][1 + order.index(k) * quarters + j]
+                    block = sources[g][1 + (k - 1) * quarters + j]
                 for i in range(width // lanes):
                     column = j * width + i * lanes
                     first[at : at + depth, column : column + lanes] = block[
@@ -161,10 +162,12 @@
     ]
     for copy in copies:
         copy.start()
+    left = chip < 2
+    origins = (chip, chip ^ 1, jnp.where(left, 2, 1), jnp.where(left, 3, 0))
     for k in range(chips):
         for g in range(cores):
             at = (k * cores + g) * depth
-            source = (chip ^ k) * cores + (core if g == 0 else 1 - core)
+            source = origins[k] * cores + (core if g == 0 else 1 - core)
             moved[at : at + depth, :] = fresh[source]
     rows = jnp.dot(env[...], moved[...], preferred_element_type=f32).astype(bf16)
     per = rows.shape[0] // shards
@@ -248,18 +251,21 @@
         compiler_params=grant(8),
         name="split",
     )(stay(latent), own)
-    order = hop_order(chips)
-    shifted = {}
-    for k in order:
-        shifted[k] = flip_tp(own, k * cores)
+    last = chips - 1
+    across, outward = [(1, 2), (2, 1)], [(1, 0), (2, last)]
+    beside = flip_tp(own, cores)
+    near = send_chips(own, across)
+    far = send_chips(own, [(0, last), (last, 0)])
+    far = far + send_chips(own, [(0, 2), (last, 1)])
+    near = near + send_chips(near, outward)
     edge_rows = swap_blocks(pieces, "tp")
     edge_rows, *ties = lax.optimization_barrier((edge_rows, *ties))
     mine = [full]
-    for k in order:
-        mine += [shifted[k]] + [flip_dom(shifted[k], j) for j in range(1, domains)]
+    for piece in (beside, near, far):
+        mine += [piece] + [flip_dom(piece, j) for j in range(1, domains)]
     others = [other_core(array) for array in mine]
     *new_rows, weight_rows = pl.pallas_call(
-        functools.partial(mlp_kernel, quarters=domains, chips=chips, chan=chan, order=order),
+        functools.partial(mlp_kernel, quarters=domains, chips=chips, chan=chan),
         out_shape=[pltpu.HBM((depth, edges), bf16)] * shards
         + [pltpu.HBM((shards, channels // shards, edges), bf16)],
         in_specs=[in_vmem] * (1 + 2 * len(mine)),
@@ -411,7 +417,7 @@
         and w_first.shape[0] % (domains * lanes) == 0
         and w_env.shape[1] % (domains * 16) == 0
         and shards % cores == 0
-        and shards & (shards - 1) == 0
+        and shards == 4 * cores
         and domains & (domains - 1) == 0
     )
     harmonic, gain_sel = pl.pallas_call(

time: 146 us -> 140 us (0.959)
  waiting for transfers between devices: 52.9 us -> 43.9 us
  starting transfers between devices: 45.1 us -> 51.6 us
  blocking collectives: 14 us -> 10.3 us
    ppermute x23 -> x21, waiting for transfers between devices: 47.2 us -> 16.8 us  [flip_tp(): return lax.ppermute(array, 'tp', [(t, t ^ mask) for t in range(count)])]
    ppermute x0 -> x4, waiting for transfers between devices: none -> 21.8 us  [send_chips(): return lax.ppermute(array, 'tp', pairs)]
    ppermute x0 -> x4, starting transfers between devices: none -> 6.33 us  [send_chips(): return lax.ppermute(array, 'tp', pairs)]
    all_to_all x1, blocking collectives: 14 us -> 10.3 us  [swap_blocks(): return lax.all_to_all(array, axis, split_axis=0, concat_axis=0, tiled=True)]
    ppermute x23 -> x21, starting transfers between devices: 24.7 us -> 25.2 us  [flip_tp(): return lax.ppermute(array, 'tp', [(t, t ^ mask) for t in range(count)])]
  transfers between devices with their start and end apart: 39 -> 41, of which waited for: 10 -> 9; matrix products, arithmetic and copies ran while one was open for 1% -> 1% of each run, Pallas kernels for 3% -> 3%
where the time goes in v3:
time: 140 us; the launch traced here: 139 us
  starting transfers between devices  51.6 us (37%)
  waiting for transfers between devices  43.9 us (31%)
  Pallas kernels  17.3 us (12%)
  local copies, waits for them, and re-layouts  14.2 us (10%)
  blocking collectives  10.3 us (7%)
    ppermute x21, starting transfers between devices, flip_tp(): return lax.ppermute(array, 'tp', [(t, t ^ mask) for t in range(count)])  25.2 us
    ppermute x4, waiting for transfers between devices, send_chips(): return lax.ppermute(array, 'tp', pairs)  21.8 us
    ppermute x21, waiting for transfers between devices, flip_tp(): return lax.ppermute(array, 'tp', [(t, t ^ mask) for t in range(count)])  16.8 us
    ppermute x15, starting transfers between devices, flip_dom(): return lax.ppermute(array, 'dom', [(i, i ^ mask) for i in range(count)])  14.3 us
    unnamed x54, local copies, waits for them, and re-layouts  14.2 us
    all_to_all x1, blocking collectives, swap_blocks(): return lax.all_to_all(array, axis, split_axis=0, concat_axis=0, tiled=True)  10.3 us
    ppermute x4, starting transfers between devices, send_chips(): return lax.ppermute(array, 'tp', pairs)  6.33 us
    pallas_call x1, Pallas kernels, spread_mlp(): pl.pallas_call(functools.partial(mlp_kernel, quarters=domains, chips=chip...  5.82 us
  transfers between devices with their start and end apart: 41, of which 9 were waited for; matrix products, arithmetic and copies ran while one was open for 1% of the time, Pallas kernels for 3%

profile of v3, /device:TPU:9, one launch (start us, length us, event | category | flops | bytes accessed | tf_op | source)
XLA Modules:
  0.0 139.0 jit_solution(5102926910221482610)
XLA Ops:
  2.0 2.1 %split.1 = bf16[8,128,512]{2,1,0:T(8,128)(2,1)} custom-call(bf16[128,4096]{1,0:T(8,128)(2,1)} %x_ref.1, bf16[576,128]{1,0:T(8,128)(2,1)S(1)} %get-tuple-element.25.tie_ref), custom_call_target="tpu_custom_call" | custom-call | tf_op jit(solution)/shard_map/split/pallas_call | solution.py:244
  4.2 5.7 %all-to-all-start = ((bf16[8,128,512]{2,1,0:T(8,128)(2,1)}), bf16[8,128,512]{2,1,0:T(8,128)(2,1)S(1)}, u32[]{:S(2)}, u32[]{:S(2)}) async-start(bf16[8,128,512]{2,1,0:T(8,128)(2,1)} %split.1), calls=%async_computation | async-start | bytes 2097152 | tf_op jit(solution)/shard_map/all_to_all | solution.py:62
  11.9 3.1 %collective-permute-start.4 = (bf16[576,128]{1,0:T(8,128)(2,1)S(1)}, bf16[576,128]{1,0:T(8,128)(2,1)S(1)}, u32[]{:S(2)}, u32[]{:S(2)}) collective-permute-start(bf16[576,128]{1,0:T(8,128)(2,1)S(1)} %get-tuple-element.25.tie_ref), channel_id=1, source_target_pairs={{2,4},{3,5},{4,2},{5,3},{10,12},{11,13},{12,10},{13,11},{18,20},{1... | collective-permute-start | bytes 442376 | tf_op jit(solution)/shard_map/ppermute | solution.py:72
  15.0 3.0 %collective-permute-start = (bf16[576,128]{1,0:T(8,128)(2,1)S(1)}, bf16[576,128]{1,0:T(8,128)(2,1)S(1)}, u32[]{:S(2)}, u32[]{:S(2)}) collective-permute-start(bf16[576,128]{1,0:T(8,128)(2,1)S(1)} %get-tuple-element.25.tie_ref), channel_id=1, source_target_pairs={{0,2},{1,3},{2,0},{3,1},{4,6},{5,7},{6,4},{7,5},{8,10},{9,11},{10,... | collective-permute-start | bytes 442376 | tf_op jit(solution)/shard_map/ppermute | solution.py:77
  18.0 14.9 %collective-permute-done.10 = bf16[576,128]{1,0:T(8,128)(2,1)S(1)} collective-permute-done((bf16[576,128]{1,0:T(8,128)(2,1)S(1)}, bf16[576,128]{1,0:T(8,128)(2,1)S(1)}, u32[]{:S(2)}, u32[]{:S(2)}) %collective-permute-start.10) | collective-permute-done | bytes 147488 | tf_op jit(solution)/shard_map/ppermute | solution.py:72
  33.0 1.7 %collective-permute-start.23 = (bf16[576,128]{1,0:T(8,128)(2,1)S(1)}, bf16[576,128]{1,0:T(8,128)(2,1)S(1)}, u32[]{:S(2)}, u32[]{:S(2)}) collective-permute-start(bf16[576,128]{1,0:T(8,128)(2,1)S(1)} %add.16.refs_9_), channel_id=1, source_target_pairs={{0,1},{1,0},{2,3},{3,2},{4,5},{5,4},{6,7},{7,6},{8,9},{9,8},{10,11... | collective-permute-start | bytes 442376 | tf_op jit(solution)/shard_map/ppermute | solution.py:77
  34.7 2.2 %collective-permute-start.13 = (bf16[576,128]{1,0:T(8,128)(2,1)S(1)}, bf16[576,128]{1,0:T(8,128)(2,1)S(1)}, u32[]{:S(2)}, u32[]{:S(2)}) collective-permute-start(bf16[576,128]{1,0:T(8,128)(2,1)S(1)} %add.16.refs_9_), channel_id=1, source_target_pairs={{0,24},{8,16},{16,8},{24,0},{1,25},{9,17},{17,9},{25,1},{2,26},{10... | collective-permute-start | bytes 442376 | tf_op jit(solution)/shard_map/ppermute | solution.py:67
  37.1 6.8 %collective-permute-done.4 = bf16[576,128]{1,0:T(8,128)(2,1)S(1)} collective-permute-done((bf16[576,128]{1,0:T(8,128)(2,1)S(1)}, bf16[576,128]{1,0:T(8,128)(2,1)S(1)}, u32[]{:S(2)}, u32[]{:S(2)}) %collective-permute-start.4) | collective-permute-done | bytes 147488 | tf_op jit(solution)/shard_map/ppermute | solution.py:72
  52.4 1.6 %collective-permute-done.3.refs_4_ = bf16[576,128]{1,0:T(8,128)(2,1)S(1)} collective-permute-done((bf16[576,128]{1,0:T(8,128)(2,1)S(1)}, bf16[576,128]{1,0:T(8,128)(2,1)S(1)}, u32[]{:S(2)}, u32[]{:S(2)}) %collective-permute-start.3) | collective-permute-done | bytes 147488 | tf_op jit(solution)/shard_map/ppermute | solution.py:67
  54.0 1.5 %collective-permute-start.25 = (bf16[576,128]{1,0:T(8,128)(2,1)S(1)}, bf16[576,128]{1,0:T(8,128)(2,1)S(1)}, u32[]{:S(2)}, u32[]{:S(2)}) collective-permute-start(bf16[576,128]{1,0:T(8,128)(2,1)S(1)} %collective-permute-done.12.refs_11_), channel_id=1, source_target_pairs={{0,1},{1,0},{2,3},{3,2},{4,5},{5,4},{6,7},{7,6},{8,9},{9,8},{10,11... | collective-permute-start | bytes 442376 | tf_op jit(solution)/shard_map/ppermute | solution.py:77
  55.5 2.2 %collective-permute-done.2.refs_3_ = bf16[576,128]{1,0:T(8,128)(2,1)S(1)} collective-permute-done((bf16[576,128]{1,0:T(8,128)(2,1)S(1)}, bf16[576,128]{1,0:T(8,128)(2,1)S(1)}, u32[]{:S(2)}, u32[]{:S(2)}) %collective-permute-start.2) | collective-permute-done | bytes 147488 | tf_op jit(solution)/shard_map/ppermute | solution.py:67
  67.4 1.4 %collective-permute-done.7.refs_7_ = bf16[576,128]{1,0:T(8,128)(2,1)} collective-permute-done((bf16[576,128]{1,0:T(8,128)(2,1)S(1)}, bf16[576,128]{1,0:T(8,128)(2,1)}, u32[]{:S(2)}, u32[]{:S(2)}) %collective-permute-start.7) | collective-permute-done | bytes 147488 | tf_op jit(solution)/shard_map/ppermute | solution.py:67
  81.1 5.8 %mlp.1 = (bf16[128,512]{1,0:T(8,128)(2,1)}, bf16[128,512]{1,0:T(8,128)(2,1)}, bf16[128,512]{1,0:T(8,128)(2,1)}, bf16[128,512]{1,0:T(8,128)(2,1)}, bf16[128,512]{...) custom-call(bf16[8,128,512]{2,1,0:T(8,128)(2,1)S(1)} %all-to-all-don, ...), custom_call_target="tpu_custom_call" | custom-call | tf_op jit(solution)/shard_map/mlp/pallas_call | solution.py:267
  87.0 10.3 %all_to_all.10.w_ref = bf16[8,32,512]{2,1,0:T(8,128)(2,1)S(1)} all-to-all(bf16[8,32,512]{2,1,0:T(8,128)(2,1)} %get-tuple-element.30), channel_id=1, replica_groups=mesh['dom'=4,'tp'=8] {'tp'}, dimensions={0} | all-to-all | bytes 524288 | tf_op jit(solution)/shard_map/all_to_all | solution.py:62
  97.3 2.8 %sums.1 = (f32[288,128]{1,0:T(8,128)S(1)}, bf16[288,128]{1,0:T(8,128)(2,1)S(1)}, bf16[288,128]{1,0:T(8,128)(2,1)S(1)}, bf16[288,128]{1,0:T(8,128)(2,1)S(1)}) custom-call(s32[32]{0:T(128)} %bitcast.13, bf16[8,32,512]{2,1,0:T(8,128)(2,1)S(1)} %all_to_all.10.w_ref, f32[10,32,128]{2,1,0:T(8,128)S(1)} %get-tuple-element.31.h_ref), custom_call_target="tpu_custom_call" | custom-call | tf_op jit(solution)/shard_map/sums/pallas_call | solution.py:448
  102.8 1.9 %collective-permute-start.33 = (bf16[128,512]{1,0:T(8,128)(2,1)}, bf16[128,512]{1,0:T(8,128)(2,1)S(1)}, u32[]{:S(2)}, u32[]{:S(2)}) collective-permute-start(bf16[128,512]{1,0:T(8,128)(2,1)} %get-tuple-element.39), channel_id=1, source_target_pairs={{0,1},{1,0},{2,3},{3,2},{4,5},{5,4},{6,7},{7,6},{8,9},{9,8},{10,11... | collective-permute-start | bytes 393224 | tf_op jit(solution)/shard_map/ppermute | solution.py:77
  104.7 1.7 %collective-permute-start.34 = (bf16[128,512]{1,0:T(8,128)(2,1)}, bf16[128,512]{1,0:T(8,128)(2,1)S(1)}, u32[]{:S(2)}, u32[]{:S(2)}) collective-permute-start(bf16[128,512]{1,0:T(8,128)(2,1)} %get-tuple-element.40), channel_id=1, source_target_pairs={{0,2},{1,3},{2,0},{3,1},{4,6},{5,7},{6,4},{7,5},{8,10},{9,11},{10,... | collective-permute-start | bytes 393224 | tf_op jit(solution)/shard_map/ppermute | solution.py:77
  109.2 4.4 %collective-permute-start.35 = (bf16[128,512]{1,0:T(8,128)(2,1)S(1)}, bf16[128,512]{1,0:T(8,128)(2,1)S(1)}, u32[]{:S(2)}, u32[]{:S(2)}) collective-permute-start(bf16[128,512]{1,0:T(8,128)(2,1)S(1)} %copy-done.26), channel_id=1, source_target_pairs={{0,3},{1,2},{2,1},{3,0},{4,7},{5,6},{6,5},{7,4},{8,11},{9,10},{10,... | collective-permute-start | bytes 393224 | tf_op jit(solution)/shard_map/ppermute | solution.py:77
  113.6 1.6 %collective-permute-start.37 = (bf16[128,512]{1,0:T(8,128)(2,1)S(1)}, bf16[128,512]{1,0:T(8,128)(2,1)S(1)}, u32[]{:S(2)}, u32[]{:S(2)}) collective-permute-start(bf16[128,512]{1,0:T(8,128)(2,1)S(1)} %copy-done.24), channel_id=1, source_target_pairs={{0,5},{1,4},{2,7},{3,6},{4,1},{5,0},{6,3},{7,2},{8,13},{9,12},{10,... | collective-permute-start | bytes 393224 | tf_op jit(solution)/shard_map/ppermute | solution.py:77
  116.5 1.5 %collective-permute-start.39 = (bf16[128,512]{1,0:T(8,128)(2,1)S(1)}, bf16[128,512]{1,0:T(8,128)(2,1)S(1)}, u32[]{:S(2)}, u32[]{:S(2)}) collective-permute-start(bf16[128,512]{1,0:T(8,128)(2,1)S(1)} %copy-done.22), channel_id=1, source_target_pairs={{0,7},{1,6},{2,5},{3,4},{4,3},{5,2},{6,1},{7,0},{8,15},{9,14},{10,... | collective-permute-start | bytes 393224 | tf_op jit(solution)/shard_map/ppermute | solution.py:77
  118.6 3.3 %invariants.1 = (f32[3,32,4096]{2,1,0:T(8,128)}, f32[8,128]{1,0:T(8,128)S(1)}) custom-call(s32[32]{0:T(128)} %bitcast.14, bf16[8,32,512]{2,1,0:T(8,128)(2,1)S(1)} %all_to_all.10.w_ref, f32[10,32,128]{2,1,0:T(8,128)S(1)} %get-tuple-element.31.h_ref, bf16[288,128]{1,0:T(8,128)(2,1)S(1)} %get-tuple-element.47.refs_0_, ...), custom_call_target="tpu_custom_call" | custom-call | tf_op jit(solution)/shard_map/invariants/pallas_call | solution.py:464
  122.0 8.5 %collective-permute-done.37.refs_5_ = bf16[128,512]{1,0:T(8,128)(2,1)S(1)} collective-permute-done((bf16[128,512]{1,0:T(8,128)(2,1)S(1)}, bf16[128,512]{1,0:T(8,128)(2,1)S(1)}, u32[]{:S(2)}, u32[]{:S(2)}) %collective-permute-start.37) | collective-permute-done | bytes 131104 | tf_op jit(solution)/shard_map/ppermute | solution.py:77
  130.5 4.1 %collective-permute-done.38.refs_6_ = bf16[128,512]{1,0:T(8,128)(2,1)S(1)} collective-permute-done((bf16[128,512]{1,0:T(8,128)(2,1)S(1)}, bf16[128,512]{1,0:T(8,128)(2,1)S(1)}, u32[]{:S(2)}, u32[]{:S(2)}) %collective-permute-start.38) | collective-permute-done | bytes 131104 | tf_op jit(solution)/shard_map/ppermute | solution.py:77
  134.6 3.4 %collective-permute-done.39.refs_7_ = bf16[128,512]{1,0:T(8,128)(2,1)S(1)} collective-permute-done((bf16[128,512]{1,0:T(8,128)(2,1)S(1)}, bf16[128,512]{1,0:T(8,128)(2,1)S(1)}, u32[]{:S(2)}, u32[]{:S(2)}) %collective-permute-start.39) | collective-permute-done | bytes 131104 | tf_op jit(solution)/shard_map/ppermute | solution.py:77
  (124 shorter events, 42.6 us)
Async XLA Ops:
  4.2 67.9 %all-to-all-start = ((bf16[8,128,512]{2,1,0:T(8,128)(2,1)}), bf16[8,128,512]{2,1,0:T(8,128)(2,1)S(1)}, u32[]{:S(2)}, u32[]{:S(2)}) async-start(bf16[8,128,512]{2,1,0:T(8,128)(2,1)} %split.1), calls=%async_computation | async-start | bytes 2097152 | tf_op jit(solution)/shard_map/all_to_all | solution.py:62
  9.9 23.1 %collective-permute-start.10 = (bf16[576,128]{1,0:T(8,128)(2,1)S(1)}, bf16[576,128]{1,0:T(8,128)(2,1)S(1)}, u32[]{:S(2)}, u32[]{:S(2)}) collective-permute-start(bf16[576,128]{1,0:T(8,128)(2,1)S(1)} %get-tuple-element.25.tie_ref), channel_id=1, source_target_pairs={{0,4},{1,5},{6,2},{7,3},{8,12},{9,13},{14,10},{15,11},{16,20},{17,... | collective-permute-start | bytes 442376 | tf_op jit(solution)/shard_map/ppermute | solution.py:72
  11.2 21.8 %collective-permute-start.9 = (bf16[576,128]{1,0:T(8,128)(2,1)S(1)}, bf16[576,128]{1,0:T(8,128)(2,1)S(1)}, u32[]{:S(2)}, u32[]{:S(2)}) collective-permute-start(bf16[576,128]{1,0:T(8,128)(2,1)S(1)} %get-tuple-element.25.tie_ref), channel_id=1, source_target_pairs={{0,6},{1,7},{6,0},{7,1},{8,14},{9,15},{14,8},{15,9},{16,22},{17,23... | collective-permute-start | bytes 442376 | tf_op jit(solution)/shard_map/ppermute | solution.py:72
  11.9 32.0 %collective-permute-start.4 = (bf16[576,128]{1,0:T(8,128)(2,1)S(1)}, bf16[576,128]{1,0:T(8,128)(2,1)S(1)}, u32[]{:S(2)}, u32[]{:S(2)}) collective-permute-start(bf16[576,128]{1,0:T(8,128)(2,1)S(1)} %get-tuple-element.25.tie_ref), channel_id=1, source_target_pairs={{2,4},{3,5},{4,2},{5,3},{10,12},{11,13},{12,10},{13,11},{18,20},{1... | collective-permute-start | bytes 442376 | tf_op jit(solution)/shard_map/ppermute | solution.py:72
  15.0 30.2 %collective-permute-start = (bf16[576,128]{1,0:T(8,128)(2,1)S(1)}, bf16[576,128]{1,0:T(8,128)(2,1)S(1)}, u32[]{:S(2)}, u32[]{:S(2)}) collective-permute-start(bf16[576,128]{1,0:T(8,128)(2,1)S(1)} %get-tuple-element.25.tie_ref), channel_id=1, source_target_pairs={{0,2},{1,3},{2,0},{3,1},{4,6},{5,7},{6,4},{7,5},{8,10},{9,11},{10,... | collective-permute-start | bytes 442376 | tf_op jit(solution)/shard_map/ppermute | solution.py:77
  33.0 13.4 %collective-permute-start.23 = (bf16[576,128]{1,0:T(8,128)(2,1)S(1)}, bf16[576,128]{1,0:T(8,128)(2,1)S(1)}, u32[]{:S(2)}, u32[]{:S(2)}) collective-permute-start(bf16[576,128]{1,0:T(8,128)(2,1)S(1)} %add.16.refs_9_), channel_id=1, source_target_pairs={{0,1},{1,0},{2,3},{3,2},{4,5},{5,4},{6,7},{7,6},{8,9},{9,8},{10,11... | collective-permute-start | bytes 442376 | tf_op jit(solution)/shard_map/ppermute | solution.py:77
  34.7 13.1 %collective-permute-start.13 = (bf16[576,128]{1,0:T(8,128)(2,1)S(1)}, bf16[576,128]{1,0:T(8,128)(2,1)S(1)}, u32[]{:S(2)}, u32[]{:S(2)}) collective-permute-start(bf16[576,128]{1,0:T(8,128)(2,1)S(1)} %add.16.refs_9_), channel_id=1, source_target_pairs={{0,24},{8,16},{16,8},{24,0},{1,25},{9,17},{17,9},{25,1},{2,26},{10... | collective-permute-start | bytes 442376 | tf_op jit(solution)/shard_map/ppermute | solution.py:67
  36.8 12.1 %collective-permute-start.12 = (bf16[576,128]{1,0:T(8,128)(2,1)S(1)}, bf16[576,128]{1,0:T(8,128)(2,1)S(1)}, u32[]{:S(2)}, u32[]{:S(2)}) collective-permute-start(bf16[576,128]{1,0:T(8,128)(2,1)S(1)} %add.16.refs_9_), channel_id=1, source_target_pairs={{0,16},{8,24},{16,0},{24,8},{1,17},{9,25},{17,1},{25,9},{2,18},{10... | collective-permute-start | bytes 442376 | tf_op jit(solution)/shard_map/ppermute | solution.py:67
  49.0 8.7 %collective-permute-start.2 = (bf16[576,128]{1,0:T(8,128)(2,1)S(1)}, bf16[576,128]{1,0:T(8,128)(2,1)S(1)}, u32[]{:S(2)}, u32[]{:S(2)}) collective-permute-start(bf16[576,128]{1,0:T(8,128)(2,1)S(1)} %collective-permute-done.refs_1_), channel_id=1, source_target_pairs={{0,16},{8,24},{16,0},{24,8},{1,17},{9,25},{17,1},{25,9},{2,18},{10... | collective-permute-start | bytes 442376 | tf_op jit(solution)/shard_map/ppermute | solution.py:67
  49.2 8.9 %collective-permute-start.1 = (bf16[576,128]{1,0:T(8,128)(2,1)S(1)}, bf16[576,128]{1,0:T(8,128)(2,1)}, u32[]{:S(2)}, u32[]{:S(2)}) collective-permute-start(bf16[576,128]{1,0:T(8,128)(2,1)S(1)} %collective-permute-done.refs_1_), channel_id=1, source_target_pairs={{0,8},{8,0},{16,24},{24,16},{1,9},{9,1},{17,25},{25,17},{2,10},{10... | collective-permute-start | bytes 442376 | tf_op jit(solution)/shard_map/ppermute | solution.py:67
  50.4 7.9 %collective-permute-start.26 = (bf16[576,128]{1,0:T(8,128)(2,1)S(1)}, bf16[576,128]{1,0:T(8,128)(2,1)S(1)}, u32[]{:S(2)}, u32[]{:S(2)}) collective-permute-start(bf16[576,128]{1,0:T(8,128)(2,1)S(1)} %collective-permute-done.13.refs_12_), channel_id=1, source_target_pairs={{0,1},{1,0},{2,3},{3,2},{4,5},{5,4},{6,7},{7,6},{8,9},{9,8},{10,11... | collective-permute-start | bytes 442376 | tf_op jit(solution)/shard_map/ppermute | solution.py:77
  52.3 20.6 %collective-permute-start.14 = (bf16[4,576,128]{2,1,0:T(8,128)(2,1)S(1)}, bf16[4,576,128]{2,1,0:T(8,128)(2,1)S(1)}, u32[]{:S(2)}, u32[]{:S(2)}) collective-permute-start(bf16[4,576,128]{2,1,0:T(8,128)(2,1)S(1)} %get-tuple-element.29.refs_0_), channel_id=1, source_target_pairs={{0,1},{1,0},{2,3},{3,2},{4,5},{5,4},{6,7},{7,6},{8,9},{9,8},{10,11... | collective-permute-start | bytes 1769480 | tf_op jit(solution)/shard_map/ppermute | solution.py:77
  58.9 6.5 %collective-permute-start.8 = (bf16[576,128]{1,0:T(8,128)(2,1)S(1)}, bf16[576,128]{1,0:T(8,128)(2,1)}, u32[]{:S(2)}, u32[]{:S(2)}) collective-permute-start(bf16[576,128]{1,0:T(8,128)(2,1)S(1)} %add.15.refs_5_), channel_id=1, source_target_pairs={{0,24},{8,16},{16,8},{24,0},{1,25},{9,17},{17,9},{25,1},{2,26},{10... | collective-permute-start | bytes 442376 | tf_op jit(solution)/shard_map/ppermute | solution.py:67
  60.6 8.2 %collective-permute-start.7 = (bf16[576,128]{1,0:T(8,128)(2,1)S(1)}, bf16[576,128]{1,0:T(8,128)(2,1)}, u32[]{:S(2)}, u32[]{:S(2)}) collective-permute-start(bf16[576,128]{1,0:T(8,128)(2,1)S(1)} %add.15.refs_5_), channel_id=1, source_target_pairs={{0,16},{8,24},{16,0},{24,8},{1,17},{9,25},{17,1},{25,9},{2,18},{10... | collective-permute-start | bytes 442376 | tf_op jit(solution)/shard_map/ppermute | solution.py:67
  61.9 7.5 %collective-permute-start.6 = (bf16[576,128]{1,0:T(8,128)(2,1)S(1)}, bf16[576,128]{1,0:T(8,128)(2,1)}, u32[]{:S(2)}, u32[]{:S(2)}) collective-permute-start(bf16[576,128]{1,0:T(8,128)(2,1)S(1)} %add.15.refs_5_), channel_id=1, source_target_pairs={{0,8},{8,0},{16,24},{24,16},{1,9},{9,1},{17,25},{25,17},{2,10},{10... | collective-permute-start | bytes 442376 | tf_op jit(solution)/shard_map/ppermute | solution.py:67
  104.7 8.8 %collective-permute-start.34 = (bf16[128,512]{1,0:T(8,128)(2,1)}, bf16[128,512]{1,0:T(8,128)(2,1)S(1)}, u32[]{:S(2)}, u32[]{:S(2)}) collective-permute-start(bf16[128,512]{1,0:T(8,128)(2,1)} %get-tuple-element.40), channel_id=1, source_target_pairs={{0,2},{1,3},{2,0},{3,1},{4,6},{5,7},{6,4},{7,5},{8,10},{9,11},{10,... | collective-permute-start | bytes 393224 | tf_op jit(solution)/shard_map/ppermute | solution.py:77
  106.4 7.1 %collective-permute-start.32 = (bf16[288,128]{1,0:T(8,128)(2,1)S(1)}, bf16[288,128]{1,0:T(8,128)(2,1)S(1)}, u32[]{:S(2)}, u32[]{:S(2)}) collective-permute-start(bf16[288,128]{1,0:T(8,128)(2,1)S(1)} %get-tuple-element.47.refs_0_), channel_id=1, source_target_pairs={{0,24},{8,16},{16,8},{24,0},{1,25},{9,17},{17,9},{25,1},{2,26},{10... | collective-permute-start | bytes 221192 | tf_op jit(solution)/shard_map/ppermute | solution.py:67
  107.6 7.6 %collective-permute-start.31 = (bf16[288,128]{1,0:T(8,128)(2,1)S(1)}, bf16[288,128]{1,0:T(8,128)(2,1)S(1)}, u32[]{:S(2)}, u32[]{:S(2)}) collective-permute-start(bf16[288,128]{1,0:T(8,128)(2,1)S(1)} %get-tuple-element.47.refs_0_), channel_id=1, source_target_pairs={{0,16},{8,24},{16,0},{24,8},{1,17},{9,25},{17,1},{25,9},{2,18},{10... | collective-permute-start | bytes 221192 | tf_op jit(solution)/shard_map/ppermute | solution.py:67
  108.2 8.3 %collective-permute-start.30 = (bf16[288,128]{1,0:T(8,128)(2,1)S(1)}, bf16[288,128]{1,0:T(8,128)(2,1)S(1)}, u32[]{:S(2)}, u32[]{:S(2)}) collective-permute-start(bf16[288,128]{1,0:T(8,128)(2,1)S(1)} %get-tuple-element.47.refs_0_), channel_id=1, source_target_pairs={{0,8},{8,0},{16,24},{24,16},{1,9},{9,1},{17,25},{25,17},{2,10},{10... | collective-permute-start | bytes 221192 | tf_op jit(solution)/shard_map/ppermute | solution.py:67
  109.2 12.8 %collective-permute-start.35 = (bf16[128,512]{1,0:T(8,128)(2,1)S(1)}, bf16[128,512]{1,0:T(8,128)(2,1)S(1)}, u32[]{:S(2)}, u32[]{:S(2)}) collective-permute-start(bf16[128,512]{1,0:T(8,128)(2,1)S(1)} %copy-done.26), channel_id=1, source_target_pairs={{0,3},{1,2},{2,1},{3,0},{4,7},{5,6},{6,5},{7,4},{8,11},{9,10},{10,... | collective-permute-start | bytes 393224 | tf_op jit(solution)/shard_map/ppermute | solution.py:77
  113.5 8.4 %collective-permute-start.36 = (bf16[128,512]{1,0:T(8,128)(2,1)S(1)}, bf16[128,512]{1,0:T(8,128)(2,1)S(1)}, u32[]{:S(2)}, u32[]{:S(2)}) collective-permute-start(bf16[128,512]{1,0:T(8,128)(2,1)S(1)} %copy-done.25), channel_id=1, source_target_pairs={{0,4},{1,5},{2,6},{3,7},{4,0},{5,1},{6,2},{7,3},{8,12},{9,13},{10,... | collective-permute-start | bytes 393224 | tf_op jit(solution)/shard_map/ppermute | solution.py:77
  113.6 16.9 %collective-permute-start.37 = (bf16[128,512]{1,0:T(8,128)(2,1)S(1)}, bf16[128,512]{1,0:T(8,128)(2,1)S(1)}, u32[]{:S(2)}, u32[]{:S(2)}) collective-permute-start(bf16[128,512]{1,0:T(8,128)(2,1)S(1)} %copy-done.24), channel_id=1, source_target_pairs={{0,5},{1,4},{2,7},{3,6},{4,1},{5,0},{6,3},{7,2},{8,13},{9,12},{10,... | collective-permute-start | bytes 393224 | tf_op jit(solution)/shard_map/ppermute | solution.py:77
  115.1 19.4 %collective-permute-start.38 = (bf16[128,512]{1,0:T(8,128)(2,1)S(1)}, bf16[128,512]{1,0:T(8,128)(2,1)S(1)}, u32[]{:S(2)}, u32[]{:S(2)}) collective-permute-start(bf16[128,512]{1,0:T(8,128)(2,1)S(1)} %copy-done.23), channel_id=1, source_target_pairs={{0,6},{1,7},{2,4},{3,5},{4,2},{5,3},{6,0},{7,1},{8,14},{9,15},{10,... | collective-permute-start | bytes 393224 | tf_op jit(solution)/shard_map/ppermute | solution.py:77
  116.5 21.5 %collective-permute-start.39 = (bf16[128,512]{1,0:T(8,128)(2,1)S(1)}, bf16[128,512]{1,0:T(8,128)(2,1)S(1)}, u32[]{:S(2)}, u32[]{:S(2)}) collective-permute-start(bf16[128,512]{1,0:T(8,128)(2,1)S(1)} %copy-done.22), channel_id=1, source_target_pairs={{0,7},{1,6},{2,5},{3,4},{4,3},{5,2},{6,1},{7,0},{8,15},{9,14},{10,... | collective-permute-start | bytes 393224 | tf_op jit(solution)/shard_map/ppermute | solution.py:77
  (44 other events, 479.6 us)

commit v4 on v2

--- a/solution.py
+++ b/solution.py
@@ -195,20 +195,26 @@
 
 
 def join_kernel(tie_ref, *refs):
-    pieces, out_ref = refs[:-1], refs[-1]
+    pieces, (out_ref, sems) = refs[:-2], refs[-2:]
     edges = pieces[0].shape[1]
+    copies = []
     for s, piece in enumerate(pieces):
         at = pl.multiple_of((lax.axis_index("tp") ^ s) * edges, lanes)
-        out_ref[:, pl.ds(at, edges)] = piece[...]
+        copies.append(pltpu.make_async_copy(piece, out_ref.at[:, pl.ds(at, edges)], sems.at[s]))
+    for copy in copies:
+        copy.start()
+    for copy in copies:
+        copy.wait()
 
 
 def join_pieces(back, tie):
     depth, edges = back[0].shape
     return pl.pallas_call(
         join_kernel,
-        out_shape=jax.ShapeDtypeStruct((depth, edges * len(back)), bf16),
+        out_shape=pltpu.HBM((depth, edges * len(back)), bf16),
         in_specs=[anywhere] + [in_vmem] * len(back),
-        out_specs=in_vmem,
+        out_specs=in_hbm,
+        scratch_shapes=[pltpu.SemaphoreType.DMA((len(back),))],
         compiler_params=grant(8),
         name="join",
     )(tie, *back)
@@ -451,7 +457,8 @@
     )(target, weights, harmonic)
     env_raw = sums[0]
     for j in range(1, domains):
-        env_raw = env_raw + flip_dom(sums[j], j).astype(f32)
+        arrived = flip_dom(sums[j], j)
+        env_raw = env_raw + arrived.astype(f32)
     env_out = env_raw.reshape(parts, chan, atoms) * gain_sel[None, :, :] * env_factor
     env_half = env_out.astype(bf16).reshape(rows, atoms)
     looked = [env_half] + [flip_dom(env_half, j) for j in range(1, domains)]

time: 146 us -> 146 us (level)
  no operation moved by 1% of the time
where the time goes in v4:
time: 146 us; the launch traced here: 145 us
  waiting for transfers between devices  52.9 us (36%)
  starting transfers between devices  45.1 us (31%)
  Pallas kernels  17.2 us (12%)
  local copies, waits for them, and re-layouts  14.2 us (10%)
  blocking collectives  14 us (10%)
    ppermute x23, waiting for transfers between devices, flip_tp(): return lax.ppermute(array, 'tp', [(t, t ^ mask) for t in range(count)])  47.2 us
    ppermute x23, starting transfers between devices, flip_tp(): return lax.ppermute(array, 'tp', [(t, t ^ mask) for t in range(count)])  24.7 us
    ppermute x15, starting transfers between devices, flip_dom(): return lax.ppermute(array, 'dom', [(i, i ^ mask) for i in range(count)])  14.6 us
    unnamed x54, local copies, waits for them, and re-layouts  14.2 us
    all_to_all x1, blocking collectives, swap_blocks(): return lax.all_to_all(array, axis, split_axis=0, concat_axis=0, tiled=True)  14 us
    pallas_call x1, Pallas kernels, spread_mlp(): pl.pallas_call(functools.partial(mlp_kernel, quarters=domains, chips=chip...  5.82 us
    all_to_all x1, starting transfers between devices, swap_blocks(): return lax.all_to_all(array, axis, split_axis=0, concat_axis=0, tiled=True)  5.75 us
    ppermute x15, waiting for transfers between devices, flip_dom(): return lax.ppermute(array, 'dom', [(i, i ^ mask) for i in range(count)])  5.67 us
  transfers between devices with their start and end apart: 39, of which 10 were waited for; matrix products, arithmetic and copies ran while one was open for 1% of the time, Pallas kernels for 3%

profile of v4, /device:TPU:9, one launch (start us, length us, event | category | flops | bytes accessed | tf_op | source)
XLA Modules:
  0.0 145.0 jit_solution(11821768415535893948)
XLA Ops:
  2.0 2.1 %split.1 = bf16[8,128,512]{2,1,0:T(8,128)(2,1)} custom-call(bf16[128,4096]{1,0:T(8,128)(2,1)} %x_ref.1, bf16[576,128]{1,0:T(8,128)(2,1)S(1)} %get-tuple-element.25.tie_ref), custom_call_target="tpu_custom_call" | custom-call | tf_op jit(solution)/shard_map/split/pallas_call | solution.py:247
  4.2 5.7 %all-to-all-start = ((bf16[8,128,512]{2,1,0:T(8,128)(2,1)}), bf16[8,128,512]{2,1,0:T(8,128)(2,1)S(1)}, u32[]{:S(2)}, u32[]{:S(2)}) async-start(bf16[8,128,512]{2,1,0:T(8,128)(2,1)} %split.1), calls=%async_computation | async-start | bytes 2097152 | tf_op jit(solution)/shard_map/all_to_all | solution.py:62
  9.9 2.1 %collective-permute-start.8 = (bf16[576,128]{1,0:T(8,128)(2,1)S(1)}, bf16[576,128]{1,0:T(8,128)(2,1)S(1)}, u32[]{:S(2)}, u32[]{:S(2)}) collective-permute-start(bf16[576,128]{1,0:T(8,128)(2,1)S(1)} %get-tuple-element.25.tie_ref), channel_id=1, source_target_pairs={{0,4},{1,5},{2,6},{3,7},{4,0},{5,1},{6,2},{7,3},{8,12},{9,13},{10,... | collective-permute-start | bytes 442376 | tf_op jit(solution)/shard_map/ppermute | solution.py:76
  12.0 1.5 %collective-permute-start = (bf16[576,128]{1,0:T(8,128)(2,1)S(1)}, bf16[576,128]{1,0:T(8,128)(2,1)S(1)}, u32[]{:S(2)}, u32[]{:S(2)}) collective-permute-start(bf16[576,128]{1,0:T(8,128)(2,1)S(1)} %get-tuple-element.25.tie_ref), channel_id=1, source_target_pairs={{0,2},{1,3},{2,0},{3,1},{4,6},{5,7},{6,4},{7,5},{8,10},{9,11},{10,... | collective-permute-start | bytes 442376 | tf_op jit(solution)/shard_map/ppermute | solution.py:76
  13.4 28.9 %collective-permute-done.8.refs_9_ = bf16[576,128]{1,0:T(8,128)(2,1)S(1)} collective-permute-done((bf16[576,128]{1,0:T(8,128)(2,1)S(1)}, bf16[576,128]{1,0:T(8,128)(2,1)S(1)}, u32[]{:S(2)}, u32[]{:S(2)}) %collective-permute-start.8) | collective-permute-done | bytes 147488 | tf_op jit(solution)/shard_map/ppermute | solution.py:76
  42.8 2.2 %collective-permute-start.11 = (bf16[576,128]{1,0:T(8,128)(2,1)S(1)}, bf16[576,128]{1,0:T(8,128)(2,1)S(1)}, u32[]{:S(2)}, u32[]{:S(2)}) collective-permute-start(bf16[576,128]{1,0:T(8,128)(2,1)S(1)} %collective-permute-done.8.refs_9_), channel_id=1, source_target_pairs={{0,24},{8,16},{16,8},{24,0},{1,25},{9,17},{17,9},{25,1},{2,26},{10... | collective-permute-start | bytes 442376 | tf_op jit(solution)/shard_map/ppermute | solution.py:67
  45.2 1.8 %collective-permute-done.4.refs_5_ = bf16[576,128]{1,0:T(8,128)(2,1)S(1)} collective-permute-done((bf16[576,128]{1,0:T(8,128)(2,1)S(1)}, bf16[576,128]{1,0:T(8,128)(2,1)S(1)}, u32[]{:S(2)}, u32[]{:S(2)}) %collective-permute-start.4) | collective-permute-done | bytes 147488 | tf_op jit(solution)/shard_map/ppermute | solution.py:76
  51.0 1.7 %collective-permute-done.10.refs_11_ = bf16[576,128]{1,0:T(8,128)(2,1)S(1)} collective-permute-done((bf16[576,128]{1,0:T(8,128)(2,1)S(1)}, bf16[576,128]{1,0:T(8,128)(2,1)S(1)}, u32[]{:S(2)}, u32[]{:S(2)}) %collective-permute-start.10) | collective-permute-done | bytes 147488 | tf_op jit(solution)/shard_map/ppermute | solution.py:67
  52.7 1.4 collective-permute-start.5
  57.6 1.7 %collective-permute-done.6.refs_7_ = bf16[576,128]{1,0:T(8,128)(2,1)S(1)} collective-permute-done((bf16[576,128]{1,0:T(8,128)(2,1)S(1)}, bf16[576,128]{1,0:T(8,128)(2,1)S(1)}, u32[]{:S(2)}, u32[]{:S(2)}) %collective-permute-start.6) | collective-permute-done | bytes 147488 | tf_op jit(solution)/shard_map/ppermute | solution.py:67
  62.7 2.3 %collective-permute-start.23 = (bf16[576,128]{1,0:T(8,128)(2,1)S(1)}, bf16[576,128]{1,0:T(8,128)(2,1)S(1)}, u32[]{:S(2)}, u32[]{:S(2)}) collective-permute-start(bf16[576,128]{1,0:T(8,128)(2,1)S(1)} %collective-permute-done.10.refs_11_), channel_id=1, source_target_pairs={{0,1},{1,0},{2,3},{3,2},{4,5},{5,4},{6,7},{7,6},{8,9},{9,8},{10,11... | collective-permute-start | bytes 442376 | tf_op jit(solution)/shard_map/ppermute | solution.py:76
  65.0 1.5 %collective-permute-done.2.refs_3_ = bf16[576,128]{1,0:T(8,128)(2,1)} collective-permute-done((bf16[576,128]{1,0:T(8,128)(2,1)S(1)}, bf16[576,128]{1,0:T(8,128)(2,1)}, u32[]{:S(2)}, u32[]{:S(2)}) %collective-permute-start.2) | collective-permute-done | bytes 147488 | tf_op jit(solution)/shard_map/ppermute | solution.py:67
  83.0 5.8 %mlp.1 = (bf16[128,512]{1,0:T(8,128)(2,1)}, bf16[128,512]{1,0:T(8,128)(2,1)}, bf16[128,512]{1,0:T(8,128)(2,1)}, bf16[128,512]{1,0:T(8,128)(2,1)}, bf16[128,512]{...) custom-call(bf16[8,128,512]{2,1,0:T(8,128)(2,1)S(1)} %all-to-all-don, ...), custom_call_target="tpu_custom_call" | custom-call | tf_op jit(solution)/shard_map/mlp/pallas_call | solution.py:267
  88.9 14.0 %all_to_all.10.w_ref = bf16[8,32,512]{2,1,0:T(8,128)(2,1)S(1)} all-to-all(bf16[8,32,512]{2,1,0:T(8,128)(2,1)} %get-tuple-element.30), channel_id=1, replica_groups=mesh['dom'=4,'tp'=8] {'tp'}, dimensions={0} | all-to-all | bytes 524288 | tf_op jit(solution)/shard_map/all_to_all | solution.py:62
  102.9 2.8 %sums.1 = (f32[288,128]{1,0:T(8,128)S(1)}, bf16[288,128]{1,0:T(8,128)(2,1)S(1)}, bf16[288,128]{1,0:T(8,128)(2,1)S(1)}, bf16[288,128]{1,0:T(8,128)(2,1)S(1)}) custom-call(s32[32]{0:T(128)} %bitcast.13, bf16[8,32,512]{2,1,0:T(8,128)(2,1)S(1)} %all_to_all.10.w_ref, f32[10,32,128]{2,1,0:T(8,128)S(1)} %get-tuple-element.31.h_ref), custom_call_target="tpu_custom_call" | custom-call | tf_op jit(solution)/shard_map/sums/pallas_call | solution.py:448
  108.4 1.9 %collective-permute-start.31 = (bf16[128,512]{1,0:T(8,128)(2,1)}, bf16[128,512]{1,0:T(8,128)(2,1)S(1)}, u32[]{:S(2)}, u32[]{:S(2)}) collective-permute-start(bf16[128,512]{1,0:T(8,128)(2,1)} %get-tuple-element.39), channel_id=1, source_target_pairs={{0,1},{1,0},{2,3},{3,2},{4,5},{5,4},{6,7},{7,6},{8,9},{9,8},{10,11... | collective-permute-start | bytes 393224 | tf_op jit(solution)/shard_map/ppermute | solution.py:76
  110.3 1.7 %collective-permute-start.32 = (bf16[128,512]{1,0:T(8,128)(2,1)}, bf16[128,512]{1,0:T(8,128)(2,1)S(1)}, u32[]{:S(2)}, u32[]{:S(2)}) collective-permute-start(bf16[128,512]{1,0:T(8,128)(2,1)} %get-tuple-element.40), channel_id=1, source_target_pairs={{0,2},{1,3},{2,0},{3,1},{4,6},{5,7},{6,4},{7,5},{8,10},{9,11},{10,... | collective-permute-start | bytes 393224 | tf_op jit(solution)/shard_map/ppermute | solution.py:76
  112.0 1.5 %collective-permute-start.30 = (bf16[288,128]{1,0:T(8,128)(2,1)S(1)}, bf16[288,128]{1,0:T(8,128)(2,1)S(1)}, u32[]{:S(2)}, u32[]{:S(2)}) collective-permute-start(bf16[288,128]{1,0:T(8,128)(2,1)S(1)} %get-tuple-element.47.refs_0_), channel_id=1, source_target_pairs={{0,24},{8,16},{16,8},{24,0},{1,25},{9,17},{17,9},{25,1},{2,26},{10... | collective-permute-start | bytes 221192 | tf_op jit(solution)/shard_map/ppermute | solution.py:67
  114.8 4.8 %collective-permute-start.33 = (bf16[128,512]{1,0:T(8,128)(2,1)S(1)}, bf16[128,512]{1,0:T(8,128)(2,1)S(1)}, u32[]{:S(2)}, u32[]{:S(2)}) collective-permute-start(bf16[128,512]{1,0:T(8,128)(2,1)S(1)} %copy-done.26), channel_id=1, source_target_pairs={{0,3},{1,2},{2,1},{3,0},{4,7},{5,6},{6,5},{7,4},{8,11},{9,10},{10,... | collective-permute-start | bytes 393224 | tf_op jit(solution)/shard_map/ppermute | solution.py:76
  119.6 1.6 %collective-permute-start.35 = (bf16[128,512]{1,0:T(8,128)(2,1)S(1)}, bf16[128,512]{1,0:T(8,128)(2,1)S(1)}, u32[]{:S(2)}, u32[]{:S(2)}) collective-permute-start(bf16[128,512]{1,0:T(8,128)(2,1)S(1)} %copy-done.24), channel_id=1, source_target_pairs={{0,5},{1,4},{2,7},{3,6},{4,1},{5,0},{6,3},{7,2},{8,13},{9,12},{10,... | collective-permute-start | bytes 393224 | tf_op jit(solution)/shard_map/ppermute | solution.py:76
  124.7 3.3 %invariants.1 = (f32[3,32,4096]{2,1,0:T(8,128)}, f32[8,128]{1,0:T(8,128)S(1)}) custom-call(s32[32]{0:T(128)} %bitcast.14, bf16[8,32,512]{2,1,0:T(8,128)(2,1)S(1)} %all_to_all.10.w_ref, f32[10,32,128]{2,1,0:T(8,128)S(1)} %get-tuple-element.31.h_ref, bf16[288,128]{1,0:T(8,128)(2,1)S(1)} %get-tuple-element.47.refs_0_, ...), custom_call_target="tpu_custom_call" | custom-call | tf_op jit(solution)/shard_map/invariants/pallas_call | solution.py:465
  128.0 8.5 %collective-permute-done.35.refs_5_ = bf16[128,512]{1,0:T(8,128)(2,1)S(1)} collective-permute-done((bf16[128,512]{1,0:T(8,128)(2,1)S(1)}, bf16[128,512]{1,0:T(8,128)(2,1)S(1)}, u32[]{:S(2)}, u32[]{:S(2)}) %collective-permute-start.35) | collective-permute-done | bytes 131104 | tf_op jit(solution)/shard_map/ppermute | solution.py:76
  136.5 4.1 %collective-permute-done.36.refs_6_ = bf16[128,512]{1,0:T(8,128)(2,1)S(1)} collective-permute-done((bf16[128,512]{1,0:T(8,128)(2,1)S(1)}, bf16[128,512]{1,0:T(8,128)(2,1)S(1)}, u32[]{:S(2)}, u32[]{:S(2)}) %collective-permute-start.36) | collective-permute-done | bytes 131104 | tf_op jit(solution)/shard_map/ppermute | solution.py:76
  140.6 3.4 %collective-permute-done.37.refs_7_ = bf16[128,512]{1,0:T(8,128)(2,1)S(1)} collective-permute-done((bf16[128,512]{1,0:T(8,128)(2,1)S(1)}, bf16[128,512]{1,0:T(8,128)(2,1)S(1)}, u32[]{:S(2)}, u32[]{:S(2)}) %collective-permute-start.37) | collective-permute-done | bytes 131104 | tf_op jit(solution)/shard_map/ppermute | solution.py:76
  (118 shorter events, 37.7 us)
Async XLA Ops:
  4.2 70.1 %all-to-all-start = ((bf16[8,128,512]{2,1,0:T(8,128)(2,1)}), bf16[8,128,512]{2,1,0:T(8,128)(2,1)S(1)}, u32[]{:S(2)}, u32[]{:S(2)}) async-start(bf16[8,128,512]{2,1,0:T(8,128)(2,1)} %split.1), calls=%async_computation | async-start | bytes 2097152 | tf_op jit(solution)/shard_map/all_to_all | solution.py:62
  9.9 32.4 %collective-permute-start.8 = (bf16[576,128]{1,0:T(8,128)(2,1)S(1)}, bf16[576,128]{1,0:T(8,128)(2,1)S(1)}, u32[]{:S(2)}, u32[]{:S(2)}) collective-permute-start(bf16[576,128]{1,0:T(8,128)(2,1)S(1)} %get-tuple-element.25.tie_ref), channel_id=1, source_target_pairs={{0,4},{1,5},{2,6},{3,7},{4,0},{5,1},{6,2},{7,3},{8,12},{9,13},{10,... | collective-permute-start | bytes 442376 | tf_op jit(solution)/shard_map/ppermute | solution.py:76
  12.0 35.1 %collective-permute-start.4 = (bf16[576,128]{1,0:T(8,128)(2,1)S(1)}, bf16[576,128]{1,0:T(8,128)(2,1)S(1)}, u32[]{:S(2)}, u32[]{:S(2)}) collective-permute-start(bf16[576,128]{1,0:T(8,128)(2,1)S(1)} %get-tuple-element.25.tie_ref), channel_id=1, source_target_pairs={{0,6},{1,7},{2,4},{3,5},{4,2},{5,3},{6,0},{7,1},{8,14},{9,15},{10,... | collective-permute-start | bytes 442376 | tf_op jit(solution)/shard_map/ppermute | solution.py:76
  12.0 36.3 %collective-permute-start = (bf16[576,128]{1,0:T(8,128)(2,1)S(1)}, bf16[576,128]{1,0:T(8,128)(2,1)S(1)}, u32[]{:S(2)}, u32[]{:S(2)}) collective-permute-start(bf16[576,128]{1,0:T(8,128)(2,1)S(1)} %get-tuple-element.25.tie_ref), channel_id=1, source_target_pairs={{0,2},{1,3},{2,0},{3,1},{4,6},{5,7},{6,4},{7,5},{8,10},{9,11},{10,... | collective-permute-start | bytes 442376 | tf_op jit(solution)/shard_map/ppermute | solution.py:76
  42.3 7.2 %collective-permute-start.21 = (bf16[576,128]{1,0:T(8,128)(2,1)S(1)}, bf16[576,128]{1,0:T(8,128)(2,1)S(1)}, u32[]{:S(2)}, u32[]{:S(2)}) collective-permute-start(bf16[576,128]{1,0:T(8,128)(2,1)S(1)} %collective-permute-done.8.refs_9_), channel_id=1, source_target_pairs={{0,1},{1,0},{2,3},{3,2},{4,5},{5,4},{6,7},{7,6},{8,9},{9,8},{10,11... | collective-permute-start | bytes 442376 | tf_op jit(solution)/shard_map/ppermute | solution.py:76
  42.8 7.9 %collective-permute-start.11 = (bf16[576,128]{1,0:T(8,128)(2,1)S(1)}, bf16[576,128]{1,0:T(8,128)(2,1)S(1)}, u32[]{:S(2)}, u32[]{:S(2)}) collective-permute-start(bf16[576,128]{1,0:T(8,128)(2,1)S(1)} %collective-permute-done.8.refs_9_), channel_id=1, source_target_pairs={{0,24},{8,16},{16,8},{24,0},{1,25},{9,17},{17,9},{25,1},{2,26},{10... | collective-permute-start | bytes 442376 | tf_op jit(solution)/shard_map/ppermute | solution.py:67
  45.0 7.7 %collective-permute-start.10 = (bf16[576,128]{1,0:T(8,128)(2,1)S(1)}, bf16[576,128]{1,0:T(8,128)(2,1)S(1)}, u32[]{:S(2)}, u32[]{:S(2)}) collective-permute-start(bf16[576,128]{1,0:T(8,128)(2,1)S(1)} %collective-permute-done.8.refs_9_), channel_id=1, source_target_pairs={{0,16},{8,24},{16,0},{24,8},{1,17},{9,25},{17,1},{25,9},{2,18},{10... | collective-permute-start | bytes 442376 | tf_op jit(solution)/shard_map/ppermute | solution.py:67
  47.1 7.1 %collective-permute-start.9 = (bf16[576,128]{1,0:T(8,128)(2,1)S(1)}, bf16[576,128]{1,0:T(8,128)(2,1)S(1)}, u32[]{:S(2)}, u32[]{:S(2)}) collective-permute-start(bf16[576,128]{1,0:T(8,128)(2,1)S(1)} %collective-permute-done.8.refs_9_), channel_id=1, source_target_pairs={{0,8},{8,0},{16,24},{24,16},{1,9},{9,1},{17,25},{25,17},{2,10},{10... | collective-permute-start | bytes 442376 | tf_op jit(solution)/shard_map/ppermute | solution.py:67
  49.5 6.8 %collective-permute-start.7 = (bf16[576,128]{1,0:T(8,128)(2,1)S(1)}, bf16[576,128]{1,0:T(8,128)(2,1)S(1)}, u32[]{:S(2)}, u32[]{:S(2)}) collective-permute-start(bf16[576,128]{1,0:T(8,128)(2,1)S(1)} %collective-permute-done.4.refs_5_), channel_id=1, source_target_pairs={{0,24},{8,16},{16,8},{24,0},{1,25},{9,17},{17,9},{25,1},{2,26},{10... | collective-permute-start | bytes 442376 | tf_op jit(solution)/shard_map/ppermute | solution.py:67
  50.8 8.6 %collective-permute-start.6 = (bf16[576,128]{1,0:T(8,128)(2,1)S(1)}, bf16[576,128]{1,0:T(8,128)(2,1)S(1)}, u32[]{:S(2)}, u32[]{:S(2)}) collective-permute-start(bf16[576,128]{1,0:T(8,128)(2,1)S(1)} %collective-permute-done.4.refs_5_), channel_id=1, source_target_pairs={{0,16},{8,24},{16,0},{24,8},{1,17},{9,25},{17,1},{25,9},{2,18},{10... | collective-permute-start | bytes 442376 | tf_op jit(solution)/shard_map/ppermute | solution.py:67
  52.7 7.3 %collective-permute-start.5 = (bf16[576,128]{1,0:T(8,128)(2,1)S(1)}, bf16[576,128]{1,0:T(8,128)(2,1)}, u32[]{:S(2)}, u32[]{:S(2)}) collective-permute-start(bf16[576,128]{1,0:T(8,128)(2,1)S(1)} %collective-permute-done.4.refs_5_), channel_id=1, source_target_pairs={{0,8},{8,0},{16,24},{24,16},{1,9},{9,1},{17,25},{25,17},{2,10},{10... | collective-permute-start | bytes 442376 | tf_op jit(solution)/shard_map/ppermute | solution.py:67
  55.6 19.2 %collective-permute-start.12 = (bf16[4,576,128]{2,1,0:T(8,128)(2,1)S(1)}, bf16[4,576,128]{2,1,0:T(8,128)(2,1)S(1)}, u32[]{:S(2)}, u32[]{:S(2)}) collective-permute-start(bf16[4,576,128]{2,1,0:T(8,128)(2,1)S(1)} %get-tuple-element.29.refs_0_), channel_id=1, source_target_pairs={{0,1},{1,0},{2,3},{3,2},{4,5},{5,4},{6,7},{7,6},{8,9},{9,8},{10,11... | collective-permute-start | bytes 1769480 | tf_op jit(solution)/shard_map/ppermute | solution.py:76
  59.3 7.2 %collective-permute-start.2 = (bf16[576,128]{1,0:T(8,128)(2,1)S(1)}, bf16[576,128]{1,0:T(8,128)(2,1)}, u32[]{:S(2)}, u32[]{:S(2)}) collective-permute-start(bf16[576,128]{1,0:T(8,128)(2,1)S(1)} %collective-permute-done.refs_1_), channel_id=1, source_target_pairs={{0,16},{8,24},{16,0},{24,8},{1,17},{9,25},{17,1},{25,9},{2,18},{10... | collective-permute-start | bytes 442376 | tf_op jit(solution)/shard_map/ppermute | solution.py:67
  60.0 7.3 %collective-permute-start.1 = (bf16[576,128]{1,0:T(8,128)(2,1)S(1)}, bf16[576,128]{1,0:T(8,128)(2,1)}, u32[]{:S(2)}, u32[]{:S(2)}) collective-permute-start(bf16[576,128]{1,0:T(8,128)(2,1)S(1)} %collective-permute-done.refs_1_), channel_id=1, source_target_pairs={{0,8},{8,0},{16,24},{24,16},{1,9},{9,1},{17,25},{25,17},{2,10},{10... | collective-permute-start | bytes 442376 | tf_op jit(solution)/shard_map/ppermute | solution.py:67
  62.7 7.0 %collective-permute-start.23 = (bf16[576,128]{1,0:T(8,128)(2,1)S(1)}, bf16[576,128]{1,0:T(8,128)(2,1)S(1)}, u32[]{:S(2)}, u32[]{:S(2)}) collective-permute-start(bf16[576,128]{1,0:T(8,128)(2,1)S(1)} %collective-permute-done.10.refs_11_), channel_id=1, source_target_pairs={{0,1},{1,0},{2,3},{3,2},{4,5},{5,4},{6,7},{7,6},{8,9},{9,8},{10,11... | collective-permute-start | bytes 442376 | tf_op jit(solution)/shard_map/ppermute | solution.py:76
  110.3 9.3 %collective-permute-start.32 = (bf16[128,512]{1,0:T(8,128)(2,1)}, bf16[128,512]{1,0:T(8,128)(2,1)S(1)}, u32[]{:S(2)}, u32[]{:S(2)}) collective-permute-start(bf16[128,512]{1,0:T(8,128)(2,1)} %get-tuple-element.40), channel_id=1, source_target_pairs={{0,2},{1,3},{2,0},{3,1},{4,6},{5,7},{6,4},{7,5},{8,10},{9,11},{10,... | collective-permute-start | bytes 393224 | tf_op jit(solution)/shard_map/ppermute | solution.py:76
  112.0 7.5 %collective-permute-start.30 = (bf16[288,128]{1,0:T(8,128)(2,1)S(1)}, bf16[288,128]{1,0:T(8,128)(2,1)S(1)}, u32[]{:S(2)}, u32[]{:S(2)}) collective-permute-start(bf16[288,128]{1,0:T(8,128)(2,1)S(1)} %get-tuple-element.47.refs_0_), channel_id=1, source_target_pairs={{0,24},{8,16},{16,8},{24,0},{1,25},{9,17},{17,9},{25,1},{2,26},{10... | collective-permute-start | bytes 221192 | tf_op jit(solution)/shard_map/ppermute | solution.py:67
  113.6 7.6 %collective-permute-start.29 = (bf16[288,128]{1,0:T(8,128)(2,1)S(1)}, bf16[288,128]{1,0:T(8,128)(2,1)S(1)}, u32[]{:S(2)}, u32[]{:S(2)}) collective-permute-start(bf16[288,128]{1,0:T(8,128)(2,1)S(1)} %get-tuple-element.47.refs_0_), channel_id=1, source_target_pairs={{0,16},{8,24},{16,0},{24,8},{1,17},{9,25},{17,1},{25,9},{2,18},{10... | collective-permute-start | bytes 221192 | tf_op jit(solution)/shard_map/ppermute | solution.py:67
  114.0 8.6 %collective-permute-start.28 = (bf16[288,128]{1,0:T(8,128)(2,1)S(1)}, bf16[288,128]{1,0:T(8,128)(2,1)S(1)}, u32[]{:S(2)}, u32[]{:S(2)}) collective-permute-start(bf16[288,128]{1,0:T(8,128)(2,1)S(1)} %get-tuple-element.47.refs_0_), channel_id=1, source_target_pairs={{0,8},{8,0},{16,24},{24,16},{1,9},{9,1},{17,25},{25,17},{2,10},{10... | collective-permute-start | bytes 221192 | tf_op jit(solution)/shard_map/ppermute | solution.py:67
  114.8 13.2 %collective-permute-start.33 = (bf16[128,512]{1,0:T(8,128)(2,1)S(1)}, bf16[128,512]{1,0:T(8,128)(2,1)S(1)}, u32[]{:S(2)}, u32[]{:S(2)}) collective-permute-start(bf16[128,512]{1,0:T(8,128)(2,1)S(1)} %copy-done.26), channel_id=1, source_target_pairs={{0,3},{1,2},{2,1},{3,0},{4,7},{5,6},{6,5},{7,4},{8,11},{9,10},{10,... | collective-permute-start | bytes 393224 | tf_op jit(solution)/shard_map/ppermute | solution.py:76
  119.6 8.4 %collective-permute-start.34 = (bf16[128,512]{1,0:T(8,128)(2,1)S(1)}, bf16[128,512]{1,0:T(8,128)(2,1)S(1)}, u32[]{:S(2)}, u32[]{:S(2)}) collective-permute-start(bf16[128,512]{1,0:T(8,128)(2,1)S(1)} %copy-done.25), channel_id=1, source_target_pairs={{0,4},{1,5},{2,6},{3,7},{4,0},{5,1},{6,2},{7,3},{8,12},{9,13},{10,... | collective-permute-start | bytes 393224 | tf_op jit(solution)/shard_map/ppermute | solution.py:76
  119.6 16.9 %collective-permute-start.35 = (bf16[128,512]{1,0:T(8,128)(2,1)S(1)}, bf16[128,512]{1,0:T(8,128)(2,1)S(1)}, u32[]{:S(2)}, u32[]{:S(2)}) collective-permute-start(bf16[128,512]{1,0:T(8,128)(2,1)S(1)} %copy-done.24), channel_id=1, source_target_pairs={{0,5},{1,4},{2,7},{3,6},{4,1},{5,0},{6,3},{7,2},{8,13},{9,12},{10,... | collective-permute-start | bytes 393224 | tf_op jit(solution)/shard_map/ppermute | solution.py:76
  121.2 19.4 %collective-permute-start.36 = (bf16[128,512]{1,0:T(8,128)(2,1)S(1)}, bf16[128,512]{1,0:T(8,128)(2,1)S(1)}, u32[]{:S(2)}, u32[]{:S(2)}) collective-permute-start(bf16[128,512]{1,0:T(8,128)(2,1)S(1)} %copy-done.23), channel_id=1, source_target_pairs={{0,6},{1,7},{2,4},{3,5},{4,2},{5,3},{6,0},{7,1},{8,14},{9,15},{10,... | collective-permute-start | bytes 393224 | tf_op jit(solution)/shard_map/ppermute | solution.py:76
  122.6 21.4 %collective-permute-start.37 = (bf16[128,512]{1,0:T(8,128)(2,1)S(1)}, bf16[128,512]{1,0:T(8,128)(2,1)S(1)}, u32[]{:S(2)}, u32[]{:S(2)}) collective-permute-start(bf16[128,512]{1,0:T(8,128)(2,1)S(1)} %copy-done.22), channel_id=1, source_target_pairs={{0,7},{1,6},{2,5},{3,4},{4,3},{5,2},{6,1},{7,0},{8,15},{9,14},{10,... | collective-permute-start | bytes 393224 | tf_op jit(solution)/shard_map/ppermute | solution.py:76
  (42 other events, 502.4 us)

commit v5 on v4

--- a/solution.py
+++ b/solution.py
@@ -337,7 +337,7 @@
     per = edges // lanes
     total[...] = jnp.zeros_like(total)
 
-    def step(s, carry):
+    def step(s):
         for i in range(per):
             block = s * per + i
             weight = w_ref[s, :, i * lanes : (i + 1) * lanes].astype(f32)
@@ -350,9 +350,9 @@
             total[slot] += lax.dot_general(
                 contrib, chosen, (((1,), (1,)), ((), ())), preferred_element_type=f32
             )
-        return carry
-
-    lax.fori_loop(0, shards, step, 0)
+
+    for s in range(shards):
+        step(s)
     for j, out in enumerate(outs):
         out[...] = total[j].astype(out.dtype)
 
@@ -367,7 +367,7 @@
     for j in range(domains):
         env[j] = refs[j][...]
 
-    def step(s, carry):
+    def step(s):
         for i in range(per):
             block = s * per + i
             weight = w_ref[s, :, i * lanes : (i + 1) * lanes].astype(f32)
@@ -378,18 +378,18 @@
                 found[m * chan : (m + 1) * chan, :] * h_ref[m, pl.ds(block, 1), :]
                 for m in range(parts)
             ]
-            at = pl.multiple_of(block * lanes, lanes)
+            at = block * lanes
             out_ref[0, :, pl.ds(at, lanes)] = products[0] * weight
             out_ref[1, :, pl.ds(at, lanes)] = sum(products[2:4], products[1]) * weight
             out_ref[2, :, pl.ds(at, lanes)] = sum(products[5:9], products[4]) * weight
         leave(s).start()
-        return carry
 
     def leave(s):
-        chunk = (slice(None), slice(None), pl.ds(pl.multiple_of(s * edges, lanes), edges))
+        chunk = (slice(None), slice(None), pl.ds(s * edges, edges))
         return pltpu.make_async_copy(out_ref.at[chunk], result_ref.at[chunk], sems.at[s])
 
-    lax.fori_loop(0, shards, step, 0)
+    for s in range(shards):
+        step(s)
     for s in range(shards):
         leave(s).wait()
 
@@ -457,8 +457,7 @@
     )(target, weights, harmonic)
     env_raw = sums[0]
     for j in range(1, domains):
-        arrived = flip_dom(sums[j], j)
-        env_raw = env_raw + arrived.astype(f32)
+        env_raw = env_raw + flip_dom(sums[j], j).astype(f32)
     env_out = env_raw.reshape(parts, chan, atoms) * gain_sel[None, :, :] * env_factor
     env_half = env_out.astype(bf16).reshape(rows, atoms)
     looked = [env_half] + [flip_dom(env_half, j) for j in range(1, domains)]

time: 146 us -> 144 us (0.986)
  Pallas kernels: 17.2 us -> 14.9 us
  transfers between devices with their start and end apart: 39 -> 39, of which waited for: 10 -> 10; matrix products, arithmetic and copies ran while one was open for 1% -> 1% of each run, Pallas kernels for 3% -> 2%
where the time goes in v5:
time: 144 us
  waiting for transfers between devices  54 us (38%)
  starting transfers between devices  45.1 us (31%)
  Pallas kernels  14.9 us (10%)
  local copies, waits for them, and re-layouts  14.2 us (10%)
  blocking collectives  14 us (10%)
    ppermute x23, waiting for transfers between devices, flip_tp(): return lax.ppermute(array, 'tp', [(t, t ^ mask) for t in range(count)])  48.4 us
    ppermute x23, starting transfers between devices, flip_tp(): return lax.ppermute(array, 'tp', [(t, t ^ mask) for t in range(count)])  24.7 us
    ppermute x15, starting transfers between devices, flip_dom(): return lax.ppermute(array, 'dom', [(i, i ^ mask) for i in range(count)])  14.6 us
    unnamed x54, local copies, waits for them, and re-layouts  14.2 us
    all_to_all x1, blocking collectives, swap_blocks(): return lax.all_to_all(array, axis, split_axis=0, concat_axis=0, tiled=True)  14 us
    pallas_call x1, Pallas kernels, spread_mlp(): pl.pallas_call(functools.partial(mlp_kernel, quarters=domains, chips=chip...  5.82 us
    all_to_all x1, starting transfers between devices, swap_blocks(): return lax.all_to_all(array, axis, split_axis=0, concat_axis=0, tiled=True)  5.75 us
    ppermute x15, waiting for transfers between devices, flip_dom(): return lax.ppermute(array, 'dom', [(i, i ^ mask) for i in range(count)])  5.67 us
  transfers between devices with their start and end apart: 39, of which 10 were waited for; matrix products, arithmetic and copies ran while one was open for 1% of the time, Pallas kernels for 2%

profile of v5, /device:TPU:9, one launch (start us, length us, event | category | flops | bytes accessed | tf_op | source)
XLA Modules:
  0.0 143.9 jit_solution(8480531124251960978)
XLA Ops:
  2.0 2.1 %split.1 = bf16[8,128,512]{2,1,0:T(8,128)(2,1)} custom-call(bf16[128,4096]{1,0:T(8,128)(2,1)} %x_ref.1, bf16[576,128]{1,0:T(8,128)(2,1)S(1)} %get-tuple-element.25.tie_ref), custom_call_target="tpu_custom_call" | custom-call | tf_op jit(solution)/shard_map/split/pallas_call | solution.py:247
  4.2 5.7 %all-to-all-start = ((bf16[8,128,512]{2,1,0:T(8,128)(2,1)}), bf16[8,128,512]{2,1,0:T(8,128)(2,1)S(1)}, u32[]{:S(2)}, u32[]{:S(2)}) async-start(bf16[8,128,512]{2,1,0:T(8,128)(2,1)} %split.1), calls=%async_computation | async-start | bytes 2097152 | tf_op jit(solution)/shard_map/all_to_all | solution.py:62
  9.9 2.1 %collective-permute-start.8 = (bf16[576,128]{1,0:T(8,128)(2,1)S(1)}, bf16[576,128]{1,0:T(8,128)(2,1)S(1)}, u32[]{:S(2)}, u32[]{:S(2)}) collective-permute-start(bf16[576,128]{1,0:T(8,128)(2,1)S(1)} %get-tuple-element.25.tie_ref), channel_id=1, source_target_pairs={{0,4},{1,5},{2,6},{3,7},{4,0},{5,1},{6,2},{7,3},{8,12},{9,13},{10,... | collective-permute-start | bytes 442376 | tf_op jit(solution)/shard_map/ppermute | solution.py:76
  12.0 1.5 %collective-permute-start = (bf16[576,128]{1,0:T(8,128)(2,1)S(1)}, bf16[576,128]{1,0:T(8,128)(2,1)S(1)}, u32[]{:S(2)}, u32[]{:S(2)}) collective-permute-start(bf16[576,128]{1,0:T(8,128)(2,1)S(1)} %get-tuple-element.25.tie_ref), channel_id=1, source_target_pairs={{0,2},{1,3},{2,0},{3,1},{4,6},{5,7},{6,4},{7,5},{8,10},{9,11},{10,... | collective-permute-start | bytes 442376 | tf_op jit(solution)/shard_map/ppermute | solution.py:76
  13.4 28.9 %collective-permute-done.8.refs_9_ = bf16[576,128]{1,0:T(8,128)(2,1)S(1)} collective-permute-done((bf16[576,128]{1,0:T(8,128)(2,1)S(1)}, bf16[576,128]{1,0:T(8,128)(2,1)S(1)}, u32[]{:S(2)}, u32[]{:S(2)}) %collective-permute-start.8) | collective-permute-done | bytes 147488 | tf_op jit(solution)/shard_map/ppermute | solution.py:76
  42.8 2.2 %collective-permute-start.11 = (bf16[576,128]{1,0:T(8,128)(2,1)S(1)}, bf16[576,128]{1,0:T(8,128)(2,1)S(1)}, u32[]{:S(2)}, u32[]{:S(2)}) collective-permute-start(bf16[576,128]{1,0:T(8,128)(2,1)S(1)} %collective-permute-done.8.refs_9_), channel_id=1, source_target_pairs={{0,24},{8,16},{16,8},{24,0},{1,25},{9,17},{17,9},{25,1},{2,26},{10... | collective-permute-start | bytes 442376 | tf_op jit(solution)/shard_map/ppermute | solution.py:67
  45.2 1.8 %collective-permute-done.4.refs_5_ = bf16[576,128]{1,0:T(8,128)(2,1)S(1)} collective-permute-done((bf16[576,128]{1,0:T(8,128)(2,1)S(1)}, bf16[576,128]{1,0:T(8,128)(2,1)S(1)}, u32[]{:S(2)}, u32[]{:S(2)}) %collective-permute-start.4) | collective-permute-done | bytes 147488 | tf_op jit(solution)/shard_map/ppermute | solution.py:76
  51.0 1.7 %collective-permute-done.10.refs_11_ = bf16[576,128]{1,0:T(8,128)(2,1)S(1)} collective-permute-done((bf16[576,128]{1,0:T(8,128)(2,1)S(1)}, bf16[576,128]{1,0:T(8,128)(2,1)S(1)}, u32[]{:S(2)}, u32[]{:S(2)}) %collective-permute-start.10) | collective-permute-done | bytes 147488 | tf_op jit(solution)/shard_map/ppermute | solution.py:67
  52.7 1.4 collective-permute-start.5
  57.6 1.7 %collective-permute-done.6.refs_7_ = bf16[576,128]{1,0:T(8,128)(2,1)S(1)} collective-permute-done((bf16[576,128]{1,0:T(8,128)(2,1)S(1)}, bf16[576,128]{1,0:T(8,128)(2,1)S(1)}, u32[]{:S(2)}, u32[]{:S(2)}) %collective-permute-start.6) | collective-permute-done | bytes 147488 | tf_op jit(solution)/shard_map/ppermute | solution.py:67
  62.7 2.3 %collective-permute-start.23 = (bf16[576,128]{1,0:T(8,128)(2,1)S(1)}, bf16[576,128]{1,0:T(8,128)(2,1)S(1)}, u32[]{:S(2)}, u32[]{:S(2)}) collective-permute-start(bf16[576,128]{1,0:T(8,128)(2,1)S(1)} %collective-permute-done.10.refs_11_), channel_id=1, source_target_pairs={{0,1},{1,0},{2,3},{3,2},{4,5},{5,4},{6,7},{7,6},{8,9},{9,8},{10,11... | collective-permute-start | bytes 442376 | tf_op jit(solution)/shard_map/ppermute | solution.py:76
  65.0 1.5 %collective-permute-done.2.refs_3_ = bf16[576,128]{1,0:T(8,128)(2,1)} collective-permute-done((bf16[576,128]{1,0:T(8,128)(2,1)S(1)}, bf16[576,128]{1,0:T(8,128)(2,1)}, u32[]{:S(2)}, u32[]{:S(2)}) %collective-permute-start.2) | collective-permute-done | bytes 147488 | tf_op jit(solution)/shard_map/ppermute | solution.py:67
  83.0 5.8 %mlp.1 = (bf16[128,512]{1,0:T(8,128)(2,1)}, bf16[128,512]{1,0:T(8,128)(2,1)}, bf16[128,512]{1,0:T(8,128)(2,1)}, bf16[128,512]{1,0:T(8,128)(2,1)}, bf16[128,512]{...) custom-call(bf16[8,128,512]{2,1,0:T(8,128)(2,1)S(1)} %all-to-all-don, ...), custom_call_target="tpu_custom_call" | custom-call | tf_op jit(solution)/shard_map/mlp/pallas_call | solution.py:267
  88.9 14.0 %all_to_all.10.w_ref = bf16[8,32,512]{2,1,0:T(8,128)(2,1)S(1)} all-to-all(bf16[8,32,512]{2,1,0:T(8,128)(2,1)} %get-tuple-element.30), channel_id=1, replica_groups=mesh['dom'=4,'tp'=8] {'tp'}, dimensions={0} | all-to-all | bytes 524288 | tf_op jit(solution)/shard_map/all_to_all | solution.py:62
  102.9 1.6 %sums.1 = (f32[288,128]{1,0:T(8,128)S(1)}, bf16[288,128]{1,0:T(8,128)(2,1)S(1)}, bf16[288,128]{1,0:T(8,128)(2,1)S(1)}, bf16[288,128]{1,0:T(8,128)(2,1)S(1)}) custom-call(s32[32]{0:T(128)} %bitcast.13, bf16[8,32,512]{2,1,0:T(8,128)(2,1)S(1)} %all_to_all.10.w_ref, f32[10,32,128]{2,1,0:T(8,128)S(1)} %get-tuple-element.31.h_ref), custom_call_target="tpu_custom_call" | custom-call | tf_op jit(solution)/shard_map/sums/pallas_call | solution.py:448
  107.2 1.9 %collective-permute-start.31 = (bf16[128,512]{1,0:T(8,128)(2,1)}, bf16[128,512]{1,0:T(8,128)(2,1)S(1)}, u32[]{:S(2)}, u32[]{:S(2)}) collective-permute-start(bf16[128,512]{1,0:T(8,128)(2,1)} %get-tuple-element.39), channel_id=1, source_target_pairs={{0,1},{1,0},{2,3},{3,2},{4,5},{5,4},{6,7},{7,6},{8,9},{9,8},{10,11... | collective-permute-start | bytes 393224 | tf_op jit(solution)/shard_map/ppermute | solution.py:76
  109.1 1.7 %collective-permute-start.32 = (bf16[128,512]{1,0:T(8,128)(2,1)}, bf16[128,512]{1,0:T(8,128)(2,1)S(1)}, u32[]{:S(2)}, u32[]{:S(2)}) collective-permute-start(bf16[128,512]{1,0:T(8,128)(2,1)} %get-tuple-element.40), channel_id=1, source_target_pairs={{0,2},{1,3},{2,0},{3,1},{4,6},{5,7},{6,4},{7,5},{8,10},{9,11},{10,... | collective-permute-start | bytes 393224 | tf_op jit(solution)/shard_map/ppermute | solution.py:76
  110.9 1.6 %collective-permute-start.30 = (bf16[288,128]{1,0:T(8,128)(2,1)S(1)}, bf16[288,128]{1,0:T(8,128)(2,1)S(1)}, u32[]{:S(2)}, u32[]{:S(2)}) collective-permute-start(bf16[288,128]{1,0:T(8,128)(2,1)S(1)} %get-tuple-element.47.refs_0_), channel_id=1, source_target_pairs={{0,24},{8,16},{16,8},{24,0},{1,25},{9,17},{17,9},{25,1},{2,26},{10... | collective-permute-start | bytes 221192 | tf_op jit(solution)/shard_map/ppermute | solution.py:67
  113.6 4.8 %collective-permute-start.33 = (bf16[128,512]{1,0:T(8,128)(2,1)S(1)}, bf16[128,512]{1,0:T(8,128)(2,1)S(1)}, u32[]{:S(2)}, u32[]{:S(2)}) collective-permute-start(bf16[128,512]{1,0:T(8,128)(2,1)S(1)} %copy-done.26), channel_id=1, source_target_pairs={{0,3},{1,2},{2,1},{3,0},{4,7},{5,6},{6,5},{7,4},{8,11},{9,10},{10,... | collective-permute-start | bytes 393224 | tf_op jit(solution)/shard_map/ppermute | solution.py:76
  118.4 1.6 %collective-permute-start.35 = (bf16[128,512]{1,0:T(8,128)(2,1)S(1)}, bf16[128,512]{1,0:T(8,128)(2,1)S(1)}, u32[]{:S(2)}, u32[]{:S(2)}) collective-permute-start(bf16[128,512]{1,0:T(8,128)(2,1)S(1)} %copy-done.24), channel_id=1, source_target_pairs={{0,5},{1,4},{2,7},{3,6},{4,1},{5,0},{6,3},{7,2},{8,13},{9,12},{10,... | collective-permute-start | bytes 393224 | tf_op jit(solution)/shard_map/ppermute | solution.py:76
  123.5 2.2 %invariants.1 = (f32[3,32,4096]{2,1,0:T(8,128)}, f32[8,128]{1,0:T(8,128)S(1)}) custom-call(s32[32]{0:T(128)} %bitcast.14, bf16[8,32,512]{2,1,0:T(8,128)(2,1)S(1)} %all_to_all.10.w_ref, f32[10,32,128]{2,1,0:T(8,128)S(1)} %get-tuple-element.31.h_ref, bf16[288,128]{1,0:T(8,128)(2,1)S(1)} %get-tuple-element.47.refs_0_, ...), custom_call_target="tpu_custom_call" | custom-call | tf_op jit(solution)/shard_map/invariants/pallas_call | solution.py:464
  125.7 9.6 %collective-permute-done.35.refs_5_ = bf16[128,512]{1,0:T(8,128)(2,1)S(1)} collective-permute-done((bf16[128,512]{1,0:T(8,128)(2,1)S(1)}, bf16[128,512]{1,0:T(8,128)(2,1)S(1)}, u32[]{:S(2)}, u32[]{:S(2)}) %collective-permute-start.35) | collective-permute-done | bytes 131104 | tf_op jit(solution)/shard_map/ppermute | solution.py:76
  135.3 4.1 %collective-permute-done.36.refs_6_ = bf16[128,512]{1,0:T(8,128)(2,1)S(1)} collective-permute-done((bf16[128,512]{1,0:T(8,128)(2,1)S(1)}, bf16[128,512]{1,0:T(8,128)(2,1)S(1)}, u32[]{:S(2)}, u32[]{:S(2)}) %collective-permute-start.36) | collective-permute-done | bytes 131104 | tf_op jit(solution)/shard_map/ppermute | solution.py:76
  139.4 3.4 %collective-permute-done.37.refs_7_ = bf16[128,512]{1,0:T(8,128)(2,1)S(1)} collective-permute-done((bf16[128,512]{1,0:T(8,128)(2,1)S(1)}, bf16[128,512]{1,0:T(8,128)(2,1)S(1)}, u32[]{:S(2)}, u32[]{:S(2)}) %collective-permute-start.37) | collective-permute-done | bytes 131104 | tf_op jit(solution)/shard_map/ppermute | solution.py:76
  (118 shorter events, 37.8 us)
Async XLA Ops:
  4.2 70.1 %all-to-all-start = ((bf16[8,128,512]{2,1,0:T(8,128)(2,1)}), bf16[8,128,512]{2,1,0:T(8,128)(2,1)S(1)}, u32[]{:S(2)}, u32[]{:S(2)}) async-start(bf16[8,128,512]{2,1,0:T(8,128)(2,1)} %split.1), calls=%async_computation | async-start | bytes 2097152 | tf_op jit(solution)/shard_map/all_to_all | solution.py:62
  9.9 32.4 %collective-permute-start.8 = (bf16[576,128]{1,0:T(8,128)(2,1)S(1)}, bf16[576,128]{1,0:T(8,128)(2,1)S(1)}, u32[]{:S(2)}, u32[]{:S(2)}) collective-permute-start(bf16[576,128]{1,0:T(8,128)(2,1)S(1)} %get-tuple-element.25.tie_ref), channel_id=1, source_target_pairs={{0,4},{1,5},{2,6},{3,7},{4,0},{5,1},{6,2},{7,3},{8,12},{9,13},{10,... | collective-permute-start | bytes 442376 | tf_op jit(solution)/shard_map/ppermute | solution.py:76
  12.0 35.1 %collective-permute-start.4 = (bf16[576,128]{1,0:T(8,128)(2,1)S(1)}, bf16[576,128]{1,0:T(8,128)(2,1)S(1)}, u32[]{:S(2)}, u32[]{:S(2)}) collective-permute-start(bf16[576,128]{1,0:T(8,128)(2,1)S(1)} %get-tuple-element.25.tie_ref), channel_id=1, source_target_pairs={{0,6},{1,7},{2,4},{3,5},{4,2},{5,3},{6,0},{7,1},{8,14},{9,15},{10,... | collective-permute-start | bytes 442376 | tf_op jit(solution)/shard_map/ppermute | solution.py:76
  12.0 36.3 %collective-permute-start = (bf16[576,128]{1,0:T(8,128)(2,1)S(1)}, bf16[576,128]{1,0:T(8,128)(2,1)S(1)}, u32[]{:S(2)}, u32[]{:S(2)}) collective-permute-start(bf16[576,128]{1,0:T(8,128)(2,1)S(1)} %get-tuple-element.25.tie_ref), channel_id=1, source_target_pairs={{0,2},{1,3},{2,0},{3,1},{4,6},{5,7},{6,4},{7,5},{8,10},{9,11},{10,... | collective-permute-start | bytes 442376 | tf_op jit(solution)/shard_map/ppermute | solution.py:76
  42.3 7.2 %collective-permute-start.21 = (bf16[576,128]{1,0:T(8,128)(2,1)S(1)}, bf16[576,128]{1,0:T(8,128)(2,1)S(1)}, u32[]{:S(2)}, u32[]{:S(2)}) collective-permute-start(bf16[576,128]{1,0:T(8,128)(2,1)S(1)} %collective-permute-done.8.refs_9_), channel_id=1, source_target_pairs={{0,1},{1,0},{2,3},{3,2},{4,5},{5,4},{6,7},{7,6},{8,9},{9,8},{10,11... | collective-permute-start | bytes 442376 | tf_op jit(solution)/shard_map/ppermute | solution.py:76
  42.8 7.9 %collective-permute-start.11 = (bf16[576,128]{1,0:T(8,128)(2,1)S(1)}, bf16[576,128]{1,0:T(8,128)(2,1)S(1)}, u32[]{:S(2)}, u32[]{:S(2)}) collective-permute-start(bf16[576,128]{1,0:T(8,128)(2,1)S(1)} %collective-permute-done.8.refs_9_), channel_id=1, source_target_pairs={{0,24},{8,16},{16,8},{24,0},{1,25},{9,17},{17,9},{25,1},{2,26},{10... | collective-permute-start | bytes 442376 | tf_op jit(solution)/shard_map/ppermute | solution.py:67
  45.0 7.7 %collective-permute-start.10 = (bf16[576,128]{1,0:T(8,128)(2,1)S(1)}, bf16[576,128]{1,0:T(8,128)(2,1)S(1)}, u32[]{:S(2)}, u32[]{:S(2)}) collective-permute-start(bf16[576,128]{1,0:T(8,128)(2,1)S(1)} %collective-permute-done.8.refs_9_), channel_id=1, source_target_pairs={{0,16},{8,24},{16,0},{24,8},{1,17},{9,25},{17,1},{25,9},{2,18},{10... | collective-permute-start | bytes 442376 | tf_op jit(solution)/shard_map/ppermute | solution.py:67
  47.1 7.1 %collective-permute-start.9 = (bf16[576,128]{1,0:T(8,128)(2,1)S(1)}, bf16[576,128]{1,0:T(8,128)(2,1)S(1)}, u32[]{:S(2)}, u32[]{:S(2)}) collective-permute-start(bf16[576,128]{1,0:T(8,128)(2,1)S(1)} %collective-permute-done.8.refs_9_), channel_id=1, source_target_pairs={{0,8},{8,0},{16,24},{24,16},{1,9},{9,1},{17,25},{25,17},{2,10},{10... | collective-permute-start | bytes 442376 | tf_op jit(solution)/shard_map/ppermute | solution.py:67
  49.5 6.8 %collective-permute-start.7 = (bf16[576,128]{1,0:T(8,128)(2,1)S(1)}, bf16[576,128]{1,0:T(8,128)(2,1)S(1)}, u32[]{:S(2)}, u32[]{:S(2)}) collective-permute-start(bf16[576,128]{1,0:T(8,128)(2,1)S(1)} %collective-permute-done.4.refs_5_), channel_id=1, source_target_pairs={{0,24},{8,16},{16,8},{24,0},{1,25},{9,17},{17,9},{25,1},{2,26},{10... | collective-permute-start | bytes 442376 | tf_op jit(solution)/shard_map/ppermute | solution.py:67
  50.8 8.6 %collective-permute-start.6 = (bf16[576,128]{1,0:T(8,128)(2,1)S(1)}, bf16[576,128]{1,0:T(8,128)(2,1)S(1)}, u32[]{:S(2)}, u32[]{:S(2)}) collective-permute-start(bf16[576,128]{1,0:T(8,128)(2,1)S(1)} %collective-permute-done.4.refs_5_), channel_id=1, source_target_pairs={{0,16},{8,24},{16,0},{24,8},{1,17},{9,25},{17,1},{25,9},{2,18},{10... | collective-permute-start | bytes 442376 | tf_op jit(solution)/shard_map/ppermute | solution.py:67
  52.7 7.3 %collective-permute-start.5 = (bf16[576,128]{1,0:T(8,128)(2,1)S(1)}, bf16[576,128]{1,0:T(8,128)(2,1)}, u32[]{:S(2)}, u32[]{:S(2)}) collective-permute-start(bf16[576,128]{1,0:T(8,128)(2,1)S(1)} %collective-permute-done.4.refs_5_), channel_id=1, source_target_pairs={{0,8},{8,0},{16,24},{24,16},{1,9},{9,1},{17,25},{25,17},{2,10},{10... | collective-permute-start | bytes 442376 | tf_op jit(solution)/shard_map/ppermute | solution.py:67
  55.6 19.2 %collective-permute-start.12 = (bf16[4,576,128]{2,1,0:T(8,128)(2,1)S(1)}, bf16[4,576,128]{2,1,0:T(8,128)(2,1)S(1)}, u32[]{:S(2)}, u32[]{:S(2)}) collective-permute-start(bf16[4,576,128]{2,1,0:T(8,128)(2,1)S(1)} %get-tuple-element.29.refs_0_), channel_id=1, source_target_pairs={{0,1},{1,0},{2,3},{3,2},{4,5},{5,4},{6,7},{7,6},{8,9},{9,8},{10,11... | collective-permute-start | bytes 1769480 | tf_op jit(solution)/shard_map/ppermute | solution.py:76
  59.3 7.2 %collective-permute-start.2 = (bf16[576,128]{1,0:T(8,128)(2,1)S(1)}, bf16[576,128]{1,0:T(8,128)(2,1)}, u32[]{:S(2)}, u32[]{:S(2)}) collective-permute-start(bf16[576,128]{1,0:T(8,128)(2,1)S(1)} %collective-permute-done.refs_1_), channel_id=1, source_target_pairs={{0,16},{8,24},{16,0},{24,8},{1,17},{9,25},{17,1},{25,9},{2,18},{10... | collective-permute-start | bytes 442376 | tf_op jit(solution)/shard_map/ppermute | solution.py:67
  60.0 7.3 %collective-permute-start.1 = (bf16[576,128]{1,0:T(8,128)(2,1)S(1)}, bf16[576,128]{1,0:T(8,128)(2,1)}, u32[]{:S(2)}, u32[]{:S(2)}) collective-permute-start(bf16[576,128]{1,0:T(8,128)(2,1)S(1)} %collective-permute-done.refs_1_), channel_id=1, source_target_pairs={{0,8},{8,0},{16,24},{24,16},{1,9},{9,1},{17,25},{25,17},{2,10},{10... | collective-permute-start | bytes 442376 | tf_op jit(solution)/shard_map/ppermute | solution.py:67
  62.7 7.0 %collective-permute-start.23 = (bf16[576,128]{1,0:T(8,128)(2,1)S(1)}, bf16[576,128]{1,0:T(8,128)(2,1)S(1)}, u32[]{:S(2)}, u32[]{:S(2)}) collective-permute-start(bf16[576,128]{1,0:T(8,128)(2,1)S(1)} %collective-permute-done.10.refs_11_), channel_id=1, source_target_pairs={{0,1},{1,0},{2,3},{3,2},{4,5},{5,4},{6,7},{7,6},{8,9},{9,8},{10,11... | collective-permute-start | bytes 442376 | tf_op jit(solution)/shard_map/ppermute | solution.py:76
  109.1 9.3 %collective-permute-start.32 = (bf16[128,512]{1,0:T(8,128)(2,1)}, bf16[128,512]{1,0:T(8,128)(2,1)S(1)}, u32[]{:S(2)}, u32[]{:S(2)}) collective-permute-start(bf16[128,512]{1,0:T(8,128)(2,1)} %get-tuple-element.40), channel_id=1, source_target_pairs={{0,2},{1,3},{2,0},{3,1},{4,6},{5,7},{6,4},{7,5},{8,10},{9,11},{10,... | collective-permute-start | bytes 393224 | tf_op jit(solution)/shard_map/ppermute | solution.py:76
  110.9 7.5 %collective-permute-start.30 = (bf16[288,128]{1,0:T(8,128)(2,1)S(1)}, bf16[288,128]{1,0:T(8,128)(2,1)S(1)}, u32[]{:S(2)}, u32[]{:S(2)}) collective-permute-start(bf16[288,128]{1,0:T(8,128)(2,1)S(1)} %get-tuple-element.47.refs_0_), channel_id=1, source_target_pairs={{0,24},{8,16},{16,8},{24,0},{1,25},{9,17},{17,9},{25,1},{2,26},{10... | collective-permute-start | bytes 221192 | tf_op jit(solution)/shard_map/ppermute | solution.py:67
  112.4 7.6 %collective-permute-start.29 = (bf16[288,128]{1,0:T(8,128)(2,1)S(1)}, bf16[288,128]{1,0:T(8,128)(2,1)S(1)}, u32[]{:S(2)}, u32[]{:S(2)}) collective-permute-start(bf16[288,128]{1,0:T(8,128)(2,1)S(1)} %get-tuple-element.47.refs_0_), channel_id=1, source_target_pairs={{0,16},{8,24},{16,0},{24,8},{1,17},{9,25},{17,1},{25,9},{2,18},{10... | collective-permute-start | bytes 221192 | tf_op jit(solution)/shard_map/ppermute | solution.py:67
  112.8 8.6 %collective-permute-start.28 = (bf16[288,128]{1,0:T(8,128)(2,1)S(1)}, bf16[288,128]{1,0:T(8,128)(2,1)S(1)}, u32[]{:S(2)}, u32[]{:S(2)}) collective-permute-start(bf16[288,128]{1,0:T(8,128)(2,1)S(1)} %get-tuple-element.47.refs_0_), channel_id=1, source_target_pairs={{0,8},{8,0},{16,24},{24,16},{1,9},{9,1},{17,25},{25,17},{2,10},{10... | collective-permute-start | bytes 221192 | tf_op jit(solution)/shard_map/ppermute | solution.py:67
  113.6 12.1 %collective-permute-start.33 = (bf16[128,512]{1,0:T(8,128)(2,1)S(1)}, bf16[128,512]{1,0:T(8,128)(2,1)S(1)}, u32[]{:S(2)}, u32[]{:S(2)}) collective-permute-start(bf16[128,512]{1,0:T(8,128)(2,1)S(1)} %copy-done.26), channel_id=1, source_target_pairs={{0,3},{1,2},{2,1},{3,0},{4,7},{5,6},{6,5},{7,4},{8,11},{9,10},{10,... | collective-permute-start | bytes 393224 | tf_op jit(solution)/shard_map/ppermute | solution.py:76
  118.4 7.3 %collective-permute-start.34 = (bf16[128,512]{1,0:T(8,128)(2,1)S(1)}, bf16[128,512]{1,0:T(8,128)(2,1)S(1)}, u32[]{:S(2)}, u32[]{:S(2)}) collective-permute-start(bf16[128,512]{1,0:T(8,128)(2,1)S(1)} %copy-done.25), channel_id=1, source_target_pairs={{0,4},{1,5},{2,6},{3,7},{4,0},{5,1},{6,2},{7,3},{8,12},{9,13},{10,... | collective-permute-start | bytes 393224 | tf_op jit(solution)/shard_map/ppermute | solution.py:76
  118.4 16.9 %collective-permute-start.35 = (bf16[128,512]{1,0:T(8,128)(2,1)S(1)}, bf16[128,512]{1,0:T(8,128)(2,1)S(1)}, u32[]{:S(2)}, u32[]{:S(2)}) collective-permute-start(bf16[128,512]{1,0:T(8,128)(2,1)S(1)} %copy-done.24), channel_id=1, source_target_pairs={{0,5},{1,4},{2,7},{3,6},{4,1},{5,0},{6,3},{7,2},{8,13},{9,12},{10,... | collective-permute-start | bytes 393224 | tf_op jit(solution)/shard_map/ppermute | solution.py:76
  120.0 19.4 %collective-permute-start.36 = (bf16[128,512]{1,0:T(8,128)(2,1)S(1)}, bf16[128,512]{1,0:T(8,128)(2,1)S(1)}, u32[]{:S(2)}, u32[]{:S(2)}) collective-permute-start(bf16[128,512]{1,0:T(8,128)(2,1)S(1)} %copy-done.23), channel_id=1, source_target_pairs={{0,6},{1,7},{2,4},{3,5},{4,2},{5,3},{6,0},{7,1},{8,14},{9,15},{10,... | collective-permute-start | bytes 393224 | tf_op jit(solution)/shard_map/ppermute | solution.py:76
  121.4 21.4 %collective-permute-start.37 = (bf16[128,512]{1,0:T(8,128)(2,1)S(1)}, bf16[128,512]{1,0:T(8,128)(2,1)S(1)}, u32[]{:S(2)}, u32[]{:S(2)}) collective-permute-start(bf16[128,512]{1,0:T(8,128)(2,1)S(1)} %copy-done.22), channel_id=1, source_target_pairs={{0,7},{1,6},{2,5},{3,4},{4,3},{5,2},{6,1},{7,0},{8,15},{9,14},{10,... | collective-permute-start | bytes 393224 | tf_op jit(solution)/shard_map/ppermute | solution.py:76
  (42 other events, 495.3 us)

commit v6 on v5

--- a/solution.py
+++ b/solution.py
@@ -149,12 +149,14 @@
                 row += width
                 start = pl.multiple_of((dom ^ j) * chan, chan)
                 env[pl.ds(start, chan), at : at + depth] = block[row : row + chan, :]
-    value = jnp.dot(first[...], moved[...], preferred_element_type=f32)
-    hidden[...] = (value / (1.0 + jnp.exp(-value))).astype(bf16)
-    update = jnp.dot(second[...], hidden[...], preferred_element_type=f32)
     for s in range(shards):
         rows = slice(s * depth, (s + 1) * depth)
-        fresh[s] = (x_ref[s].astype(f32) + update[rows, :]).astype(bf16)
+        value = jnp.dot(first[rows, :], moved[...], preferred_element_type=f32)
+        hidden[rows, :] = (value / (1.0 + jnp.exp(-value))).astype(bf16)
+    for s in range(shards):
+        rows = slice(s * depth, (s + 1) * depth)
+        update = jnp.dot(second[rows, :], hidden[...], preferred_element_type=f32)
+        fresh[s] = (x_ref[s].astype(f32) + update).astype(bf16)
     copies = [
         pltpu.make_async_copy(fresh.at[place ^ s], out, sems.at[s])
         for s, out in enumerate(new_refs)

time: 144 us -> 144 us (level)
  no operation moved by 1% of the time
where the time goes in v6:
time: 144 us
  waiting for transfers between devices  54 us (38%)
  starting transfers between devices  45.1 us (31%)
  Pallas kernels  14.9 us (10%)
  local copies, waits for them, and re-layouts  14.2 us (10%)
  blocking collectives  14 us (10%)
    ppermute x23, waiting for transfers between devices, flip_tp(): return lax.ppermute(array, 'tp', [(t, t ^ mask) for t in range(count)])  48.4 us
    ppermute x23, starting transfers between devices, flip_tp(): return lax.ppermute(array, 'tp', [(t, t ^ mask) for t in range(count)])  24.7 us
    ppermute x15, starting transfers between devices, flip_dom(): return lax.ppermute(array, 'dom', [(i, i ^ mask) for i in range(count)])  14.6 us
    unnamed x54, local copies, waits for them, and re-layouts  14.2 us
    all_to_all x1, blocking collectives, swap_blocks(): return lax.all_to_all(array, axis, split_axis=0, concat_axis=0, tiled=True)  14 us
    pallas_call x1, Pallas kernels, spread_mlp(): pl.pallas_call(functools.partial(mlp_kernel, quarters=domains, chips=chip...  5.75 us
    all_to_all x1, starting transfers between devices, swap_blocks(): return lax.all_to_all(array, axis, split_axis=0, concat_axis=0, tiled=True)  5.75 us
    ppermute x15, waiting for transfers between devices, flip_dom(): return lax.ppermute(array, 'dom', [(i, i ^ mask) for i in range(count)])  5.67 us
  transfers between devices with their start and end apart: 39, of which 10 were waited for; matrix products, arithmetic and copies ran while one was open for 1% of the time, Pallas kernels for 2%

profile of v6, /device:TPU:9, one launch (start us, length us, event | category | flops | bytes accessed | tf_op | source)
XLA Modules:
  0.0 143.8 jit_solution(7851487687369918536)
XLA Ops:
  2.0 2.1 %split.1 = bf16[8,128,512]{2,1,0:T(8,128)(2,1)} custom-call(bf16[128,4096]{1,0:T(8,128)(2,1)} %x_ref.1, bf16[576,128]{1,0:T(8,128)(2,1)S(1)} %get-tuple-element.25.tie_ref), custom_call_target="tpu_custom_call" | custom-call | tf_op jit(solution)/shard_map/split/pallas_call | solution.py:249
  4.2 5.7 %all-to-all-start = ((bf16[8,128,512]{2,1,0:T(8,128)(2,1)}), bf16[8,128,512]{2,1,0:T(8,128)(2,1)S(1)}, u32[]{:S(2)}, u32[]{:S(2)}) async-start(bf16[8,128,512]{2,1,0:T(8,128)(2,1)} %split.1), calls=%async_computation | async-start | bytes 2097152 | tf_op jit(solution)/shard_map/all_to_all | solution.py:62
  9.9 2.1 %collective-permute-start.8 = (bf16[576,128]{1,0:T(8,128)(2,1)S(1)}, bf16[576,128]{1,0:T(8,128)(2,1)S(1)}, u32[]{:S(2)}, u32[]{:S(2)}) collective-permute-start(bf16[576,128]{1,0:T(8,128)(2,1)S(1)} %get-tuple-element.25.tie_ref), channel_id=1, source_target_pairs={{0,4},{1,5},{2,6},{3,7},{4,0},{5,1},{6,2},{7,3},{8,12},{9,13},{10,... | collective-permute-start | bytes 442376 | tf_op jit(solution)/shard_map/ppermute | solution.py:76
  12.0 1.5 %collective-permute-start = (bf16[576,128]{1,0:T(8,128)(2,1)S(1)}, bf16[576,128]{1,0:T(8,128)(2,1)S(1)}, u32[]{:S(2)}, u32[]{:S(2)}) collective-permute-start(bf16[576,128]{1,0:T(8,128)(2,1)S(1)} %get-tuple-element.25.tie_ref), channel_id=1, source_target_pairs={{0,2},{1,3},{2,0},{3,1},{4,6},{5,7},{6,4},{7,5},{8,10},{9,11},{10,... | collective-permute-start | bytes 442376 | tf_op jit(solution)/shard_map/ppermute | solution.py:76
  13.4 28.9 %collective-permute-done.8.refs_9_ = bf16[576,128]{1,0:T(8,128)(2,1)S(1)} collective-permute-done((bf16[576,128]{1,0:T(8,128)(2,1)S(1)}, bf16[576,128]{1,0:T(8,128)(2,1)S(1)}, u32[]{:S(2)}, u32[]{:S(2)}) %collective-permute-start.8) | collective-permute-done | bytes 147488 | tf_op jit(solution)/shard_map/ppermute | solution.py:76
  42.8 2.2 %collective-permute-start.11 = (bf16[576,128]{1,0:T(8,128)(2,1)S(1)}, bf16[576,128]{1,0:T(8,128)(2,1)S(1)}, u32[]{:S(2)}, u32[]{:S(2)}) collective-permute-start(bf16[576,128]{1,0:T(8,128)(2,1)S(1)} %collective-permute-done.8.refs_9_), channel_id=1, source_target_pairs={{0,24},{8,16},{16,8},{24,0},{1,25},{9,17},{17,9},{25,1},{2,26},{10... | collective-permute-start | bytes 442376 | tf_op jit(solution)/shard_map/ppermute | solution.py:67
  45.2 1.8 %collective-permute-done.4.refs_5_ = bf16[576,128]{1,0:T(8,128)(2,1)S(1)} collective-permute-done((bf16[576,128]{1,0:T(8,128)(2,1)S(1)}, bf16[576,128]{1,0:T(8,128)(2,1)S(1)}, u32[]{:S(2)}, u32[]{:S(2)}) %collective-permute-start.4) | collective-permute-done | bytes 147488 | tf_op jit(solution)/shard_map/ppermute | solution.py:76
  51.0 1.7 %collective-permute-done.10.refs_11_ = bf16[576,128]{1,0:T(8,128)(2,1)S(1)} collective-permute-done((bf16[576,128]{1,0:T(8,128)(2,1)S(1)}, bf16[576,128]{1,0:T(8,128)(2,1)S(1)}, u32[]{:S(2)}, u32[]{:S(2)}) %collective-permute-start.10) | collective-permute-done | bytes 147488 | tf_op jit(solution)/shard_map/ppermute | solution.py:67
  52.7 1.4 collective-permute-start.5
  57.6 1.7 %collective-permute-done.6.refs_7_ = bf16[576,128]{1,0:T(8,128)(2,1)S(1)} collective-permute-done((bf16[576,128]{1,0:T(8,128)(2,1)S(1)}, bf16[576,128]{1,0:T(8,128)(2,1)S(1)}, u32[]{:S(2)}, u32[]{:S(2)}) %collective-permute-start.6) | collective-permute-done | bytes 147488 | tf_op jit(solution)/shard_map/ppermute | solution.py:67
  62.7 2.3 %collective-permute-start.23 = (bf16[576,128]{1,0:T(8,128)(2,1)S(1)}, bf16[576,128]{1,0:T(8,128)(2,1)S(1)}, u32[]{:S(2)}, u32[]{:S(2)}) collective-permute-start(bf16[576,128]{1,0:T(8,128)(2,1)S(1)} %collective-permute-done.10.refs_11_), channel_id=1, source_target_pairs={{0,1},{1,0},{2,3},{3,2},{4,5},{5,4},{6,7},{7,6},{8,9},{9,8},{10,11... | collective-permute-start | bytes 442376 | tf_op jit(solution)/shard_map/ppermute | solution.py:76
  65.0 1.5 %collective-permute-done.2.refs_3_ = bf16[576,128]{1,0:T(8,128)(2,1)} collective-permute-done((bf16[576,128]{1,0:T(8,128)(2,1)S(1)}, bf16[576,128]{1,0:T(8,128)(2,1)}, u32[]{:S(2)}, u32[]{:S(2)}) %collective-permute-start.2) | collective-permute-done | bytes 147488 | tf_op jit(solution)/shard_map/ppermute | solution.py:67
  83.0 5.8 %mlp.1 = (bf16[128,512]{1,0:T(8,128)(2,1)}, bf16[128,512]{1,0:T(8,128)(2,1)}, bf16[128,512]{1,0:T(8,128)(2,1)}, bf16[128,512]{1,0:T(8,128)(2,1)}, bf16[128,512]{...) custom-call(bf16[8,128,512]{2,1,0:T(8,128)(2,1)S(1)} %all-to-all-don, ...), custom_call_target="tpu_custom_call" | custom-call | tf_op jit(solution)/shard_map/mlp/pallas_call | solution.py:269
  88.8 14.0 %all_to_all.10.w_ref = bf16[8,32,512]{2,1,0:T(8,128)(2,1)S(1)} all-to-all(bf16[8,32,512]{2,1,0:T(8,128)(2,1)} %get-tuple-element.30), channel_id=1, replica_groups=mesh['dom'=4,'tp'=8] {'tp'}, dimensions={0} | all-to-all | bytes 524288 | tf_op jit(solution)/shard_map/all_to_all | solution.py:62
  102.8 1.6 %sums.1 = (f32[288,128]{1,0:T(8,128)S(1)}, bf16[288,128]{1,0:T(8,128)(2,1)S(1)}, bf16[288,128]{1,0:T(8,128)(2,1)S(1)}, bf16[288,128]{1,0:T(8,128)(2,1)S(1)}) custom-call(s32[32]{0:T(128)} %bitcast.13, bf16[8,32,512]{2,1,0:T(8,128)(2,1)S(1)} %all_to_all.10.w_ref, f32[10,32,128]{2,1,0:T(8,128)S(1)} %get-tuple-element.31.h_ref), custom_call_target="tpu_custom_call" | custom-call | tf_op jit(solution)/shard_map/sums/pallas_call | solution.py:450
  107.2 1.9 %collective-permute-start.31 = (bf16[128,512]{1,0:T(8,128)(2,1)}, bf16[128,512]{1,0:T(8,128)(2,1)S(1)}, u32[]{:S(2)}, u32[]{:S(2)}) collective-permute-start(bf16[128,512]{1,0:T(8,128)(2,1)} %get-tuple-element.39), channel_id=1, source_target_pairs={{0,1},{1,0},{2,3},{3,2},{4,5},{5,4},{6,7},{7,6},{8,9},{9,8},{10,11... | collective-permute-start | bytes 393224 | tf_op jit(solution)/shard_map/ppermute | solution.py:76
  109.0 1.7 %collective-permute-start.32 = (bf16[128,512]{1,0:T(8,128)(2,1)}, bf16[128,512]{1,0:T(8,128)(2,1)S(1)}, u32[]{:S(2)}, u32[]{:S(2)}) collective-permute-start(bf16[128,512]{1,0:T(8,128)(2,1)} %get-tuple-element.40), channel_id=1, source_target_pairs={{0,2},{1,3},{2,0},{3,1},{4,6},{5,7},{6,4},{7,5},{8,10},{9,11},{10,... | collective-permute-start | bytes 393224 | tf_op jit(solution)/shard_map/ppermute | solution.py:76
  110.8 1.6 %collective-permute-start.30 = (bf16[288,128]{1,0:T(8,128)(2,1)S(1)}, bf16[288,128]{1,0:T(8,128)(2,1)S(1)}, u32[]{:S(2)}, u32[]{:S(2)}) collective-permute-start(bf16[288,128]{1,0:T(8,128)(2,1)S(1)} %get-tuple-element.47.refs_0_), channel_id=1, source_target_pairs={{0,24},{8,16},{16,8},{24,0},{1,25},{9,17},{17,9},{25,1},{2,26},{10... | collective-permute-start | bytes 221192 | tf_op jit(solution)/shard_map/ppermute | solution.py:67
  113.5 4.8 %collective-permute-start.33 = (bf16[128,512]{1,0:T(8,128)(2,1)S(1)}, bf16[128,512]{1,0:T(8,128)(2,1)S(1)}, u32[]{:S(2)}, u32[]{:S(2)}) collective-permute-start(bf16[128,512]{1,0:T(8,128)(2,1)S(1)} %copy-done.26), channel_id=1, source_target_pairs={{0,3},{1,2},{2,1},{3,0},{4,7},{5,6},{6,5},{7,4},{8,11},{9,10},{10,... | collective-permute-start | bytes 393224 | tf_op jit(solution)/shard_map/ppermute | solution.py:76
  118.3 1.6 %collective-permute-start.35 = (bf16[128,512]{1,0:T(8,128)(2,1)S(1)}, bf16[128,512]{1,0:T(8,128)(2,1)S(1)}, u32[]{:S(2)}, u32[]{:S(2)}) collective-permute-start(bf16[128,512]{1,0:T(8,128)(2,1)S(1)} %copy-done.24), channel_id=1, source_target_pairs={{0,5},{1,4},{2,7},{3,6},{4,1},{5,0},{6,3},{7,2},{8,13},{9,12},{10,... | collective-permute-start | bytes 393224 | tf_op jit(solution)/shard_map/ppermute | solution.py:76
  123.4 2.2 %invariants.1 = (f32[3,32,4096]{2,1,0:T(8,128)}, f32[8,128]{1,0:T(8,128)S(1)}) custom-call(s32[32]{0:T(128)} %bitcast.14, bf16[8,32,512]{2,1,0:T(8,128)(2,1)S(1)} %all_to_all.10.w_ref, f32[10,32,128]{2,1,0:T(8,128)S(1)} %get-tuple-element.31.h_ref, bf16[288,128]{1,0:T(8,128)(2,1)S(1)} %get-tuple-element.47.refs_0_, ...), custom_call_target="tpu_custom_call" | custom-call | tf_op jit(solution)/shard_map/invariants/pallas_call | solution.py:466
  125.6 9.6 %collective-permute-done.35.refs_5_ = bf16[128,512]{1,0:T(8,128)(2,1)S(1)} collective-permute-done((bf16[128,512]{1,0:T(8,128)(2,1)S(1)}, bf16[128,512]{1,0:T(8,128)(2,1)S(1)}, u32[]{:S(2)}, u32[]{:S(2)}) %collective-permute-start.35) | collective-permute-done | bytes 131104 | tf_op jit(solution)/shard_map/ppermute | solution.py:76
  135.2 4.1 %collective-permute-done.36.refs_6_ = bf16[128,512]{1,0:T(8,128)(2,1)S(1)} collective-permute-done((bf16[128,512]{1,0:T(8,128)(2,1)S(1)}, bf16[128,512]{1,0:T(8,128)(2,1)S(1)}, u32[]{:S(2)}, u32[]{:S(2)}) %collective-permute-start.36) | collective-permute-done | bytes 131104 | tf_op jit(solution)/shard_map/ppermute | solution.py:76
  139.4 3.4 %collective-permute-done.37.refs_7_ = bf16[128,512]{1,0:T(8,128)(2,1)S(1)} collective-permute-done((bf16[128,512]{1,0:T(8,128)(2,1)S(1)}, bf16[128,512]{1,0:T(8,128)(2,1)S(1)}, u32[]{:S(2)}, u32[]{:S(2)}) %collective-permute-start.37) | collective-permute-done | bytes 131104 | tf_op jit(solution)/shard_map/ppermute | solution.py:76
  (118 shorter events, 37.8 us)
Async XLA Ops:
  4.2 70.1 %all-to-all-start = ((bf16[8,128,512]{2,1,0:T(8,128)(2,1)}), bf16[8,128,512]{2,1,0:T(8,128)(2,1)S(1)}, u32[]{:S(2)}, u32[]{:S(2)}) async-start(bf16[8,128,512]{2,1,0:T(8,128)(2,1)} %split.1), calls=%async_computation | async-start | bytes 2097152 | tf_op jit(solution)/shard_map/all_to_all | solution.py:62
  9.9 32.4 %collective-permute-start.8 = (bf16[576,128]{1,0:T(8,128)(2,1)S(1)}, bf16[576,128]{1,0:T(8,128)(2,1)S(1)}, u32[]{:S(2)}, u32[]{:S(2)}) collective-permute-start(bf16[576,128]{1,0:T(8,128)(2,1)S(1)} %get-tuple-element.25.tie_ref), channel_id=1, source_target_pairs={{0,4},{1,5},{2,6},{3,7},{4,0},{5,1},{6,2},{7,3},{8,12},{9,13},{10,... | collective-permute-start | bytes 442376 | tf_op jit(solution)/shard_map/ppermute | solution.py:76
  12.0 35.1 %collective-permute-start.4 = (bf16[576,128]{1,0:T(8,128)(2,1)S(1)}, bf16[576,128]{1,0:T(8,128)(2,1)S(1)}, u32[]{:S(2)}, u32[]{:S(2)}) collective-permute-start(bf16[576,128]{1,0:T(8,128)(2,1)S(1)} %get-tuple-element.25.tie_ref), channel_id=1, source_target_pairs={{0,6},{1,7},{2,4},{3,5},{4,2},{5,3},{6,0},{7,1},{8,14},{9,15},{10,... | collective-permute-start | bytes 442376 | tf_op jit(solution)/shard_map/ppermute | solution.py:76
  12.0 36.3 %collective-permute-start = (bf16[576,128]{1,0:T(8,128)(2,1)S(1)}, bf16[576,128]{1,0:T(8,128)(2,1)S(1)}, u32[]{:S(2)}, u32[]{:S(2)}) collective-permute-start(bf16[576,128]{1,0:T(8,128)(2,1)S(1)} %get-tuple-element.25.tie_ref), channel_id=1, source_target_pairs={{0,2},{1,3},{2,0},{3,1},{4,6},{5,7},{6,4},{7,5},{8,10},{9,11},{10,... | collective-permute-start | bytes 442376 | tf_op jit(solution)/shard_map/ppermute | solution.py:76
  42.3 7.2 %collective-permute-start.21 = (bf16[576,128]{1,0:T(8,128)(2,1)S(1)}, bf16[576,128]{1,0:T(8,128)(2,1)S(1)}, u32[]{:S(2)}, u32[]{:S(2)}) collective-permute-start(bf16[576,128]{1,0:T(8,128)(2,1)S(1)} %collective-permute-done.8.refs_9_), channel_id=1, source_target_pairs={{0,1},{1,0},{2,3},{3,2},{4,5},{5,4},{6,7},{7,6},{8,9},{9,8},{10,11... | collective-permute-start | bytes 442376 | tf_op jit(solution)/shard_map/ppermute | solution.py:76
  42.8 7.9 %collective-permute-start.11 = (bf16[576,128]{1,0:T(8,128)(2,1)S(1)}, bf16[576,128]{1,0:T(8,128)(2,1)S(1)}, u32[]{:S(2)}, u32[]{:S(2)}) collective-permute-start(bf16[576,128]{1,0:T(8,128)(2,1)S(1)} %collective-permute-done.8.refs_9_), channel_id=1, source_target_pairs={{0,24},{8,16},{16,8},{24,0},{1,25},{9,17},{17,9},{25,1},{2,26},{10... | collective-permute-start | bytes 442376 | tf_op jit(solution)/shard_map/ppermute | solution.py:67
  45.0 7.7 %collective-permute-start.10 = (bf16[576,128]{1,0:T(8,128)(2,1)S(1)}, bf16[576,128]{1,0:T(8,128)(2,1)S(1)}, u32[]{:S(2)}, u32[]{:S(2)}) collective-permute-start(bf16[576,128]{1,0:T(8,128)(2,1)S(1)} %collective-permute-done.8.refs_9_), channel_id=1, source_target_pairs={{0,16},{8,24},{16,0},{24,8},{1,17},{9,25},{17,1},{25,9},{2,18},{10... | collective-permute-start | bytes 442376 | tf_op jit(solution)/shard_map/ppermute | solution.py:67
  47.1 7.1 %collective-permute-start.9 = (bf16[576,128]{1,0:T(8,128)(2,1)S(1)}, bf16[576,128]{1,0:T(8,128)(2,1)S(1)}, u32[]{:S(2)}, u32[]{:S(2)}) collective-permute-start(bf16[576,128]{1,0:T(8,128)(2,1)S(1)} %collective-permute-done.8.refs_9_), channel_id=1, source_target_pairs={{0,8},{8,0},{16,24},{24,16},{1,9},{9,1},{17,25},{25,17},{2,10},{10... | collective-permute-start | bytes 442376 | tf_op jit(solution)/shard_map/ppermute | solution.py:67
  49.5 6.8 %collective-permute-start.7 = (bf16[576,128]{1,0:T(8,128)(2,1)S(1)}, bf16[576,128]{1,0:T(8,128)(2,1)S(1)}, u32[]{:S(2)}, u32[]{:S(2)}) collective-permute-start(bf16[576,128]{1,0:T(8,128)(2,1)S(1)} %collective-permute-done.4.refs_5_), channel_id=1, source_target_pairs={{0,24},{8,16},{16,8},{24,0},{1,25},{9,17},{17,9},{25,1},{2,26},{10... | collective-permute-start | bytes 442376 | tf_op jit(solution)/shard_map/ppermute | solution.py:67
  50.8 8.6 %collective-permute-start.6 = (bf16[576,128]{1,0:T(8,128)(2,1)S(1)}, bf16[576,128]{1,0:T(8,128)(2,1)S(1)}, u32[]{:S(2)}, u32[]{:S(2)}) collective-permute-start(bf16[576,128]{1,0:T(8,128)(2,1)S(1)} %collective-permute-done.4.refs_5_), channel_id=1, source_target_pairs={{0,16},{8,24},{16,0},{24,8},{1,17},{9,25},{17,1},{25,9},{2,18},{10... | collective-permute-start | bytes 442376 | tf_op jit(solution)/shard_map/ppermute | solution.py:67
  52.7 7.3 %collective-permute-start.5 = (bf16[576,128]{1,0:T(8,128)(2,1)S(1)}, bf16[576,128]{1,0:T(8,128)(2,1)}, u32[]{:S(2)}, u32[]{:S(2)}) collective-permute-start(bf16[576,128]{1,0:T(8,128)(2,1)S(1)} %collective-permute-done.4.refs_5_), channel_id=1, source_target_pairs={{0,8},{8,0},{16,24},{24,16},{1,9},{9,1},{17,25},{25,17},{2,10},{10... | collective-permute-start | bytes 442376 | tf_op jit(solution)/shard_map/ppermute | solution.py:67
  55.6 19.2 %collective-permute-start.12 = (bf16[4,576,128]{2,1,0:T(8,128)(2,1)S(1)}, bf16[4,576,128]{2,1,0:T(8,128)(2,1)S(1)}, u32[]{:S(2)}, u32[]{:S(2)}) collective-permute-start(bf16[4,576,128]{2,1,0:T(8,128)(2,1)S(1)} %get-tuple-element.29.refs_0_), channel_id=1, source_target_pairs={{0,1},{1,0},{2,3},{3,2},{4,5},{5,4},{6,7},{7,6},{8,9},{9,8},{10,11... | collective-permute-start | bytes 1769480 | tf_op jit(solution)/shard_map/ppermute | solution.py:76
  59.3 7.2 %collective-permute-start.2 = (bf16[576,128]{1,0:T(8,128)(2,1)S(1)}, bf16[576,128]{1,0:T(8,128)(2,1)}, u32[]{:S(2)}, u32[]{:S(2)}) collective-permute-start(bf16[576,128]{1,0:T(8,128)(2,1)S(1)} %collective-permute-done.refs_1_), channel_id=1, source_target_pairs={{0,16},{8,24},{16,0},{24,8},{1,17},{9,25},{17,1},{25,9},{2,18},{10... | collective-permute-start | bytes 442376 | tf_op jit(solution)/shard_map/ppermute | solution.py:67
  60.0 7.3 %collective-permute-start.1 = (bf16[576,128]{1,0:T(8,128)(2,1)S(1)}, bf16[576,128]{1,0:T(8,128)(2,1)}, u32[]{:S(2)}, u32[]{:S(2)}) collective-permute-start(bf16[576,128]{1,0:T(8,128)(2,1)S(1)} %collective-permute-done.refs_1_), channel_id=1, source_target_pairs={{0,8},{8,0},{16,24},{24,16},{1,9},{9,1},{17,25},{25,17},{2,10},{10... | collective-permute-start | bytes 442376 | tf_op jit(solution)/shard_map/ppermute | solution.py:67
  62.7 7.0 %collective-permute-start.23 = (bf16[576,128]{1,0:T(8,128)(2,1)S(1)}, bf16[576,128]{1,0:T(8,128)(2,1)S(1)}, u32[]{:S(2)}, u32[]{:S(2)}) collective-permute-start(bf16[576,128]{1,0:T(8,128)(2,1)S(1)} %collective-permute-done.10.refs_11_), channel_id=1, source_target_pairs={{0,1},{1,0},{2,3},{3,2},{4,5},{5,4},{6,7},{7,6},{8,9},{9,8},{10,11... | collective-permute-start | bytes 442376 | tf_op jit(solution)/shard_map/ppermute | solution.py:76
  109.0 9.3 %collective-permute-start.32 = (bf16[128,512]{1,0:T(8,128)(2,1)}, bf16[128,512]{1,0:T(8,128)(2,1)S(1)}, u32[]{:S(2)}, u32[]{:S(2)}) collective-permute-start(bf16[128,512]{1,0:T(8,128)(2,1)} %get-tuple-element.40), channel_id=1, source_target_pairs={{0,2},{1,3},{2,0},{3,1},{4,6},{5,7},{6,4},{7,5},{8,10},{9,11},{10,... | collective-permute-start | bytes 393224 | tf_op jit(solution)/shard_map/ppermute | solution.py:76
  110.8 7.5 %collective-permute-start.30 = (bf16[288,128]{1,0:T(8,128)(2,1)S(1)}, bf16[288,128]{1,0:T(8,128)(2,1)S(1)}, u32[]{:S(2)}, u32[]{:S(2)}) collective-permute-start(bf16[288,128]{1,0:T(8,128)(2,1)S(1)} %get-tuple-element.47.refs_0_), channel_id=1, source_target_pairs={{0,24},{8,16},{16,8},{24,0},{1,25},{9,17},{17,9},{25,1},{2,26},{10... | collective-permute-start | bytes 221192 | tf_op jit(solution)/shard_map/ppermute | solution.py:67
  112.3 7.6 %collective-permute-start.29 = (bf16[288,128]{1,0:T(8,128)(2,1)S(1)}, bf16[288,128]{1,0:T(8,128)(2,1)S(1)}, u32[]{:S(2)}, u32[]{:S(2)}) collective-permute-start(bf16[288,128]{1,0:T(8,128)(2,1)S(1)} %get-tuple-element.47.refs_0_), channel_id=1, source_target_pairs={{0,16},{8,24},{16,0},{24,8},{1,17},{9,25},{17,1},{25,9},{2,18},{10... | collective-permute-start | bytes 221192 | tf_op jit(solution)/shard_map/ppermute | solution.py:67
  112.7 8.6 %collective-permute-start.28 = (bf16[288,128]{1,0:T(8,128)(2,1)S(1)}, bf16[288,128]{1,0:T(8,128)(2,1)S(1)}, u32[]{:S(2)}, u32[]{:S(2)}) collective-permute-start(bf16[288,128]{1,0:T(8,128)(2,1)S(1)} %get-tuple-element.47.refs_0_), channel_id=1, source_target_pairs={{0,8},{8,0},{16,24},{24,16},{1,9},{9,1},{17,25},{25,17},{2,10},{10... | collective-permute-start | bytes 221192 | tf_op jit(solution)/shard_map/ppermute | solution.py:67
  113.5 12.1 %collective-permute-start.33 = (bf16[128,512]{1,0:T(8,128)(2,1)S(1)}, bf16[128,512]{1,0:T(8,128)(2,1)S(1)}, u32[]{:S(2)}, u32[]{:S(2)}) collective-permute-start(bf16[128,512]{1,0:T(8,128)(2,1)S(1)} %copy-done.26), channel_id=1, source_target_pairs={{0,3},{1,2},{2,1},{3,0},{4,7},{5,6},{6,5},{7,4},{8,11},{9,10},{10,... | collective-permute-start | bytes 393224 | tf_op jit(solution)/shard_map/ppermute | solution.py:76
  118.3 7.3 %collective-permute-start.34 = (bf16[128,512]{1,0:T(8,128)(2,1)S(1)}, bf16[128,512]{1,0:T(8,128)(2,1)S(1)}, u32[]{:S(2)}, u32[]{:S(2)}) collective-permute-start(bf16[128,512]{1,0:T(8,128)(2,1)S(1)} %copy-done.25), channel_id=1, source_target_pairs={{0,4},{1,5},{2,6},{3,7},{4,0},{5,1},{6,2},{7,3},{8,12},{9,13},{10,... | collective-permute-start | bytes 393224 | tf_op jit(solution)/shard_map/ppermute | solution.py:76
  118.3 16.9 %collective-permute-start.35 = (bf16[128,512]{1,0:T(8,128)(2,1)S(1)}, bf16[128,512]{1,0:T(8,128)(2,1)S(1)}, u32[]{:S(2)}, u32[]{:S(2)}) collective-permute-start(bf16[128,512]{1,0:T(8,128)(2,1)S(1)} %copy-done.24), channel_id=1, source_target_pairs={{0,5},{1,4},{2,7},{3,6},{4,1},{5,0},{6,3},{7,2},{8,13},{9,12},{10,... | collective-permute-start | bytes 393224 | tf_op jit(solution)/shard_map/ppermute | solution.py:76
  119.9 19.4 %collective-permute-start.36 = (bf16[128,512]{1,0:T(8,128)(2,1)S(1)}, bf16[128,512]{1,0:T(8,128)(2,1)S(1)}, u32[]{:S(2)}, u32[]{:S(2)}) collective-permute-start(bf16[128,512]{1,0:T(8,128)(2,1)S(1)} %copy-done.23), channel_id=1, source_target_pairs={{0,6},{1,7},{2,4},{3,5},{4,2},{5,3},{6,0},{7,1},{8,14},{9,15},{10,... | collective-permute-start | bytes 393224 | tf_op jit(solution)/shard_map/ppermute | solution.py:76
  121.3 21.4 %collective-permute-start.37 = (bf16[128,512]{1,0:T(8,128)(2,1)S(1)}, bf16[128,512]{1,0:T(8,128)(2,1)S(1)}, u32[]{:S(2)}, u32[]{:S(2)}) collective-permute-start(bf16[128,512]{1,0:T(8,128)(2,1)S(1)} %copy-done.22), channel_id=1, source_target_pairs={{0,7},{1,6},{2,5},{3,4},{4,3},{5,2},{6,1},{7,0},{8,15},{9,14},{10,... | collective-permute-start | bytes 393224 | tf_op jit(solution)/shard_map/ppermute | solution.py:76
  (42 other events, 495.3 us)
